TPU v7x, 32 devices: a whole 2x2x4 slice. The times are simulated.
32 devices in a mesh: seq: 2 (over x), fsdp: 16 (over z, y, core).
Axes of the slice: x: 2, y: 2, z: 4, core: 2. Of those that a mesh axis runs over, the one named last changes fastest.
Arguments:
- tokens_in: bfloat16 [32, 2048, 768], P('fsdp', 'seq')
- segment_ids: int32 [32, 2048], P('fsdp'), may hold values from 0 to 15, never falling along the last dimension, each value on 1 to 1024 neighbouring positions
- random_blocks: int32 [32, 32, 3], P('fsdp'), may hold values from 0 to 31
- global_blocks: int32 [32, 2], P('fsdp'), may hold values from 0 to 31
- w_query: bfloat16 [768, 768], P('fsdp'), may hold values from -0.15625 to 0.15625
- b_query: bfloat16 [768], P('fsdp'), may hold values from -1.5 to 1.5
- w_key: bfloat16 [768, 768], P('fsdp'), may hold values from -0.15625 to 0.15625
- w_value: bfloat16 [768, 768], P('fsdp'), may hold values from -0.21875 to 0.21875
- b_value: bfloat16 [768], P('fsdp'), may hold values from -1.5 to 1.5
- w_attn_out: bfloat16 [768, 768], P('fsdp'), may hold values from -0.875 to 0.875
- b_attn_out: bfloat16 [768], P('fsdp'), may hold values from -1.5 to 1.5
- ln1_gain: bfloat16 [768], P('fsdp'), may hold values from 0.5 to 1.5
- ln1_bias: bfloat16 [768], P('fsdp'), may hold values from -1.5 to 1.5
- w_inner: bfloat16 [768, 3072], P('fsdp')
- b_inner: bfloat16 [3072], P('fsdp'), may hold values from -1.5 to 1.5
- w_outer: bfloat16 [3072, 768], P('fsdp'), may hold values from -0.109375 to 0.109375
- b_outer: bfloat16 [768], P('fsdp'), may hold values from -1.5 to 1.5
- ln2_gain: bfloat16 [768], P('fsdp'), may hold values from 0.5 to 1.5
- ln2_bias: bfloat16 [768], P('fsdp'), may hold values from -1.5 to 1.5
- out_grad: bfloat16 [32, 2048, 768], P('fsdp', 'seq'), may hold values from -6 to 6
Outputs:
- out_tokens: bfloat16 [32, 2048, 768], P('fsdp', 'seq')
- d_tokens_in: bfloat16 [32, 2048, 768], P('fsdp', 'seq')
- d_w_query: float32 [768, 768], P('fsdp')
- d_b_query: float32 [768], P('fsdp')
- d_w_key: float32 [768, 768], P('fsdp')
- d_w_value: float32 [768, 768], P('fsdp')
- d_b_value: float32 [768], P('fsdp')
- d_w_attn_out: float32 [768, 768], P('fsdp')
- d_b_attn_out: float32 [768], P('fsdp')
- d_ln1_gain: float32 [768], P('fsdp')
- d_ln1_bias: float32 [768], P('fsdp')
- d_w_inner: float32 [768, 3072], P('fsdp')
- d_b_inner: float32 [3072], P('fsdp')
- d_w_outer: float32 [3072, 768], P('fsdp')
- d_b_outer: float32 [768], P('fsdp')
- d_ln2_gain: float32 [768], P('fsdp')
- d_ln2_bias: float32 [768], P('fsdp')
- rms_values: float32 [3], replicated
Inputs may be any that keep to these rules, and one draw needn't show every extreme that they name: `segment_ids`: along a sequence the ids never fall; each id marks one document. `random_blocks`: block numbers of the same sequence, repeats allowed. `global_blocks`: block numbers of the same sequence, the two may coincide.
All inputs are finite; a program needn't handle non-finite values.
Results may differ from a plain program's by a relative error of at most 0.015.
Values may be sent and summed in bfloat16 or wider, within the bound.
A program may use at most 320 MiB of HBM per device.

v0:
```python
import functools
import math

import jax
import jax.numpy as jnp
from jax import lax
from jax.experimental import pallas as pl
from jax.experimental.pallas import tpu as pltpu
from jax.sharding import PartitionSpec as P

HD = 64
BLK = 64
CHUNK = 4
NEG = -1e30


def plan_blocks(seg, rand, glob):
    rows, full_len = seg.shape
    nb = full_len // BLK
    ids = jnp.arange(nb, dtype=jnp.int32)
    is_global = jnp.any(ids[None, :, None] == glob[:, None, :], axis=-1)
    picked = jnp.any(rand[:, :, None, :] == ids[None, None, :, None], axis=-1)
    nearby = jnp.abs(ids[:, None] - ids[None, :]) <= 1
    admitted = nearby[None] | picked | is_global[:, :, None] | is_global[:, None, :]
    by_block = seg.reshape(rows, nb, BLK)
    low, high = by_block[:, :, 0], by_block[:, :, BLK - 1]
    meets = (low[:, :, None] <= high[:, None, :]) & (low[:, None, :] <= high[:, :, None])
    active = (admitted & meets).astype(jnp.int32)
    upto = (ids[:, None] <= ids[None, :]).astype(jnp.int32)
    place = jnp.sum(active[:, :, :, None] * upto[None, None], axis=2) - 1
    count = jnp.sum(active, axis=2)
    hit = (place[:, :, :, None] == ids[None, None, None, :]) & (active[:, :, :, None] > 0)
    listed = jnp.sum(jnp.where(hit, ids[None, None, :, None], 0), axis=2)
    listed = jnp.where(ids[None, None, :] < count[:, :, None], listed, nb)
    chunks = (count + (CHUNK - 1)) // CHUNK
    seg_cols = jnp.concatenate([seg, jnp.full((rows, BLK), -1, jnp.int32)], axis=1)
    seg_cols = jnp.broadcast_to(seg_cols[:, :, None], (rows, full_len + BLK, 128))
    seg_rows = jnp.concatenate([by_block, by_block], axis=2)[:, :, None, :]
    return chunks, listed.reshape(rows, nb * nb), seg_cols, seg_rows


def lane_low(rows):
    return lax.broadcasted_iota(jnp.int32, (rows, 128), 1) < HD


def diag128(dup_t):
    row = lax.broadcasted_iota(jnp.int32, (128, 128), 0) < HD
    col = lax.broadcasted_iota(jnp.int32, (128, 128), 1) < HD
    return jnp.where(row == col, dup_t, jnp.zeros_like(dup_t))


def transposed_twice(tile):
    both = jnp.concatenate([tile, tile], axis=0)
    return both.T


def head_rows(acc):
    turned = jnp.concatenate([acc, acc], axis=0).T
    return jnp.where(lane_low(HD), turned[:HD], turned[HD:])


def pick_diag(full, half):
    lanes = slice(half * 128, half * 128 + 128)
    top = full[half * 128 : half * 128 + HD, lanes]
    low = full[half * 128 + HD : half * 128 + 128, lanes]
    return jnp.where(lane_low(HD), top, low)


def chunk_ids(list_ref, row, base, nb):
    ids = [list_ref[row, base + j] for j in range(CHUNK)]
    safe = [jnp.where(b == nb, 0, b) for b in ids]
    return ids, safe


def block_rows(ref, blocks, lanes):
    return jnp.concatenate(
        [ref[0, pl.ds(pl.multiple_of(b * BLK, BLK), BLK), lanes] for b in blocks], axis=0
    )


def turned_blocks(ref, blocks, rows):
    low = lane_low(rows.stop - rows.start)
    tiles = [ref[b, rows, :] for b in blocks]
    return jnp.concatenate(
        [jnp.where(low, tiles[i], tiles[i + 1]) for i in range(0, CHUNK, 2)], axis=1
    )


def turn_all(src_ref, dst_ref, nb, width):
    def body(b, _):
        start = pl.multiple_of(b * BLK, BLK)
        for t in range(width // 128):
            tile = src_ref[0, pl.ds(start, BLK), t * 128 : t * 128 + 128]
            dst_ref[b, t * 128 : t * 128 + 128, :] = transposed_twice(tile)
        return 0

    lax.fori_loop(0, nb, body, 0)


def dot_f32(left, right):
    return lax.dot_general(
        left, right, (((1,), (0,)), ((), ())), preferred_element_type=jnp.float32
    )


def forward_kernel(group, n_ref, list_ref, q_ref, k_ref, v_ref, segc_ref, segr_ref,
                   o_ref, lse_ref, vt_ref, qst_ref, m_ref, l_ref, acc_ref):
    row = pl.program_id(0)
    width = q_ref.shape[2]
    nb = q_ref.shape[1] // BLK
    groups, halves = width // group, group // 128
    turn_all(v_ref, vt_ref, nb, width)
    qst_ref[...] = jnp.zeros_like(qst_ref)

    def per_query(a, _):
        start = pl.multiple_of(a * BLK, BLK)
        for t in range(width // 128):
            tile = q_ref[0, pl.ds(start, BLK), t * 128 : t * 128 + 128] * 0.125
            g, u = t // halves, t % halves
            qst_ref[g, u * 128 : u * 128 + 128, u * 128 : u * 128 + 128] = diag128(
                transposed_twice(tile.astype(jnp.bfloat16))
            )
        seg_q = segr_ref[0, a]
        m_ref[...] = jnp.full_like(m_ref, NEG)
        l_ref[...] = jnp.zeros_like(l_ref)
        acc_ref[...] = jnp.zeros_like(acc_ref)

        def per_chunk(c, _):
            ids, safe = chunk_ids(list_ref, row, a * nb + c * CHUNK, nb)
            seg_k = block_rows(segc_ref, ids, slice(0, 128))
            allowed = seg_k == seg_q
            for g in range(groups):
                lanes = slice(g * group, g * group + group)
                s_t = dot_f32(block_rows(k_ref, safe, lanes), qst_ref[g])
                weights, alphas = [], []
                for u in range(halves):
                    t = g * halves + u
                    s = jnp.where(allowed, s_t[:, u * 128 : u * 128 + 128], NEG)
                    m_old = m_ref[t]
                    m_new = jnp.maximum(m_old, jnp.max(s, axis=0, keepdims=True))
                    p = jnp.exp(s - m_new)
                    alpha = jnp.exp(m_old - m_new)
                    l_ref[t] = alpha * l_ref[t] + jnp.sum(p, axis=0, keepdims=True)
                    m_ref[t] = m_new
                    weights.append(p.astype(jnp.bfloat16))
                    alphas.append(alpha)
                p_t = jnp.concatenate(weights, axis=1) if halves > 1 else weights[0]
                o_t = dot_f32(turned_blocks(vt_ref, safe, lanes), p_t)
                for u in range(halves):
                    t = g * halves + u
                    acc_ref[t] = alphas[u] * acc_ref[t] + pick_diag(o_t, u)
            return 0

        lax.fori_loop(0, n_ref[row, a], per_chunk, 0)
        for t in range(width // 128):
            total = l_ref[t]
            out = acc_ref[t] / total
            o_ref[0, pl.ds(start, BLK), t * 128 : t * 128 + 128] = head_rows(out).astype(
                jnp.bfloat16
            )
            lse_ref[0, a, :, t * 128 : t * 128 + 128] = m_ref[t] + jnp.log(total)
        return 0

    lax.fori_loop(0, nb, per_query, 0)


def group_of(width):
    return 256 if width % 256 == 0 else 128


def whole_spec(shape):
    rest = (0,) * (len(shape) - 1)
    return pl.BlockSpec((1,) + tuple(shape[1:]), lambda r, *_: (r,) + rest)


def one_spec(shape):
    rest = (0,) * (len(shape) - 1)
    return pl.BlockSpec((1,) + tuple(shape[1:]), lambda r, *_: (r,) + rest,
                        pipeline_mode=pl.Buffered(1))


def attention_forward(q, k, v, plan):
    chunks, listed, seg_cols, seg_rows = plan
    rows, full_len, width = q.shape
    nb, group = full_len // BLK, group_of(width)
    tiles = width // 128
    pairs = rows * full_len * full_len // 4 * width
    args = (q, k, v, seg_cols, seg_rows)
    return pl.pallas_call(
        functools.partial(forward_kernel, group),
        out_shape=(
            jax.ShapeDtypeStruct((rows, full_len, width), jnp.bfloat16),
            jax.ShapeDtypeStruct((rows, nb, 1, width), jnp.float32),
        ),
        grid_spec=pltpu.PrefetchScalarGridSpec(
            num_scalar_prefetch=2,
            grid=(rows,),
            in_specs=[one_spec(x.shape) for x in args],
            out_specs=(one_spec((rows, full_len, width)), one_spec((rows, nb, 1, width))),
            scratch_shapes=[
                pltpu.VMEM((nb, width, 128), jnp.bfloat16),
                pltpu.VMEM((width // group, group, group), jnp.bfloat16),
                pltpu.VMEM((tiles, 1, 128), jnp.float32),
                pltpu.VMEM((tiles, 1, 128), jnp.float32),
                pltpu.VMEM((tiles, HD, 128), jnp.float32),
            ],
        ),
        compiler_params=pltpu.CompilerParams(vmem_limit_bytes=48 << 20),
        cost_estimate=pl.CostEstimate(
            flops=64 * pairs, transcendentals=pairs // HD, bytes_accessed=8 * q.size
        ),
        name="attention_forward",
    )(chunks, listed, *args)


def backward_kernel(group, n_ref, list_ref, q_ref, k_ref, v_ref, o_ref, do_ref, lse_ref,
                    segc_ref, segr_ref, dq_ref, dk_ref, dv_ref,
                    kt_ref, qst_ref, qs_ref, dost_ref, dos_ref, delta_ref, acc_ref,
                    dk_acc, dv_acc):
    row = pl.program_id(0)
    full_len, width = q_ref.shape[1], q_ref.shape[2]
    nb = full_len // BLK
    groups, halves = width // group, group // 128
    turn_all(k_ref, kt_ref, nb, width)
    for ref in (qst_ref, qs_ref, dost_ref, dos_ref, dk_acc, dv_acc):
        ref[...] = jnp.zeros_like(ref)
    low = lane_low(HD)

    def per_query(a, _):
        start = pl.multiple_of(a * BLK, BLK)
        for t in range(width // 128):
            g, u = t // halves, t % halves
            lanes = slice(t * 128, t * 128 + 128)
            square = slice(u * 128, u * 128 + 128)
            q_tile = (q_ref[0, pl.ds(start, BLK), lanes] * 0.125).astype(jnp.bfloat16)
            g_tile = do_ref[0, pl.ds(start, BLK), lanes]
            o_tile = o_ref[0, pl.ds(start, BLK), lanes]
            g_turn = transposed_twice(g_tile)
            qst_ref[g, square, square] = diag128(transposed_twice(q_tile))
            dost_ref[g, square, square] = diag128(g_turn)
            qs_ref[g, square, square] = diag128(jnp.concatenate([q_tile, q_tile], axis=0))
            dos_ref[g, square, square] = diag128(jnp.concatenate([g_tile, g_tile], axis=0))
            product = g_turn.astype(jnp.float32) * transposed_twice(o_tile).astype(jnp.float32)
            delta_ref[t] = jnp.where(
                low[:1],
                jnp.sum(product[:HD], axis=0, keepdims=True),
                jnp.sum(product[HD:], axis=0, keepdims=True),
            )
        seg_q = segr_ref[0, a]
        acc_ref[...] = jnp.zeros_like(acc_ref)

        def per_chunk(c, _):
            ids, safe = chunk_ids(list_ref, row, a * nb + c * CHUNK, nb)
            seg_k = block_rows(segc_ref, ids, slice(0, 128))
            allowed = seg_k == seg_q
            for g in range(groups):
                lanes = slice(g * group, g * group + group)
                s_t = dot_f32(block_rows(k_ref, safe, lanes), qst_ref[g])
                dp_t = dot_f32(block_rows(v_ref, safe, lanes), dost_ref[g])
                p_parts, ds_parts = [], []
                for u in range(halves):
                    t = g * halves + u
                    half = slice(u * 128, u * 128 + 128)
                    lse = lse_ref[0, a, :, t * 128 : t * 128 + 128]
                    p = jnp.exp(jnp.where(allowed, s_t[:, half], NEG) - lse)
                    ds = p * (dp_t[:, half] - delta_ref[t])
                    p_parts.append(p.astype(jnp.bfloat16))
                    ds_parts.append(ds.astype(jnp.bfloat16))
                p_t = jnp.concatenate(p_parts, axis=1) if halves > 1 else p_parts[0]
                ds_t = jnp.concatenate(ds_parts, axis=1) if halves > 1 else ds_parts[0]
                dv = dot_f32(p_t, dos_ref[g])
                dk = dot_f32(ds_t, qs_ref[g])
                dq_t = dot_f32(turned_blocks(kt_ref, safe, lanes), ds_t)
                for j in range(CHUNK):
                    where = pl.ds(pl.multiple_of(safe[j] * BLK, BLK), BLK)
                    part = slice(j * BLK, j * BLK + BLK)
                    dv_acc[where, lanes] += dv[part]
                    dk_acc[where, lanes] += dk[part]
                for u in range(halves):
                    acc_ref[g * halves + u] += pick_diag(dq_t, u)
            return 0

        lax.fori_loop(0, n_ref[row, a], per_chunk, 0)
        for t in range(width // 128):
            dq_ref[0, pl.ds(start, BLK), t * 128 : t * 128 + 128] = (
                head_rows(acc_ref[t]) * 0.125
            ).astype(jnp.bfloat16)
        return 0

    lax.fori_loop(0, nb, per_query, 0)

    def flush(a, _):
        where = pl.ds(pl.multiple_of(a * BLK, BLK), BLK)
        dk_ref[0, where, :] = dk_acc[where, :].astype(jnp.bfloat16)
        dv_ref[0, where, :] = dv_acc[where, :].astype(jnp.bfloat16)
        return 0

    lax.fori_loop(0, nb, flush, 0)


def attention_backward(q, k, v, o, do, lse, plan):
    chunks, listed, seg_cols, seg_rows = plan
    rows, full_len, width = q.shape
    nb, group = full_len // BLK, group_of(width)
    tiles, groups = width // 128, width // group
    pairs = rows * full_len * full_len // 4 * width
    args = (q, k, v, o, do, lse, seg_cols, seg_rows)
    like = jax.ShapeDtypeStruct((rows, full_len, width), jnp.bfloat16)
    square = pltpu.VMEM((groups, group, group), jnp.bfloat16)
    return pl.pallas_call(
        functools.partial(backward_kernel, group),
        out_shape=(like, like, like),
        grid_spec=pltpu.PrefetchScalarGridSpec(
            num_scalar_prefetch=2,
            grid=(rows,),
            in_specs=[one_spec(x.shape) for x in args],
            out_specs=tuple(one_spec(like.shape) for _ in range(3)),
            scratch_shapes=[
                pltpu.VMEM((nb, width, 128), jnp.bfloat16),
                square, square, square, square,
                pltpu.VMEM((tiles, 1, 128), jnp.float32),
                pltpu.VMEM((tiles, HD, 128), jnp.float32),
                pltpu.VMEM((full_len, width), jnp.float32),
                pltpu.VMEM((full_len, width), jnp.float32),
            ],
        ),
        compiler_params=pltpu.CompilerParams(vmem_limit_bytes=58 << 20),
        cost_estimate=pl.CostEstimate(
            flops=100 * pairs, transcendentals=pairs // HD, bytes_accessed=16 * q.size
        ),
        name="attention_backward",
    )(chunks, listed, *args)


def pair_bit(index, bit):
    return lax.rem(index // (1 << bit), 2)


def pair_of(index, bit):
    return index + (1 - 2 * pair_bit(index, bit)) * (1 << bit)


def all_arrived(bits):
    me = lax.axis_index("fsdp")
    barrier = pltpu.get_barrier_semaphore()
    for bit in range(bits):
        pl.semaphore_signal(
            barrier, inc=1, device_id={"fsdp": pair_of(me, bit)},
            device_id_type=pl.DeviceIdType.MESH,
        )
    pl.semaphore_signal(
        barrier, inc=1, device_id={"seq": 1 - lax.axis_index("seq")},
        device_id_type=pl.DeviceIdType.MESH,
    )
    pl.semaphore_wait(barrier, bits + 1)


def qkv_backward_kernel(
    bits, x_in, dq_in, dk_in, dv_in, w_in, res_in, small_in,
    wq_out, wk_out, wv_out, small_out, tok_out,
    x, xt, grads, w, wt, res, tok, kept, sends, lands, final, small, small_land, result,
    in_sem, tok_send, tok_land, own_sem, send_sem, land_sem, x_send, x_land,
    small_send, small_recv, out_sem,
):
    me, side = lax.axis_index("fsdp"), lax.axis_index("seq")
    half = tok.shape[2] * tok.shape[1]
    piece, pieces = tok.shape[2], tok.shape[1]
    own, width = wq_out.shape
    owners = 1 << bits
    sources = (dq_in, dk_in, dv_in)
    loads = [
        pltpu.make_async_copy(w_in.at[:, pl.ds(0, 3 * width)], w, in_sem.at[0]),
        pltpu.make_async_copy(res_in, res, in_sem.at[1]),
        pltpu.make_async_copy(small_in, small.at[0], in_sem.at[2]),
        pltpu.make_async_copy(x_in, x, in_sem.at[3]),
    ] + [pltpu.make_async_copy(sources[i], grads.at[i], in_sem.at[4 + i]) for i in range(3)]
    for i in (0, 3, 4, 5, 6, 1, 2):
        loads[i].start()
    all_arrived(bits)
    loads[0].wait()
    for i in range(3):
        wt[i * width : (i + 1) * width, :] = w[:, i * width : (i + 1) * width].T
    loads[3].wait()

    def turn(r, _):
        xt[r] = x[pl.ds(pl.multiple_of(r * piece, piece), piece), :].T
        return 0

    lax.fori_loop(0, 2 * pieces, turn, 0)
    for i in (4, 5, 6, 1):
        loads[i].wait()

    def token_rows(start):
        total = res[pl.ds(start, piece), :].astype(jnp.float32)
        for i in range(3):
            total = total + dot_f32(
                grads[i, pl.ds(start, piece), :], wt[i * width : (i + 1) * width, :]
            )
        return total.astype(jnp.bfloat16)

    def sent(i):
        return pltpu.make_async_remote_copy(
            src_ref=tok.at[0, i],
            dst_ref=tok_out.at[side, pl.ds(pl.multiple_of(i * piece, piece), piece)],
            send_sem=tok_send.at[i], recv_sem=tok_land.at[i],
            device_id={"seq": 1 - side}, device_id_type=pl.DeviceIdType.MESH,
        )

    def landed(i):
        return pltpu.make_async_remote_copy(
            src_ref=tok.at[0, i],
            dst_ref=tok_out.at[1 - side, pl.ds(pl.multiple_of(i * piece, piece), piece)],
            send_sem=tok_send.at[i], recv_sem=tok_land.at[i],
            device_id={"seq": 1 - side}, device_id_type=pl.DeviceIdType.MESH,
        )

    def stays(i):
        return pltpu.make_async_copy(
            tok.at[1, i],
            tok_out.at[side, pl.ds(pl.multiple_of(i * piece, piece), piece)],
            own_sem.at[i],
        )

    def send_piece(i, _):
        start = pl.multiple_of((1 - side) * half + i * piece, piece)
        tok[0, i] = token_rows(start)
        sent(i).start()
        return 0

    lax.fori_loop(0, pieces, send_piece, 0)

    def keep_piece(i, _):
        start = pl.multiple_of(side * half + i * piece, piece)
        tok[1, i] = token_rows(start)
        stays(i).start()
        return 0

    low_bit = pair_bit(me, 0) == 0
    tile = 8 if owners % 8 == 0 else owners
    first_of = [0]
    for bit in range(bits):
        first_of.append(first_of[-1] + (owners >> (bit + 1)))

    def weights(i):
        def rows(m, _):
            rows_here = pl.ds(pl.multiple_of(m * tile * own, tile * own), tile * own)
            block = dot_f32(
                jnp.concatenate([xt[r, rows_here, :] for r in range(2 * pieces)], axis=1), grads[i]
            ).reshape(tile // 2, 2, own, width)
            even, odd = block[:, 0], block[:, 1]
            spot = pl.ds(m * (tile // 2), tile // 2)
            kept[i, spot] = jnp.where(low_bit, even, odd)
            sends[i, spot] = jnp.where(low_bit, odd, even).astype(jnp.bfloat16)
            return 0

        lax.fori_loop(0, owners // tile, rows, 0)

    def hop(i, bit):
        count = owners >> (bit + 1)
        spot = pl.ds(first_of[bit], count)
        return pltpu.make_async_remote_copy(
            src_ref=sends.at[i, spot], dst_ref=lands.at[i, spot],
            send_sem=send_sem.at[i, bit], recv_sem=land_sem.at[i, bit],
            device_id={"fsdp": pair_of(me, bit)}, device_id_type=pl.DeviceIdType.MESH,
        )

    def cross(i):
        return pltpu.make_async_remote_copy(
            src_ref=final.at[0, i], dst_ref=final.at[1, i],
            send_sem=x_send.at[i], recv_sem=x_land.at[i],
            device_id={"seq": 1 - side}, device_id_type=pl.DeviceIdType.MESH,
        )

    def advance(i, bit):
        hop(i, bit).wait_recv()
        base = first_of[bit]
        if bit + 1 == bits:
            total = kept[i, base] + lands[i, base].astype(jnp.float32)
            final[0, i] = total.astype(jnp.bfloat16)
            cross(i).start()
            return
        nxt = pair_bit(me, bit + 1)

        def one(j, _):
            stay, go = 2 * j + nxt, 2 * j + 1 - nxt
            kept[i, first_of[bit + 1] + j] = kept[i, base + stay] + lands[
                i, base + stay
            ].astype(jnp.float32)
            sends[i, first_of[bit + 1] + j] = (
                kept[i, base + go] + lands[i, base + go].astype(jnp.float32)
            ).astype(jnp.bfloat16)
            return 0

        lax.fori_loop(0, owners >> (bit + 2), one, 0)
        hop(i, bit + 1).start()

    outs = (wq_out, wk_out, wv_out)

    def written(i):
        return pltpu.make_async_copy(result.at[i], outs[i], out_sem.at[i])

    def finish(i):
        cross(i).wait_recv()
        result[i] = final[0, i].astype(jnp.float32) + final[1, i].astype(jnp.float32)
        written(i).start()

    def small_hop(bit):
        where = {"fsdp": pair_of(me, bit)} if bit < bits else {"seq": 1 - side}
        return pltpu.make_async_remote_copy(
            src_ref=small.at[bit], dst_ref=small_land.at[bit],
            send_sem=small_send.at[bit], recv_sem=small_recv.at[bit],
            device_id=where, device_id_type=pl.DeviceIdType.MESH,
        )

    def small_advance(bit):
        small_hop(bit).wait_recv()
        small[bit + 1] = small[bit] + small_land[bit]
        if bit < bits:
            small_hop(bit + 1).start()

    loads[2].wait()
    weights(0)
    hop(0, 0).start()
    for spot, i in ((0, 0), (1, 2)):
        def column_sums(c, total):
            block = grads[i, pl.ds(pl.multiple_of(c * 128, 128), 128), :].astype(jnp.float32)
            return total + jnp.sum(block.reshape(16, 8, width), axis=0)

        total = lax.fori_loop(
            0, grads.shape[1] // 128, column_sums, jnp.zeros((8, width), jnp.float32)
        )
        small[0, spot : spot + 1] = jnp.sum(total, axis=0, keepdims=True)
    small_hop(0).start()
    weights(1)
    hop(1, 0).start()
    advance(0, 0)
    small_advance(0)
    weights(2)
    hop(2, 0).start()
    plan = []
    for step in range(1, bits + 2):
        todo = []
        for i in range(3):
            bit = step - i
            if 0 <= bit < bits:
                todo.append((i, bit))
        plan.append((todo, step))
    done = 0
    for todo, step in plan:
        for i, bit in todo:
            advance(i, bit)
        if step <= bits:
            small_advance(step)
        if done < pieces:
            keep_piece(done, 0)
            done += 1
    for i in range(3):
        finish(i)
    small_copy = pltpu.make_async_copy(small.at[bits + 1], small_out, out_sem.at[3])
    small_copy.start()
    while done < pieces:
        keep_piece(done, 0)
        done += 1
    for i in range(3):
        written(i).wait()
        cross(i).wait_send()
        for bit in range(bits):
            hop(i, bit).wait_send()
    for bit in range(bits + 1):
        small_hop(bit).wait_send()
    small_copy.wait()
    for i in range(pieces):
        stays(i).wait()
        sent(i).wait_send()
        landed(i).wait_recv()


def qkv_backward(x, dq, dk, dv, w, resid, small, own):
    tokens, width = dq.shape
    bits = lax.axis_size("fsdp").bit_length() - 1
    owners = 1 << bits
    pieces = 4
    piece = tokens // 2 // pieces
    dma = pltpu.SemaphoreType.DMA
    f32, bf16 = jnp.float32, jnp.bfloat16
    shard = jax.ShapeDtypeStruct((own, width), f32)
    anywhere = pl.BlockSpec(memory_space=pl.ANY)
    return pl.pallas_call(
        functools.partial(qkv_backward_kernel, bits),
        out_shape=(
            shard, shard, shard,
            jax.ShapeDtypeStruct(small.shape, f32),
            jax.ShapeDtypeStruct((2, tokens // 2, width), bf16),
        ),
        in_specs=[anywhere] * 7,
        out_specs=(anywhere,) * 5,
        scratch_shapes=[
            pltpu.VMEM((tokens, width), bf16),
            pltpu.VMEM((2 * pieces, width, piece), bf16),
            pltpu.VMEM((3, tokens, width), bf16),
            pltpu.VMEM((width, 3 * width), bf16),
            pltpu.VMEM((3 * width, width), bf16),
            pltpu.VMEM((tokens, width), bf16),
            pltpu.VMEM((2, pieces, piece, width), bf16),
            pltpu.VMEM((3, owners - 1, own, width), f32),
            pltpu.VMEM((3, owners - 1, own, width), bf16),
            pltpu.VMEM((3, owners - 1, own, width), bf16),
            pltpu.VMEM((2, 3, own, width), bf16),
            pltpu.VMEM((bits + 2,) + small.shape, f32),
            pltpu.VMEM((bits + 1,) + small.shape, f32),
            pltpu.VMEM((3, own, width), f32),
            dma((7,)), dma((pieces,)), dma((pieces,)), dma((pieces,)),
            dma((3, bits)), dma((3, bits)), dma((3,)), dma((3,)),
            dma((bits + 1,)), dma((bits + 1,)), dma((4,)),
        ],
        compiler_params=pltpu.CompilerParams(
            collective_id=1, has_side_effects=True, vmem_limit_bytes=60 << 20
        ),
        cost_estimate=pl.CostEstimate(
            flops=40 * tokens * width * width, transcendentals=0,
            bytes_accessed=16 * tokens * width,
        ),
        name="qkv_backward",
    )(x, dq, dk, dv, w, resid, small)


eps_norm = 1e-06


def dot_rows(left, right):
    return lax.dot_general(
        left, right, (((0,), (0,)), ((), ())), preferred_element_type=jnp.float32
    )


def dot_nt(left, right):
    return lax.dot_general(
        left, right, (((1,), (1,)), ((), ())), preferred_element_type=jnp.float32
    )


def row_mean(values):
    return jnp.mean(values, axis=-1, keepdims=True)


GELU_K = math.sqrt(2.0 / math.pi)
GELU_A = 0.044715


def gelu_pair(u):
    square = u * u
    t = jnp.tanh(u * (GELU_K + (GELU_K * GELU_A) * square))
    half = 0.5 + 0.5 * t
    slope = half + (u * (half * (1.0 - t))) * (GELU_K + (3.0 * GELU_K * GELU_A) * square)
    return u * half, slope


OUT_B, GAIN_1, BIAS_1, OUTER_B, GAIN_2, BIAS_2, INNER_B = 2, 3, 4, 5, 6, 7, 8
STEP_ROWS = 64
SMALL_ROWS = 16


def middle_kernel(
    chunks, weights_in, small, att, tokens, cotangent,
    out, d_attn, d_att, d_weights, sums,
    w, acc, act, slope, z_one, flow, rs_one, normed, normed_t, d_mlp, load_sem, store_sem,
):
    step, steps = pl.program_id(0), pl.num_programs(0)
    rows, width = att.shape
    f32, bf16 = jnp.float32, jnp.bfloat16
    count = 2 * chunks + 1

    def load(i):
        return pltpu.make_async_copy(
            weights_in.at[:, pl.ds(i * width, width)], w.at[i], load_sem.at[i]
        )

    def store(i):
        return pltpu.make_async_copy(
            w.at[i], d_weights.at[:, pl.ds(i * width, width)], store_sem.at[i]
        )

    @pl.when(step == 0)
    def _():
        for i in range(count):
            load(i).start()
        sums[...] = jnp.zeros_like(sums)

        def clear(i, _):
            acc[i] = jnp.zeros_like(acc[i])
            return 0

        lax.fori_loop(0, count, clear, 0)
        for i in range(count):
            load(i).wait()

    def vector(i):
        return small[i : i + 1, :]

    def add_sum(i, values):
        sums[pl.ds(i, 1), :] += jnp.sum(values, axis=0, keepdims=True)

    def by_rows(body):
        def one(r, _):
            body(pl.ds(pl.multiple_of(r * STEP_ROWS, STEP_ROWS), STEP_ROWS))
            return 0

        lax.fori_loop(0, rows // STEP_ROWS, one, 0)

    flow[...] = dot_f32(att[...], w[0])

    def norm_one(r):
        attn = flow[r, :] + vector(OUT_B)
        resid = tokens[r, :].astype(f32) + attn
        add_sum(INNER_B + chunks, resid * resid)
        add_sum(INNER_B + chunks + 1, attn * attn)
        centred = resid - row_mean(resid)
        scale = lax.rsqrt(row_mean(centred * centred) + eps_norm)
        z = centred * scale
        z_one[r, :] = z
        rs_one[r, :] = scale
        normed[r, :] = (z * vector(GAIN_1) + vector(BIAS_1)).astype(bf16)

    by_rows(norm_one)
    normed_t[...] = normed[...].T

    def inner(c, _):
        for n in range(width // 256):
            cols = slice(n * 256, n * 256 + 256)
            pre = dot_f32(normed[...], w[1 + c, :, cols]) + small[pl.ds(INNER_B + c, 1), cols]
            value, grade = gelu_pair(pre)
            act[c, :, cols] = value.astype(bf16)
            slope[c, :, cols] = grade.astype(bf16)
        return 0

    lax.fori_loop(0, chunks, inner, 0)
    flow[...] = dot_f32(act[0], w[1 + chunks])

    def outer(c, _):
        flow[...] += dot_f32(act[c], w[1 + chunks + c])
        return 0

    lax.fori_loop(1, chunks, outer, 0)

    def norm_two(r):
        mlp = flow[r, :] + vector(OUTER_B)
        add_sum(INNER_B + chunks + 2, mlp * mlp)
        resid = z_one[r, :] * vector(GAIN_1) + vector(BIAS_1) + mlp
        centred = resid - row_mean(resid)
        scale = lax.rsqrt(row_mean(centred * centred) + eps_norm)
        z = centred * scale
        out[r, :] = (z * vector(GAIN_2) + vector(BIAS_2)).astype(bf16)
        grad = cotangent[r, :].astype(f32)
        add_sum(GAIN_2, grad * z)
        add_sum(BIAS_2, grad)
        grad = grad * vector(GAIN_2)
        d_resid = scale * (grad - row_mean(grad) - z * row_mean(grad * z))
        low = d_resid.astype(bf16)
        add_sum(OUTER_B, low.astype(f32))
        d_mlp[r, :] = low
        flow[r, :] = d_resid

    by_rows(norm_two)

    def back(c, _):
        for n in range(width // 256):
            cols = slice(n * 256, n * 256 + 256)
            d_act = dot_nt(d_mlp[...], w[1 + chunks + c, cols, :])
            d_pre = (slope[c, :, cols].astype(f32) * d_act).astype(bf16)
            sums[pl.ds(INNER_B + c, 1), cols] += jnp.sum(
                d_pre.astype(f32), axis=0, keepdims=True
            )
            slope[c, :, cols] = d_pre
        acc[1 + chunks + c] += dot_rows(act[c], d_mlp[...])
        acc[1 + c] += dot_f32(normed_t[...], slope[c])
        flow[...] += dot_nt(slope[c], w[1 + c])

        @pl.when(step == steps - 1)
        def _():
            for i in (1 + c, 1 + chunks + c):
                w[i] = acc[i].astype(bf16)
                store(i).start()

        return 0

    lax.fori_loop(0, chunks, back, 0)

    def norm_one_back(r):
        grad = flow[r, :]
        z = z_one[r, :]
        add_sum(GAIN_1, grad * z)
        add_sum(BIAS_1, grad)
        grad = grad * vector(GAIN_1)
        d_resid = rs_one[r, :] * (grad - row_mean(grad) - z * row_mean(grad * z))
        low = d_resid.astype(bf16)
        add_sum(OUT_B, low.astype(f32))
        d_attn[r, :] = low

    by_rows(norm_one_back)
    acc[0] += dot_rows(att[...], d_attn[...])
    d_att[...] = dot_nt(d_attn[...], w[0]).astype(bf16)

    @pl.when(step == steps - 1)
    def _():
        w[0] = acc[0].astype(bf16)
        store(0).start()
        for i in range(count):
            store(i).wait()


def middle(weights, small, att, tokens, cotangent):
    tok_count, width = att.shape
    chunks = (weights.shape[1] // width - 1) // 2
    count = 2 * chunks + 1
    rows = 512
    f32, bf16 = jnp.float32, jnp.bfloat16
    tile = pl.BlockSpec((rows, width), lambda i: (i, 0))
    fixed = pl.BlockSpec(small.shape, lambda i: (0, 0), pipeline_mode=pl.Buffered(1))
    anywhere = pl.BlockSpec(memory_space=pl.ANY)
    like = jax.ShapeDtypeStruct((tok_count, width), bf16)
    flops = 6 * tok_count * width * width * count
    return pl.pallas_call(
        functools.partial(middle_kernel, chunks),
        grid=(tok_count // rows,),
        out_shape=(
            like, like, like,
            jax.ShapeDtypeStruct(weights.shape, bf16),
            jax.ShapeDtypeStruct(small.shape, f32),
        ),
        in_specs=[anywhere, fixed, tile, tile, tile],
        out_specs=(tile, tile, tile, anywhere, pl.BlockSpec(small.shape, lambda i: (0, 0))),
        scratch_shapes=[
            pltpu.VMEM((count, width, width), bf16),
            pltpu.VMEM((count, width, width), f32),
            pltpu.VMEM((chunks, rows, width), bf16),
            pltpu.VMEM((chunks, rows, width), bf16),
            pltpu.VMEM((rows, width), f32),
            pltpu.VMEM((rows, width), f32),
            pltpu.VMEM((rows, 1), f32),
            pltpu.VMEM((rows, width), bf16),
            pltpu.VMEM((width, rows), bf16),
            pltpu.VMEM((rows, width), bf16),
            pltpu.SemaphoreType.DMA((count,)),
            pltpu.SemaphoreType.DMA((count,)),
        ],
        compiler_params=pltpu.CompilerParams(vmem_limit_bytes=62 << 20),
        cost_estimate=pl.CostEstimate(
            flops=2 * flops, transcendentals=tok_count * width * chunks,
            bytes_accessed=12 * tok_count * width + 4 * weights.size,
        ),
        name="middle",
    )(weights, small, att, tokens, cotangent)


def contract_rows(left, right):
    return lax.dot_general(
        left, right, (((0,), (0,)), ((), ())), preferred_element_type=jnp.float32
    )


def times_transpose(left, right):
    return lax.dot_general(
        left, right, (((1,), (1,)), ((), ())), preferred_element_type=jnp.float32
    )


def butterfly_sum(values, axis):
    size = lax.axis_size(axis)
    if size & (size - 1):
        return lax.psum(values, axis)
    step = 1
    while step < size:
        pairs = [(i, i ^ step) for i in range(size)]
        values = values + lax.ppermute(values, axis, pairs)
        step *= 2
    return values


def sum_seq(values):
    if lax.axis_size("seq") == 2:
        other = lax.ppermute(values, "seq", [(0, 1), (1, 0)])
        return values.astype(jnp.float32) + other.astype(jnp.float32)
    return lax.psum(values, "seq").astype(jnp.float32)


class Regroup:
    def __init__(self, row_count):
        self.size = lax.axis_size("seq")
        self.ways = math.gcd(row_count, self.size)
        self.parts = self.size // self.ways
        self.rows = row_count // self.ways
        me = lax.axis_index("seq")
        self.place = lax.rem(me, self.ways)
        self.row_group = me // self.parts

    def targets(self, turn):
        ways, parts = self.ways, self.parts
        return [
            (s, ((s % ways + turn) % ways) * parts + s // ways) for s in range(self.size)
        ]

    def move(self, values, pairs):
        if all(a == b for a, b in pairs):
            return values
        return lax.ppermute(values, "seq", pairs)

    def gather(self, values):
        rows, local, width = self.rows, values.shape[1], values.shape[2]
        out = jnp.zeros((rows, self.ways, local, width), values.dtype)
        for turn in range(self.ways):
            pick = lax.rem(self.place + turn, self.ways)
            chunk = lax.dynamic_slice_in_dim(values, pick * rows, rows, 0)
            chunk = self.move(chunk, self.targets(turn))
            spot = lax.rem(self.row_group - turn + self.ways, self.ways)
            out = lax.dynamic_update_slice_in_dim(out, chunk[:, None], spot, 1)
        return out.reshape(rows, self.ways * local, width)

    def scatter(self, values):
        rows, width = self.rows, values.shape[2]
        local = values.shape[1] // self.ways
        values = values.reshape(rows, self.ways, local, width)
        out = jnp.zeros((rows * self.ways, local, width), values.dtype)
        for turn in range(self.ways):
            spot = lax.rem(self.row_group - turn + self.ways, self.ways)
            chunk = lax.dynamic_slice_in_dim(values, spot, 1, 1)[:, 0]
            chunk = self.move(chunk, [(b, a) for a, b in self.targets(turn)])
            pick = lax.rem(self.place + turn, self.ways)
            out = lax.dynamic_update_slice_in_dim(out, chunk, pick * rows, 0)
        return out

    def pick_rows(self, values):
        return lax.dynamic_slice_in_dim(values, self.row_group * self.rows, self.rows, 0)

    def groups(self):
        return [
            [r * self.parts + j for j in range(self.parts)] for r in range(self.ways)
        ]

    def to_heads(self, values):
        if self.parts == 1:
            return values
        return lax.all_to_all(
            values, "seq", split_axis=2, concat_axis=1, tiled=True,
            axis_index_groups=self.groups(),
        )

    def from_heads(self, values):
        if self.parts == 1:
            return values
        return lax.all_to_all(
            values, "seq", split_axis=1, concat_axis=2, tiled=True,
            axis_index_groups=self.groups(),
        )


def shards(
    tokens_in,
    segment_ids,
    random_blocks,
    global_blocks,
    w_query,
    b_query,
    w_key,
    w_value,
    b_value,
    w_attn_out,
    b_attn_out,
    ln1_gain,
    ln1_bias,
    w_inner,
    b_inner,
    w_outer,
    b_outer,
    ln2_gain,
    ln2_bias,
    out_grad,
):
    row_count, local_len, width = tokens_in.shape
    seq_count = lax.axis_size("seq")
    fsdp_count = lax.axis_size("fsdp")
    tok_count = row_count * local_len
    own = w_query.shape[0]
    chunks = b_inner.shape[0] // own
    regroup = Regroup(row_count)
    paired = row_count == 2 and seq_count == 2 and fsdp_count & (fsdp_count - 1) == 0

    vectors = [b_query, b_value, b_attn_out, ln1_gain, ln1_bias, b_outer, ln2_gain, ln2_bias]
    columns = [x[:, None] for x in vectors] + [b_inner.reshape(own, chunks)]
    used = len(vectors) + chunks
    columns.append(jnp.zeros((own, 128 - used), jnp.bfloat16))
    first = jnp.concatenate([w_query, w_key, w_value] + columns, axis=1)
    first = lax.all_gather(first, "fsdp", axis=0, tiled=True)
    inner_own = w_inner.reshape(own, width, chunks).transpose(0, 2, 1).reshape(own, -1)
    second = jnp.concatenate([w_attn_out, inner_own, w_outer.reshape(own, -1)], axis=1)
    second = lax.all_gather(second, "fsdp", axis=0, tiled=True)
    qkv_w = first[:, : 3 * width]
    small = first[:, 3 * width : 3 * width + SMALL_ROWS].astype(jnp.float32).T

    flat_in = regroup.gather(tokens_in).reshape(tok_count, width)
    plan = plan_blocks(
        regroup.pick_rows(segment_ids),
        regroup.pick_rows(random_blocks),
        regroup.pick_rows(global_blocks),
    )

    def split_rows(values):
        return values.reshape(regroup.rows, tok_count // regroup.rows, width)

    qkv_bias = jnp.concatenate([small[0], jnp.zeros_like(small[0]), small[1]])
    qkv = (jnp.dot(flat_in, qkv_w, preferred_element_type=jnp.float32) + qkv_bias).astype(
        jnp.bfloat16
    )
    qkv, out_grad = lax.optimization_barrier((qkv, out_grad))
    flat_grad = regroup.gather(out_grad).reshape(tok_count, width)
    q, k, v = (
        regroup.to_heads(split_rows(qkv[:, i * width : (i + 1) * width])) for i in range(3)
    )
    att, lse = attention_forward(q, k, v, plan)
    att_flat = regroup.from_heads(att).reshape(tok_count, width)
    out_tokens, d_attn, d_att, d_second, sums = middle(
        second, small, att_flat, flat_in, flat_grad
    )
    out_tokens = regroup.scatter(split_rows(out_tokens))

    def scattered(values):
        return lax.psum_scatter(values, "fsdp", scatter_dimension=0, tiled=True)

    d_second = scattered(d_second)
    d_att, out_tokens = lax.optimization_barrier((d_att, out_tokens))
    dq, dk, dv = attention_backward(
        q, k, v, att, regroup.to_heads(split_rows(d_att)), lse, plan
    )
    dq, dk, dv = (regroup.from_heads(x).reshape(tok_count, width) for x in (dq, dk, dv))
    mine = lax.axis_index("fsdp")
    if paired:
        d_query_w, d_key_w, d_value_w, sums, d_tokens_in = qkv_backward(
            flat_in, dq, dk, dv, first, d_attn, sums, own
        )
    else:
        for spot, part in ((0, dq), (1, dv)):
            sums = sums.at[spot].set(jnp.sum(part.astype(jnp.float32), axis=0))
        sums = butterfly_sum(butterfly_sum(sums, "fsdp"), "seq")
        d_query_w, d_key_w, d_value_w = (
            sum_seq(scattered(contract_rows(flat_in, x).astype(jnp.bfloat16)))
            for x in (dq, dk, dv)
        )
        d_tokens = d_attn.astype(jnp.float32)
        for i, part in enumerate((dq, dk, dv)):
            d_tokens = d_tokens + times_transpose(part, qkv_w[:, i * width : (i + 1) * width])
        d_tokens_in = regroup.scatter(split_rows(d_tokens.astype(jnp.bfloat16)))
    d_second = sum_seq(d_second)
    d_inner_w = (
        d_second[:, width : (1 + chunks) * width]
        .reshape(own, chunks, width)
        .transpose(0, 2, 1)
        .reshape(own, -1)
    )
    d_outer_w = d_second[:, (1 + chunks) * width :].reshape(own * chunks, width)
    d_vec = lax.dynamic_slice_in_dim(sums, mine * own, own, 1)
    entry_total = tok_count * width * seq_count * fsdp_count
    rms_values = jnp.sqrt(
        jnp.sum(sums[INNER_B + chunks : INNER_B + chunks + 3], axis=1) / entry_total
    )
    return (
        out_tokens,
        d_tokens_in,
        d_query_w,
        d_vec[0],
        d_key_w,
        d_value_w,
        d_vec[1],
        d_second[:, :width],
        d_vec[OUT_B],
        d_vec[GAIN_1],
        d_vec[BIAS_1],
        d_inner_w,
        d_vec[INNER_B : INNER_B + chunks].T.reshape(-1),
        d_outer_w,
        d_vec[OUTER_B],
        d_vec[GAIN_2],
        d_vec[BIAS_2],
        rms_values,
    )


def solution(mesh):
    in_specs = (
        P("fsdp", "seq", None),
        P("fsdp", None),
        P("fsdp", None, None),
        P("fsdp", None),
        P("fsdp", None),
        P("fsdp"),
        P("fsdp", None),
        P("fsdp", None),
        P("fsdp"),
        P("fsdp", None),
        P("fsdp"),
        P("fsdp"),
        P("fsdp"),
        P("fsdp", None),
        P("fsdp"),
        P("fsdp", None),
        P("fsdp"),
        P("fsdp"),
        P("fsdp"),
        P("fsdp", "seq", None),
    )
    out_specs = (
        P("fsdp", "seq", None),
        P("fsdp", "seq", None),
        P("fsdp", None),
        P("fsdp"),
        P("fsdp", None),
        P("fsdp", None),
        P("fsdp"),
        P("fsdp", None),
        P("fsdp"),
        P("fsdp"),
        P("fsdp"),
        P("fsdp", None),
        P("fsdp"),
        P("fsdp", None),
        P("fsdp"),
        P("fsdp"),
        P("fsdp"),
        P(),
    )
    return jax.shard_map(shards, mesh=mesh, in_specs=in_specs, out_specs=out_specs, check_vma=False)
```

profile of v0, /device:TPU:0, one launch (start us, length us, event | category | flops | bytes accessed | tf_op | source)
XLA Modules:
  0.0 485.2 jit_solution(17964220448519089272)
XLA Ops:
  8.0 0.8 copy.68
  8.8 0.8 copy.69
  9.5 0.9 copy.70
  10.4 0.8 copy.71
  11.3 0.8 copy.72
  12.8 0.8 copy.74
  13.5 0.8 reshape.729
  14.3 1.8 concatenate.16
  16.1 2.1 copy.65
  18.3 2.2 copy.66
  20.5 1.0 copy.80
  21.5 1.9 reshape.728
  23.4 1.8 pad_maximum_fusion
  25.3 1.3 constant_dynamic-slice_fusion.2
  26.6 2.9 collective-permute-start
  32.5 1.9 broadcast.463.clone
  34.4 1.2 bitcast_dynamic-update-slice_fusion.4
  35.7 28.5 %collective-permute-done = bf16[1,1024,768]{2,1,0:T(8,128)(2,1)} collective-permute-done((bf16[1,1024,768]{2,1,0:T(8,128)(2,1)}, bf16[1,1024,768]{2,1,0:T(8,128)(2,1)}, u32[]{:S(2)}, u32[]{:S(2)}) %collective-permute-start) | collective-permute-done | bytes 1572896 | tf_op jit(solution)/shard_map/ppermute | solution.py:905
  64.2 2.7 bitcast_dynamic-update-slice_fusion.3
  66.9 1.0 convert_bitcast_fusion
  68.3 10.3 %add_convert_fusion = bf16[2048,2304]{1,0:T(8,128)(2,1)S(1)} fusion(bf16[2048,768]{1,0:T(8,128)(2,1)} %bitcast.16.tokens.x_in, f32[2304]{0:T(1024)S(1)} %pad_maximum_fusion.1, bf16[768,2432]{1,0:T(8,128)(2,1)} %all-gather.5.cloned.1.call-done.w_in), kind=kOutput, calls=%fused_computation | convolution fusion | flops 7257194496 | bytes 16131072 | tf_op jit(solution)/shard_map/dot_general | solution.py:1010
  78.7 1.3 constant_dynamic-slice_fusion.1
  80.0 1.7 collective-permute-start.1
  81.7 3.7 slice_bitcast_fusion
  85.8 52.2 %attention_forward.1 = (bf16[1,2048,768]{2,1,0:T(8,128)(2,1)S(1)}, f32[1,32,1,768]{3,2,1,0:T(1,128)S(1)}) custom-call(s32[1,32]{1,0:T(1,128)S(1)} %and_select_fusion.n_ref, s32[1,1024]{1,0:T(1,128)S(1)} %compare_select_fusion.list_ref, bf16[1,2048,768]{2,1,0:T(8,128)(2,1)} %get-tuple-element.102.q_ref, bf16[1,2048,768]{2,1,0:T(8,128)(2,1)} %get-tuple-element.101.k_ref, ...), custom_call_target="tpu_custom_call" | custom-call | flops 51539607552 | bytes 12582912 | tf_op jit(solution)/shard_map/attention_forward/pallas_call | solution.py:189
  138.0 1.6 copy-done.5
  140.3 0.8 copy.75.small
  141.0 1.9 broadcast.463
  142.9 1.2 copy-done.10
  144.1 1.2 bitcast_dynamic-update-slice_fusion.2
  145.3 2.8 bitcast_dynamic-update-slice_fusion.1
  148.1 8.8 %all-gather.3.cloned.1.call-done.weights_in = bf16[768,6912]{1,0:T(8,128)(2,1)} async-done(((bf16[48,6912]{1,0:T(8,128)(2,1)}), bf16[768,6912]{1,0:T(8,128)(2,1)}) %all-gather.3.cloned.1.call-update) | async-done | bytes 10616848 | tf_op jit(solution)/shard_map/all_gather | solution.py:995
  156.9 121.9 %middle.1 = (bf16[2048,768]{1,0:T(8,128)(2,1)}, bf16[2048,768]{1,0:T(8,128)(2,1)}, bf16[2048,768]{1,0:T(8,128)(2,1)}, bf16[768,6912]{1,0:T(8,128)(2,1)}, f32[16,768]{1,0:T(8,128)}) custom-call(bf16[768,6912]{1,0:T(8,128)(2,1)} %all-gather.3.cloned.1.call-done.weights_in, f32[16,768]{1,0:T(8,128)} %copy.75.small, bf16[2048,768]{1,0:T(8,128)(2,1)} %bitcast.85, ...), custom_call_target="tpu_custom_call" | custom-call | flops 130459631616 | bytes 40108032 | tf_op jit(solution)/shard_map/middle/pallas_call | solution.py:822
  278.8 1.9 copy-done.11
  280.6 1.3 dynamic-slice_bitcast_fusion
  281.9 1.5 collective-permute-start.2
  283.4 1.9 broadcast_in_dim.113
  285.2 1.2 bitcast_dynamic-update-slice_fusion
  286.5 32.3 %collective-permute-done.2 = bf16[1,1024,768]{2,1,0:T(8,128)(2,1)} collective-permute-done((bf16[1,1024,768]{2,1,0:T(8,128)(2,1)}, bf16[1,1024,768]{2,1,0:T(8,128)(2,1)}, u32[]{:S(2)}, u32[]{:S(2)}) %collective-permute-start.2) | collective-permute-done | bytes 1572896 | tf_op jit(solution)/shard_map/ppermute | solution.py:905
  318.8 2.7 constant_dynamic-update-slice_fusion
  321.4 84.2 %attention_backward.1 = (bf16[1,2048,768]{2,1,0:T(8,128)(2,1)}, bf16[1,2048,768]{2,1,0:T(8,128)(2,1)}, bf16[1,2048,768]{2,1,0:T(8,128)(2,1)}) custom-call(s32[1,32]{1,0:T(1,128)} %copy-done.6, s32[1,1024]{1,0:T(1,128)} %copy-done.4, bf16[1,2048,768]{2,1,0:T(8,128)(2,1)} %get-tuple-element.102.q_ref, bf16[1,2048,768]{2,1,0:T(8,128)(2,1)} %get-tuple-element.101.k_ref, ...), custom_call_target="tpu_custom_call" | custom-call | flops 80530636800 | bytes 25165824 | tf_op jit(solution)/shard_map/attention_backward/pallas_call | solution.py:310
  405.7 58.4 %qkv_backward.1 = (f32[48,768]{1,0:T(8,128)}, f32[48,768]{1,0:T(8,128)}, f32[48,768]{1,0:T(8,128)}, f32[16,768]{1,0:T(8,128)}, bf16[2,1024,768]{2,1,0:T(8,128)(2,1)}) custom-call(bf16[2048,768]{1,0:T(8,128)(2,1)} %bitcast.16.tokens.x_in, bf16[2048,768]{1,0:T(8,128)(2,1)} %bitcast.102, bf16[2048,768]{1,0:T(8,128)(2,1)} %bitcast.103, ...), custom_call_target="tpu_custom_call" | custom-call | flops 48318382080 | bytes 25165824 | tf_op jit(solution)/shard_map/qkv_backward/pallas_call | solution.py:588
  464.1 0.8 dynamic-slice_bitcast_fusion.1
  465.7 1.6 dynamic-slice_bitcast_fusion.2
  467.3 0.9 slice_reduce_fusion.4
  470.6 1.3 copy.78
  471.9 1.0 reshape.742
  472.9 3.8 copy.93
  (87 shorter events, 11.3 us)
Async XLA Ops:
  7.2 23.6 %copy-start = (s32[2,32,3]{1,0,2:T(2,128)S(1)}, s32[2,32,3]{1,0,2:T(2,128)}, u32[]{:S(2)}) copy-start(s32[2,32,3]{1,0,2:T(2,128)} %param.22) | copy-start | bytes 2308
  7.2 16.2 %copy-start.16 = (bf16[48,768]{1,0:T(8,128)(2,1)S(1)}, bf16[48,768]{1,0:T(8,128)(2,1)}, u32[]{:S(2)}) copy-start(bf16[48,768]{1,0:T(8,128)(2,1)} %param.29) | copy-start | bytes 221188
  7.2 59.7 %all-gather.5.cloned.1.call-start = ((), (), s32[]{:S(2)}) async-start(), calls=%async_computation.2 | async-start | bytes 3969024 | tf_op jit(solution)/shard_map/all_gather | solution.py:992
  9.5 15.8 %copy-start.8 = (bf16[2,1024,768]{2,1,0:T(8,128)(2,1)S(1)}, bf16[2,1024,768]{2,1,0:T(8,128)(2,1)}, u32[]{:S(2)}) copy-start(bf16[2,1024,768]{2,1,0:T(8,128)(2,1)} %param.20) | copy-start | bytes 9437188
  16.1 140.8 %all-gather.3.cloned.1.call-start = ((), (), s32[]{:S(2)}) async-start(), calls=%async_computation.1 | async-start | bytes 11280384 | tf_op jit(solution)/shard_map/all_gather | solution.py:995
  20.5 9.5 %copy-start.17 = (s32[2,2048]{1,0:T(2,128)S(1)}, s32[2,2048]{1,0:T(2,128)}, u32[]{:S(2)}) copy-start(s32[2,2048]{1,0:T(2,128)} %param.21) | copy-start | bytes 49156
  20.5 10.3 %copy-start.18 = (s32[2,2]{1,0:T(2,128)S(1)}, s32[2,2]{1,0:T(2,128)}, u32[]{:S(2)}) copy-start(s32[2,2]{1,0:T(2,128)} %param.23) | copy-start | bytes 52
  25.2 380.4 %reduce-scatter.2.cloned.1.call-start = ((), (), s32[]{:S(2)}) async-start(), calls=%async_computation.3 | async-start | bytes 11280384 | tf_op jit(solution)/shard_map/reduce_scatter | solution.py:1026
  26.6 37.6 %collective-permute-start = (bf16[1,1024,768]{2,1,0:T(8,128)(2,1)}, bf16[1,1024,768]{2,1,0:T(8,128)(2,1)}, u32[]{:S(2)}, u32[]{:S(2)}) collective-permute-start(bf16[1,1024,768]{2,1,0:T(8,128)(2,1)} %constant_dynamic-slice_fusion.2), channel_id=1, source_target_pairs={{0,16},{16,0},{1,17},{17,1},{2,18},{18,2},{3,19},{19,3},{4,20},{20... | collective-permute-start | bytes 4718600 | tf_op jit(solution)/shard_map/ppermute | solution.py:905
  32.5 53.2 %copy-start.3 = (s32[1,32,128]{2,1,0:T(8,128)}, s32[1,32,128]{2,1,0:T(8,128)S(1)}, u32[]{:S(2)}) copy-start(s32[1,32,128]{2,1,0:T(8,128)S(1)} %pad_add_fusion) | copy-start | bytes 49156
  35.6 50.1 %copy-start.6 = (s32[1,32]{1,0:T(1,128)}, s32[1,32]{1,0:T(1,128)S(1)}, u32[]{:S(2)}) copy-start(s32[1,32]{1,0:T(1,128)S(1)} %and_select_fusion.n_ref) | copy-start | bytes 388
  35.7 50.1 %copy-start.4 = (s32[1,1024]{1,0:T(1,128)}, s32[1,1024]{1,0:T(1,128)S(1)}, u32[]{:S(2)}) copy-start(s32[1,1024]{1,0:T(1,128)S(1)} %compare_select_fusion.list_ref) | copy-start | bytes 12292
  68.3 10.4 %copy-start.9 = (bf16[2,1024,768]{2,1,0:T(8,128)(2,1)S(1)}, bf16[2,1024,768]{2,1,0:T(8,128)(2,1)}, u32[]{:S(2)}) copy-start(bf16[2,1024,768]{2,1,0:T(8,128)(2,1)} %param.39) | copy-start | bytes 9437188
  80.0 65.3 %collective-permute-start.1 = (bf16[1,1024,768]{2,1,0:T(8,128)(2,1)}, bf16[1,1024,768]{2,1,0:T(8,128)(2,1)}, u32[]{:S(2)}, u32[]{:S(2)}) collective-permute-start(bf16[1,1024,768]{2,1,0:T(8,128)(2,1)} %constant_dynamic-slice_fusion.1), channel_id=1, source_target_pairs={{0,16},{16,0},{1,17},{17,1},{2,18},{18,2},{3,19},{19,3},{4,20},{20... | collective-permute-start | bytes 4718600 | tf_op jit(solution)/shard_map/ppermute | solution.py:905
  85.8 52.2 %copy-start.2 = (s32[1,2112,128]{2,1,0:T(8,128)}, s32[1,2112,128]{2,1,0:T(8,128)S(1)}, u32[]{:S(2)}) copy-start(s32[1,2112,128]{2,1,0:T(8,128)S(1)} %broadcast_in_dim.109.segc_ref) | copy-start | bytes 3244036
  138.0 1.6 copy-start.5
  139.6 0.6 copy-start.7
  141.0 3.0 copy-start.10
  278.7 1.9 copy-start.11
  281.9 36.9 %collective-permute-start.2 = (bf16[1,1024,768]{2,1,0:T(8,128)(2,1)}, bf16[1,1024,768]{2,1,0:T(8,128)(2,1)}, u32[]{:S(2)}, u32[]{:S(2)}) collective-permute-start(bf16[1,1024,768]{2,1,0:T(8,128)(2,1)} %dynamic-slice_bitcast_fusion), channel_id=1, source_target_pairs={{16,0},{0,16},{17,1},{1,17},{18,2},{2,18},{19,3},{3,19},{20,4},{4,... | collective-permute-start | bytes 4718600 | tf_op jit(solution)/shard_map/ppermute | solution.py:905
  405.7 63.0 %collective-permute-start.3 = (bf16[48,6912]{1,0:T(8,128)(2,1)}, bf16[48,6912]{1,0:T(8,128)(2,1)S(1)}, u32[]{:S(2)}, u32[]{:S(2)}) collective-permute-start(bf16[48,6912]{1,0:T(8,128)(2,1)} %reduce-scatter.2.cloned.1.call-done), channel_id=1, source_target_pairs={{0,16},{16,0},{1,17},{17,1},{2,18},{18,2},{3,19},{19,3},{4,20},{20... | collective-permute-start | bytes 1990664 | tf_op jit(solution)/shard_map/ppermute | solution.py:881
  405.7 63.0 %copy-start.12 = (bf16[48,6912]{1,0:T(8,128)(2,1)S(1)}, bf16[48,6912]{1,0:T(8,128)(2,1)}, u32[]{:S(2)}) copy-start(bf16[48,6912]{1,0:T(8,128)(2,1)} %reduce-scatter.2.cloned.1.call-done) | copy-start | bytes 1990660
  472.9 5.8 %copy-start.1 = (s32[2,32,3]{1,0,2:T(2,128)S(1)}, s32[2,32,3]{1,0,2:T(2,128)}, u32[]{:S(2)}) copy-start(s32[2,32,3]{1,0,2:T(2,128)} %param.22) | copy-start | bytes 2308
  472.9 3.8 copy-start.15
  472.9 4.5 copy-start.14
  472.9 5.1 %copy-start.13 = (f32[48,768]{1,0:T(8,128)S(1)}, f32[48,768]{1,0:T(8,128)}, u32[]{:S(2)}) copy-start(f32[48,768]{1,0:T(8,128)} %get-tuple-element.137) | copy-start | bytes 442372
Sparse Core Ops, SparseCore 0:
  16.2 50.5 all-gather.4
  69.1 87.7 all-gather.2
  278.9 118.4 reduce-scatter.1
where the time goes:
time: 485 us
  Pallas kernels  317 us (65%)
  waiting for transfers between devices  69.6 us (14%)
  local copies, waits for them, and re-layouts  62.7 us (13%)
  between operations  14.2 us (3%)
  matrix products  10.3 us (2%)
  starting transfers between devices  6.23 us (1%)
  other arithmetic  5.43 us (1%)
    pallas_call x1, Pallas kernels, middle(): pl.pallas_call(functools.partial(middle_kernel, chunks), grid=(tok_count...  122 us
    pallas_call x1, Pallas kernels, attention_backward(): pl.pallas_call(functools.partial(backward_kernel, group), out_shape=(like...  84.2 us
    ppermute x3, waiting for transfers between devices, move(): return lax.ppermute(values, 'seq', pairs)  60.8 us
    pallas_call x1, Pallas kernels, qkv_backward(): pl.pallas_call(functools.partial(qkv_backward_kernel, bits), out_shape=(s...  58.4 us
    pallas_call x1, Pallas kernels, attention_forward(): pl.pallas_call(functools.partial(forward_kernel, group), out_shape=(jax.S...  52.2 us
    unnamed x46, local copies, waits for them, and re-layouts  15.5 us
    dot_general x1, matrix products, shards(): jnp.dot(flat_in, qkv_w, preferred_element_type=jnp.float32) + qkv_bias  10.3 us
  transfers between devices with their start and end apart: 7, of which 3 were waited for; matrix products, arithmetic and copies ran while one was open for 11% of the time, Pallas kernels for 40%

commit v1 on v0

--- a/solution.py
+++ b/solution.py
@@ -369,7 +369,7 @@
     owners = 1 << bits
     sources = (dq_in, dk_in, dv_in)
     loads = [
-        pltpu.make_async_copy(w_in.at[:, pl.ds(0, 3 * width)], w, in_sem.at[0]),
+        pltpu.make_async_copy(w_in, w, in_sem.at[0]),
         pltpu.make_async_copy(res_in, res, in_sem.at[1]),
         pltpu.make_async_copy(small_in, small.at[0], in_sem.at[2]),
         pltpu.make_async_copy(x_in, x, in_sem.at[3]),
@@ -379,7 +379,8 @@
     all_arrived(bits)
     loads[0].wait()
     for i in range(3):
-        wt[i * width : (i + 1) * width, :] = w[:, i * width : (i + 1) * width].T
+        first = part_start(width, i)
+        wt[i * width : (i + 1) * width, :] = w[:, first : first + width].T
     loads[3].wait()
 
     def turn(r, _):
@@ -598,7 +599,7 @@
             pltpu.VMEM((tokens, width), bf16),
             pltpu.VMEM((2 * pieces, width, piece), bf16),
             pltpu.VMEM((3, tokens, width), bf16),
-            pltpu.VMEM((width, 3 * width), bf16),
+            pltpu.VMEM(w.shape, bf16),
             pltpu.VMEM((3 * width, width), bf16),
             pltpu.VMEM((tokens, width), bf16),
             pltpu.VMEM((2, pieces, piece, width), bf16),
@@ -622,6 +623,198 @@
         ),
         name="qkv_backward",
     )(x, dq, dk, dv, w, resid, small)
+
+
+def qkv_forward_kernel(
+    bits, tokens_in, own_in,
+    x_out, q_out, k_out, v_out, w_out, small_out,
+    x, w, qkv, small,
+    own_sem, tok_send, tok_land, load_sem, send_sem, land_sem, x_sem, out_sem, w_sem, small_sem,
+):
+    me, side = lax.axis_index("fsdp"), lax.axis_index("seq")
+    pieces, piece, width = x.shape[1], x.shape[2], x.shape[3]
+    mine = [pair_bit(me, bit) for bit in range(bits)]
+    columns = part_columns(width)
+    outs = (q_out, k_out, v_out)
+
+    def slot(bit, part):
+        here = [slice(None)] * (bits - 1 - bit) + [mine[b] for b in range(bit, -1, -1)]
+        return tuple(here) + (slice(None), columns[part])
+
+    own_tokens = pltpu.make_async_copy(tokens_in.at[side], x.at[side], own_sem.at[0])
+    own_tokens.start()
+
+    def load(part):
+        spot = tuple(mine[b] for b in range(bits - 1, -1, -1)) + (slice(None), columns[part])
+        return pltpu.make_async_copy(
+            own_in.at[:, columns[part]], w.at[spot], load_sem.at[part]
+        )
+
+    for part in range(3):
+        load(part).start()
+    all_arrived(bits)
+
+    def sent(i):
+        return pltpu.make_async_remote_copy(
+            src_ref=tokens_in.at[1 - side, i], dst_ref=x.at[side, i],
+            send_sem=tok_send.at[i], recv_sem=tok_land.at[i],
+            device_id={"seq": 1 - side}, device_id_type=pl.DeviceIdType.MESH,
+        )
+
+    def landed(i):
+        return pltpu.make_async_remote_copy(
+            src_ref=tokens_in.at[1 - side, i], dst_ref=x.at[1 - side, i],
+            send_sem=tok_send.at[i], recv_sem=tok_land.at[i],
+            device_id={"seq": 1 - side}, device_id_type=pl.DeviceIdType.MESH,
+        )
+
+    def hop(part, turn):
+        bit = bits - 1 - turn
+        return pltpu.make_async_remote_copy(
+            src_ref=w.at[slot(bit, part)], dst_ref=w.at[slot(bit, part)],
+            send_sem=send_sem.at[part, turn], recv_sem=land_sem.at[part, turn],
+            device_id={"fsdp": pair_of(me, bit)}, device_id_type=pl.DeviceIdType.MESH,
+        )
+
+    for part in range(3):
+        load(part).wait()
+        hop(part, 0).start()
+    for i in range(pieces):
+        sent(i).start()
+
+    def x_copy(half, i):
+        return pltpu.make_async_copy(x.at[half, i], x_out.at[half, i], x_sem.at[half, i])
+
+    def out_copy(part, half, i):
+        return pltpu.make_async_copy(
+            qkv.at[part, half, i], outs[part].at[half, i], out_sem.at[part, half, i]
+        )
+
+    def w_copy(part):
+        spot = (slice(None),) * (bits + 1) + (columns[part],)
+        return pltpu.make_async_copy(w.at[spot], w_out.at[spot], w_sem.at[part])
+
+    def project(part, half, i):
+        first = part_start(width, part)
+        spot = (slice(None),) * (bits + 1) + (slice(first, first + width),)
+        total = dot_f32(x[half, i], w[spot].reshape(width, width))
+        if part == 0:
+            total = total + small[0:1, :]
+        if part == 2:
+            total = total + small[1:2, :]
+        qkv[part, half, i] = total.astype(jnp.bfloat16)
+        out_copy(part, half, i).start()
+
+    def each_own(part):
+        def one(i, _):
+            project(part, side, i)
+            return 0
+
+        lax.fori_loop(0, pieces, one, 0)
+
+    def arrived(part):
+        w_copy(part).start()
+        if part == 0:
+            spot = (slice(None),) * (bits + 1) + (slice(width, width + 128),)
+            turned = w[spot].reshape(width, 128).astype(jnp.float32).T
+            small[...] = turned[: small.shape[0]]
+            pltpu.make_async_copy(small, small_out, small_sem.at[0]).start()
+            own_tokens.wait()
+        each_own(part)
+
+    for step in range(bits + 2):
+        full = None
+        for part in range(3):
+            turn = step - part
+            if 0 <= turn < bits:
+                hop(part, turn).wait_recv()
+                if turn + 1 < bits:
+                    hop(part, turn + 1).start()
+                else:
+                    full = part
+        if full is not None:
+            arrived(full)
+    for i in range(pieces):
+        x_copy(side, i).start()
+
+    def other(i, _):
+        landed(i).wait_recv()
+        x_copy(1 - side, i).start()
+        for part in range(3):
+            project(part, 1 - side, i)
+        return 0
+
+    lax.fori_loop(0, pieces, other, 0)
+    for i in range(pieces):
+        sent(i).wait_send()
+    for part in range(3):
+        w_copy(part).wait()
+        for turn in range(bits):
+            hop(part, turn).wait_send()
+    pltpu.make_async_copy(small, small_out, small_sem.at[0]).wait()
+    for half in range(2):
+        for i in range(pieces):
+            x_copy(half, i).wait()
+            for part in range(3):
+                out_copy(part, half, i).wait()
+
+
+def part_start(width, part):
+    return part * width + (128 if part else 0)
+
+
+def part_columns(width):
+    return (
+        slice(0, width + 128),
+        slice(width + 128, 2 * width + 128),
+        slice(2 * width + 128, 3 * width + 128),
+    )
+
+
+def qkv_forward(tokens_in, own_pack):
+    rows, local, width = tokens_in.shape
+    own, columns = own_pack.shape
+    bits = lax.axis_size("fsdp").bit_length() - 1
+    pieces = 4
+    piece = local // pieces
+    dma = pltpu.SemaphoreType.DMA
+    bf16 = jnp.bfloat16
+    halves = (2, pieces, piece, width)
+    gathered = (2,) * bits + (own, columns)
+    anywhere = pl.BlockSpec(memory_space=pl.ANY)
+    like = jax.ShapeDtypeStruct(halves, bf16)
+    x, q, k, v, weights, small = pl.pallas_call(
+        functools.partial(qkv_forward_kernel, bits),
+        out_shape=(
+            like, like, like, like,
+            jax.ShapeDtypeStruct(gathered, bf16),
+            jax.ShapeDtypeStruct((SMALL_ROWS, width), jnp.float32),
+        ),
+        in_specs=[anywhere] * 2,
+        out_specs=(anywhere,) * 6,
+        scratch_shapes=[
+            pltpu.VMEM(halves, bf16),
+            pltpu.VMEM(gathered, bf16),
+            pltpu.VMEM((3,) + halves, bf16),
+            pltpu.VMEM((SMALL_ROWS, width), jnp.float32),
+            dma((1,)), dma((pieces,)), dma((pieces,)), dma((3,)),
+            dma((3, bits)), dma((3, bits)), dma((2, pieces)), dma((3, 2, pieces)),
+            dma((3,)), dma((1,)),
+        ],
+        compiler_params=pltpu.CompilerParams(
+            collective_id=2, has_side_effects=True, vmem_limit_bytes=30 << 20
+        ),
+        cost_estimate=pl.CostEstimate(
+            flops=18 * rows * local * width * width, transcendentals=0,
+            bytes_accessed=16 * rows * local * width,
+        ),
+        name="qkv_forward",
+    )(tokens_in.reshape(halves), own_pack)
+    flat = rows * local, width
+    return (
+        x.reshape(flat), q.reshape(flat), k.reshape(flat), v.reshape(flat),
+        weights.reshape(-1, columns), small,
+    )
 
 
 eps_norm = 1e-06
@@ -988,15 +1181,10 @@
     columns = [x[:, None] for x in vectors] + [b_inner.reshape(own, chunks)]
     used = len(vectors) + chunks
     columns.append(jnp.zeros((own, 128 - used), jnp.bfloat16))
-    first = jnp.concatenate([w_query, w_key, w_value] + columns, axis=1)
-    first = lax.all_gather(first, "fsdp", axis=0, tiled=True)
+    first = jnp.concatenate([w_query] + columns + [w_key, w_value], axis=1)
     inner_own = w_inner.reshape(own, width, chunks).transpose(0, 2, 1).reshape(own, -1)
     second = jnp.concatenate([w_attn_out, inner_own, w_outer.reshape(own, -1)], axis=1)
     second = lax.all_gather(second, "fsdp", axis=0, tiled=True)
-    qkv_w = first[:, : 3 * width]
-    small = first[:, 3 * width : 3 * width + SMALL_ROWS].astype(jnp.float32).T
-
-    flat_in = regroup.gather(tokens_in).reshape(tok_count, width)
     plan = plan_blocks(
         regroup.pick_rows(segment_ids),
         regroup.pick_rows(random_blocks),
@@ -1006,15 +1194,24 @@
     def split_rows(values):
         return values.reshape(regroup.rows, tok_count // regroup.rows, width)
 
-    qkv_bias = jnp.concatenate([small[0], jnp.zeros_like(small[0]), small[1]])
-    qkv = (jnp.dot(flat_in, qkv_w, preferred_element_type=jnp.float32) + qkv_bias).astype(
-        jnp.bfloat16
-    )
-    qkv, out_grad = lax.optimization_barrier((qkv, out_grad))
+    def part_of(values, i):
+        return values[:, part_start(width, i) : part_start(width, i) + width]
+
+    if paired:
+        flat_in, *qkv, first, small = qkv_forward(tokens_in, first)
+    else:
+        first = lax.all_gather(first, "fsdp", axis=0, tiled=True)
+        small = first[:, width : width + SMALL_ROWS].astype(jnp.float32).T
+        flat_in = regroup.gather(tokens_in).reshape(tok_count, width)
+        biases = (small[0], jnp.zeros_like(small[0]), small[1])
+        qkv = [
+            (jnp.dot(flat_in, part_of(first, i), preferred_element_type=jnp.float32)
+             + biases[i]).astype(jnp.bfloat16)
+            for i in range(3)
+        ]
+    q, out_grad = lax.optimization_barrier((qkv[0], out_grad))
     flat_grad = regroup.gather(out_grad).reshape(tok_count, width)
-    q, k, v = (
-        regroup.to_heads(split_rows(qkv[:, i * width : (i + 1) * width])) for i in range(3)
-    )
+    q, k, v = (regroup.to_heads(split_rows(x)) for x in (q, qkv[1], qkv[2]))
     att, lse = attention_forward(q, k, v, plan)
     att_flat = regroup.from_heads(att).reshape(tok_count, width)
     out_tokens, d_attn, d_att, d_second, sums = middle(
@@ -1026,16 +1223,17 @@
         return lax.psum_scatter(values, "fsdp", scatter_dimension=0, tiled=True)
 
     d_second = scattered(d_second)
-    d_att, out_tokens = lax.optimization_barrier((d_att, out_tokens))
     dq, dk, dv = attention_backward(
         q, k, v, att, regroup.to_heads(split_rows(d_att)), lse, plan
     )
     dq, dk, dv = (regroup.from_heads(x).reshape(tok_count, width) for x in (dq, dk, dv))
     mine = lax.axis_index("fsdp")
+    dq, out_tokens = lax.optimization_barrier((dq, out_tokens))
     if paired:
         d_query_w, d_key_w, d_value_w, sums, d_tokens_in = qkv_backward(
             flat_in, dq, dk, dv, first, d_attn, sums, own
         )
+        d_second, sums = lax.optimization_barrier((d_second, sums))
     else:
         for spot, part in ((0, dq), (1, dv)):
             sums = sums.at[spot].set(jnp.sum(part.astype(jnp.float32), axis=0))
@@ -1046,7 +1244,7 @@
         )
         d_tokens = d_attn.astype(jnp.float32)
         for i, part in enumerate((dq, dk, dv)):
-            d_tokens = d_tokens + times_transpose(part, qkv_w[:, i * width : (i + 1) * width])
+            d_tokens = d_tokens + times_transpose(part, part_of(first, i))
         d_tokens_in = regroup.scatter(split_rows(d_tokens.astype(jnp.bfloat16)))
     d_second = sum_seq(d_second)
     d_inner_w = (

time: 485 us -> 469 us (0.967)
  Pallas kernels: 317 us -> 383 us
  waiting for transfers between devices: 69.6 us -> 11.9 us
  local copies, waits for them, and re-layouts: 62.7 us -> 48.6 us
  matrix products: 10.3 us -> 0 us
    pallas_call x0 -> x1, Pallas kernels: none -> 68.6 us  [qkv_forward(): pl.pallas_call(functools.partial(qkv_forward_kernel, bits), out_shape=(li...]
    ppermute x3 -> x2, waiting for transfers between devices: 60.8 us -> 0.01 us  [move(): return lax.ppermute(values, 'seq', pairs)]
    ppermute x1, waiting for transfers between devices: 0.01 us -> 11.9 us  [sum_seq(): other = lax.ppermute(values, 'seq', [(0, 1), (1, 0)])]
    dot_general x1 -> x0, matrix products: 10.3 us -> none  [shards(): jnp.dot(flat_in, qkv_w, preferred_element_type=jnp.float32) + qkv_bias]
    unnamed x46 -> x80, local copies, waits for them, and re-layouts: 15.5 us -> 25 us
    pallas_call x1, Pallas kernels: 58.4 us -> 67.7 us  [qkv_backward(): pl.pallas_call(functools.partial(qkv_backward_kernel, bits), out_shape=(s...]
    all_gather x1, waiting for transfers between devices: 8.77 us -> 0.01 us  [shards(): second = lax.all_gather(second, 'fsdp', axis=0, tiled=True)]
    pallas_call x1, Pallas kernels: 84.2 us -> 77 us  [attention_backward(): pl.pallas_call(functools.partial(backward_kernel, group), out_shape=(like...]
  transfers between devices with their start and end apart: 7 -> 5, of which waited for: 3 -> 1; matrix products, arithmetic and copies ran while one was open for 11% -> 5% of each run, Pallas kernels for 40% -> 56%
where the time goes in v1:
time: 469 us; the launch traced here: 468 us
  Pallas kernels  383 us (82%)
  local copies, waits for them, and re-layouts  48.6 us (10%)
  between operations  14.6 us (3%)
  waiting for transfers between devices  11.9 us (3%)
  starting transfers between devices  5.21 us (1%)
    pallas_call x1, Pallas kernels, middle(): pl.pallas_call(functools.partial(middle_kernel, chunks), grid=(tok_count...  122 us
    pallas_call x1, Pallas kernels, attention_backward(): pl.pallas_call(functools.partial(backward_kernel, group), out_shape=(like...  77 us
    pallas_call x1, Pallas kernels, qkv_forward(): pl.pallas_call(functools.partial(qkv_forward_kernel, bits), out_shape=(li...  68.6 us
    pallas_call x1, Pallas kernels, qkv_backward(): pl.pallas_call(functools.partial(qkv_backward_kernel, bits), out_shape=(s...  67.7 us
    pallas_call x1, Pallas kernels, attention_forward(): pl.pallas_call(functools.partial(forward_kernel, group), out_shape=(jax.S...  47.7 us
    unnamed x80, local copies, waits for them, and re-layouts  25 us
    ppermute x1, waiting for transfers between devices, sum_seq(): other = lax.ppermute(values, 'seq', [(0, 1), (1, 0)])  11.9 us
  transfers between devices with their start and end apart: 5, of which 1 were waited for; matrix products, arithmetic and copies ran while one was open for 5% of the time, Pallas kernels for 56%

profile of v1, /device:TPU:0, one launch (start us, length us, event | category | flops | bytes accessed | tf_op | source)
XLA Modules:
  0.0 468.1 jit_solution(13452630464925893656)
XLA Ops:
  7.4 1.4 copy.71
  8.8 0.6 copy.72
  9.5 1.1 reshape.738
  10.6 0.9 pad_maximum_fusion
  12.8 1.9 copy-done.5
  14.7 68.6 %qkv_forward.1 = (bf16[2,4,256,768]{3,2,1,0:T(8,128)(2,1)S(1)}, bf16[2,4,256,768]{3,2,1,0:T(8,128)(2,1)S(1)}, bf16[2,4,256,768]{3,2,1,0:T(8,128)(2,1)S(1)}, bf16...) custom-call(bf16[2,4,256,768]{3,2,1,0:T(8,128)(2,1)S(1)} %bitcast.78, ...), custom_call_target="tpu_custom_call" | custom-call | flops 21743271936 | bytes 25165824 | tf_op jit(solution)/shard_map/qkv_forward/pallas_call | solution.py:786
  83.3 1.8 copy-done.6
  85.1 1.7 copy-done.7
  86.8 1.7 copy-done.8
  88.5 1.7 copy-done.9
  90.2 1.7 copy-done.10
  91.9 0.6 copy-done.13
  92.5 1.3 constant_dynamic-slice_fusion.1
  93.8 3.7 collective-permute-start
  97.6 0.5 broadcast.470
  98.1 0.7 fusion.15
  99.6 0.4 select_reduce_fusion
  101.0 47.7 %attention_forward.1 = (bf16[1,2048,768]{2,1,0:T(8,128)(2,1)S(1)}, f32[1,32,1,768]{3,2,1,0:T(1,128)S(1)}) custom-call(s32[1,32]{1,0:T(1,128)S(1)} %and_select_fusion.n_ref, s32[1,1024]{1,0:T(1,128)S(1)} %compare_select_fusion.list_ref, bf16[1,2048,768]{2,1,0:T(8,128)(2,1)} %bitcast.82, bf16[1,2048,768]{2,1,0:T(8,128)(2,1)} %bitcast.84, ...), custom_call_target="tpu_custom_call" | custom-call | flops 51539607552 | bytes 12582912 | tf_op jit(solution)/shard_map/attention_forward/pallas_call | solution.py:189
  148.7 1.6 copy-done.11
  150.3 0.6 copy-done.14
  150.9 1.9 broadcast_in_dim.101
  152.9 1.1 copy-done.16
  154.0 1.2 bitcast_dynamic-update-slice_fusion.2
  155.2 2.7 bitcast_dynamic-update-slice_fusion.1
  157.9 122.1 %middle.1 = (bf16[2048,768]{1,0:T(8,128)(2,1)}, bf16[2048,768]{1,0:T(8,128)(2,1)}, bf16[2048,768]{1,0:T(8,128)(2,1)}, bf16[768,6912]{1,0:T(8,128)(2,1)}, f32[16,768]{1,0:T(8,128)}) custom-call(bf16[768,6912]{1,0:T(8,128)(2,1)} %all-gather.2.cloned.1.call-done.weights_in, f32[16,768]{1,0:T(8,128)} %copy-done.13, bf16[2048,768]{1,0:T(8,128)(2,1)} %bitcast.88, ...), custom_call_target="tpu_custom_call" | custom-call | flops 130459631616 | bytes 40108032 | tf_op jit(solution)/shard_map/middle/pallas_call | solution.py:1015
  280.1 1.9 copy-done.17
  281.9 1.3 dynamic-slice_bitcast_fusion
  283.2 1.1 collective-permute-start.1
  284.3 77.0 %attention_backward.1 = (bf16[1,2048,768]{2,1,0:T(8,128)(2,1)}, bf16[1,2048,768]{2,1,0:T(8,128)(2,1)}, bf16[1,2048,768]{2,1,0:T(8,128)(2,1)}) custom-call(s32[1,32]{1,0:T(1,128)} %copy-done.12, s32[1,1024]{1,0:T(1,128)} %copy-done.4, bf16[1,2048,768]{2,1,0:T(8,128)(2,1)} %bitcast.83, bf16[1,2048,768]{2,1,0:T(8,128)(2,1)} %bitcast.85, ...), custom_call_target="tpu_custom_call" | custom-call | flops 80530636800 | bytes 25165824 | tf_op jit(solution)/shard_map/attention_backward/pallas_call | solution.py:310
  361.3 1.9 broadcast_in_dim.104
  363.2 1.2 bitcast_dynamic-update-slice_fusion
  364.4 1.2 constant_dynamic-update-slice_fusion
  365.7 67.7 %qkv_backward.1 = (f32[48,768]{1,0:T(8,128)}, f32[48,768]{1,0:T(8,128)}, f32[48,768]{1,0:T(8,128)}, f32[16,768]{1,0:T(8,128)}, bf16[2,1024,768]{2,1,0:T(8,128)(2,1)}) custom-call(bf16[2048,768]{1,0:T(8,128)(2,1)} %bitcast.81, bf16[2048,768]{1,0:T(8,128)(2,1)} %bitcast.104, bf16[2048,768]{1,0:T(8,128)(2,1)} %bitcast.105, bf16[2048,768]{1,0:T(8,128)(2,1)} %bitcast.106, ...), custom_call_target="tpu_custom_call" | custom-call | flops 48318382080 | bytes 25165824 | tf_op jit(solution)/shard_map/qkv_backward/pallas_call | solution.py:589
  433.7 0.8 dynamic-slice_bitcast_fusion.1
  434.6 0.7 reshape.748
  435.2 1.6 dynamic-slice_bitcast_fusion.2
  436.8 0.9 slice_reduce_fusion.2
  437.7 0.5 multiply_sqrt_fusion
  438.2 11.9 %collective-permute-done.2 = bf16[48,6912]{1,0:T(8,128)(2,1)S(1)} collective-permute-done((bf16[48,6912]{1,0:T(8,128)(2,1)}, bf16[48,6912]{1,0:T(8,128)(2,1)S(1)}, u32[]{:S(2)}, u32[]{:S(2)}) %collective-permute-start.2) | collective-permute-done | bytes 663584 | tf_op jit(solution)/shard_map/ppermute | solution.py:1074
  450.1 1.3 convert_add_fusion
  451.5 0.7 slice.62
  452.4 0.7 copy.73
  453.2 1.3 copy.75
  454.5 1.0 reshape.749
  455.4 3.8 copy.88
  459.3 0.7 copy.89
  459.9 0.7 copy.90
  460.6 0.7 copy.91
  (106 shorter events, 3.9 us)
Async XLA Ops:
  7.2 91.6 %copy-start = (s32[2,32,3]{1,0,2:T(2,128)S(1)}, s32[2,32,3]{1,0,2:T(2,128)}, u32[]{:S(2)}) copy-start(s32[2,32,3]{1,0,2:T(2,128)} %param.22) | copy-start | bytes 2308
  7.2 3.4 copy-start.24
  7.2 4.3 copy-start.26
  7.2 4.5 copy-start.27
  7.2 4.6 copy-start.28
  7.3 4.7 copy-start.29
  7.3 4.8 %copy-start.30 = (bf16[48]{0:T(256)(128)(2,1)S(1)}, bf16[48]{0:T(256)(128)(2,1)}, u32[]{:S(2)}) copy-start(bf16[48]{0:T(256)(128)(2,1)} %param.32) | copy-start | bytes 292
  7.3 4.9 %copy-start.31 = (bf16[48]{0:T(256)(128)(2,1)S(1)}, bf16[48]{0:T(256)(128)(2,1)}, u32[]{:S(2)}) copy-start(bf16[48]{0:T(256)(128)(2,1)} %param.36) | copy-start | bytes 292
  7.3 5.0 %copy-start.32 = (bf16[48]{0:T(256)(128)(2,1)S(1)}, bf16[48]{0:T(256)(128)(2,1)}, u32[]{:S(2)}) copy-start(bf16[48]{0:T(256)(128)(2,1)} %param.37) | copy-start | bytes 292
  7.3 5.1 %copy-start.33 = (bf16[48]{0:T(256)(128)(2,1)S(1)}, bf16[48]{0:T(256)(128)(2,1)}, u32[]{:S(2)}) copy-start(bf16[48]{0:T(256)(128)(2,1)} %param.38) | copy-start | bytes 292
  7.3 5.2 %copy-start.34 = (bf16[192]{0:T(256)(128)(2,1)S(1)}, bf16[192]{0:T(256)(128)(2,1)}, u32[]{:S(2)}) copy-start(bf16[192]{0:T(256)(128)(2,1)} %param.34) | copy-start | bytes 1156
  7.3 5.3 %copy-start.21 = (bf16[48,768]{1,0:T(8,128)(2,1)S(1)}, bf16[48,768]{1,0:T(8,128)(2,1)}, u32[]{:S(2)}) copy-start(bf16[48,768]{1,0:T(8,128)(2,1)} %param.24) | copy-start | bytes 221188
  7.3 5.3 %copy-start.22 = (bf16[48,768]{1,0:T(8,128)(2,1)S(1)}, bf16[48,768]{1,0:T(8,128)(2,1)}, u32[]{:S(2)}) copy-start(bf16[48,768]{1,0:T(8,128)(2,1)} %param.26) | copy-start | bytes 221188
  7.3 5.3 %copy-start.23 = (bf16[48,768]{1,0:T(8,128)(2,1)S(1)}, bf16[48,768]{1,0:T(8,128)(2,1)}, u32[]{:S(2)}) copy-start(bf16[48,768]{1,0:T(8,128)(2,1)} %param.27) | copy-start | bytes 221188
  7.3 150.5 %all-gather.2.cloned.1.call-start = ((), (), s32[]{:S(2)}) async-start(), calls=%async_computation.1 | async-start | bytes 11280384 | tf_op jit(solution)/shard_map/all_gather | solution.py:1187
  11.5 421.9 %reduce-scatter.2.cloned.1.call-start = ((), (), s32[]{:S(2)}) async-start(), calls=%async_computation.2 | async-start | bytes 11280384 | tf_op jit(solution)/shard_map/reduce_scatter | solution.py:1223
  12.8 1.9 copy-start.5
  14.6 77.9 %copy-start.15 = (bf16[2,1024,768]{2,1,0:T(8,128)(2,1)S(1)}, bf16[2,1024,768]{2,1,0:T(8,128)(2,1)}, u32[]{:S(2)}) copy-start(bf16[2,1024,768]{2,1,0:T(8,128)(2,1)} %param.39) | copy-start | bytes 9437188
  83.3 1.8 copy-start.6
  85.1 1.7 copy-start.7
  86.8 1.7 copy-start.8
  88.5 1.7 copy-start.9
  90.2 1.7 copy-start.10
  91.9 0.6 copy-start.13
  92.5 5.5 %copy-start.25 = (s32[2,2048]{1,0:T(2,128)S(1)}, s32[2,2048]{1,0:T(2,128)}, u32[]{:S(2)}) copy-start(s32[2,2048]{1,0:T(2,128)} %param.21) | copy-start | bytes 49156
  92.5 6.3 %copy-start.35 = (s32[2,2]{1,0:T(2,128)S(1)}, s32[2,2]{1,0:T(2,128)}, u32[]{:S(2)}) copy-start(s32[2,2]{1,0:T(2,128)} %param.23) | copy-start | bytes 52
  93.8 61.4 %collective-permute-start = (bf16[1,1024,768]{2,1,0:T(8,128)(2,1)}, bf16[1,1024,768]{2,1,0:T(8,128)(2,1)}, u32[]{:S(2)}, u32[]{:S(2)}) collective-permute-start(bf16[1,1024,768]{2,1,0:T(8,128)(2,1)} %constant_dynamic-slice_fusion.1), channel_id=1, source_target_pairs={{0,16},{16,0},{1,17},{17,1},{2,18},{18,2},{3,19},{19,3},{4,20},{20... | collective-permute-start | bytes 4718600 | tf_op jit(solution)/shard_map/ppermute | solution.py:1098
  100.6 48.1 %copy-start.3 = (s32[1,32,128]{2,1,0:T(8,128)}, s32[1,32,128]{2,1,0:T(8,128)S(1)}, u32[]{:S(2)}) copy-start(s32[1,32,128]{2,1,0:T(8,128)S(1)} %pad_add_fusion) | copy-start | bytes 49156
  100.6 48.1 %copy-start.12 = (s32[1,32]{1,0:T(1,128)}, s32[1,32]{1,0:T(1,128)S(1)}, u32[]{:S(2)}) copy-start(s32[1,32]{1,0:T(1,128)S(1)} %and_select_fusion.n_ref) | copy-start | bytes 388
  100.6 48.1 %copy-start.4 = (s32[1,1024]{1,0:T(1,128)}, s32[1,1024]{1,0:T(1,128)S(1)}, u32[]{:S(2)}) copy-start(s32[1,1024]{1,0:T(1,128)S(1)} %compare_select_fusion.list_ref) | copy-start | bytes 12292
  101.0 47.7 %copy-start.2 = (s32[1,2112,128]{2,1,0:T(8,128)}, s32[1,2112,128]{2,1,0:T(8,128)S(1)}, u32[]{:S(2)}) copy-start(s32[1,2112,128]{2,1,0:T(8,128)S(1)} %broadcast_in_dim.99.segc_ref) | copy-start | bytes 3244036
  148.7 1.6 copy-start.11
  150.3 0.6 copy-start.14
  150.9 3.0 copy-start.16
  280.0 1.9 copy-start.17
  283.2 81.2 %collective-permute-start.1 = (bf16[1,1024,768]{2,1,0:T(8,128)(2,1)}, bf16[1,1024,768]{2,1,0:T(8,128)(2,1)S(1)}, u32[]{:S(2)}, u32[]{:S(2)}) collective-permute-start(bf16[1,1024,768]{2,1,0:T(8,128)(2,1)} %dynamic-slice_bitcast_fusion), channel_id=1, source_target_pairs={{16,0},{0,16},{17,1},{1,17},{18,2},{2,18},{19,3},{3,19},{20,4},{4,... | collective-permute-start | bytes 4718600 | tf_op jit(solution)/shard_map/ppermute | solution.py:1098
  433.4 16.7 %collective-permute-start.2 = (bf16[48,6912]{1,0:T(8,128)(2,1)}, bf16[48,6912]{1,0:T(8,128)(2,1)S(1)}, u32[]{:S(2)}, u32[]{:S(2)}) collective-permute-start(bf16[48,6912]{1,0:T(8,128)(2,1)} %reduce-scatter.2.cloned.1.call-done), channel_id=1, source_target_pairs={{0,16},{16,0},{1,17},{17,1},{2,18},{18,2},{3,19},{19,3},{4,20},{20... | collective-permute-start | bytes 1990664 | tf_op jit(solution)/shard_map/ppermute | solution.py:1074
  455.4 5.8 %copy-start.1 = (s32[2,32,3]{1,0,2:T(2,128)S(1)}, s32[2,32,3]{1,0,2:T(2,128)}, u32[]{:S(2)}) copy-start(s32[2,32,3]{1,0,2:T(2,128)} %param.22) | copy-start | bytes 2308
  455.4 3.8 copy-start.20
  455.4 4.5 copy-start.19
  455.4 5.1 %copy-start.18 = (f32[48,768]{1,0:T(8,128)S(1)}, f32[48,768]{1,0:T(8,128)}, u32[]{:S(2)}) copy-start(f32[48,768]{1,0:T(8,128)} %get-tuple-element.148) | copy-start | bytes 442372
Sparse Core Ops, SparseCore 0:
  11.6 103.1 all-gather.1
  280.2 127.8 reduce-scatter.1

commit v2 on v1

--- a/solution.py
+++ b/solution.py
@@ -36,7 +36,7 @@
     seg_cols = jnp.concatenate([seg, jnp.full((rows, BLK), -1, jnp.int32)], axis=1)
     seg_cols = jnp.broadcast_to(seg_cols[:, :, None], (rows, full_len + BLK, 128))
     seg_rows = jnp.concatenate([by_block, by_block], axis=2)[:, :, None, :]
-    return chunks, listed.reshape(rows, nb * nb), seg_cols, seg_rows
+    return chunks, listed.reshape(rows, nb * nb), jnp.sum(chunks, axis=1), seg_cols, seg_rows
 
 
 def lane_low(rows):
@@ -66,8 +66,9 @@
     return jnp.where(lane_low(HD), top, low)
 
 
-def chunk_ids(list_ref, row, base, nb):
-    ids = [list_ref[row, base + j] for j in range(CHUNK)]
+def chunk_ids(list_ref, row, base, nb, real):
+    base = jnp.minimum(base, nb * nb - CHUNK)
+    ids = [jnp.where(real, list_ref[row, base + j], nb) for j in range(CHUNK)]
     safe = [jnp.where(b == nb, 0, b) for b in ids]
     return ids, safe
 
@@ -94,7 +95,7 @@
             dst_ref[b, t * 128 : t * 128 + 128, :] = transposed_twice(tile)
         return 0
 
-    lax.fori_loop(0, nb, body, 0)
+    lax.fori_loop(0, nb, body, 0, unroll=4)
 
 
 def dot_f32(left, right):
@@ -103,65 +104,101 @@
     )
 
 
-def forward_kernel(group, n_ref, list_ref, q_ref, k_ref, v_ref, segc_ref, segr_ref,
+def next_item(n_ref, row, nb, a, c):
+    more = c + 1 < n_ref[row, a]
+    following = jnp.where(more, a, jnp.minimum(a + 1, nb - 1))
+    return following, jnp.where(more, c + 1, 0)
+
+
+def run_items(n_ref, total_ref, row, nb, ready, item, finish):
+    total = total_ref[row]
+
+    def following(a, c):
+        return next_item(n_ref, row, nb, a, c)
+
+    def turn(i, carry):
+        before, between, a, c = carry
+        base = lax.rem(i, 2) * 2
+        finish(before)
+        finish(between)
+        a_two, c_two = following(a, c)
+        a_three, c_three = following(a_two, c_two)
+        a_four, c_four = following(a_three, c_three)
+        ready(a_three, 2 - base)
+        ready(a_four, 3 - base)
+        real = 2 * i + 1 < total
+        a_two, c_two = jnp.where(real, a_two, a), jnp.where(real, c_two, c + 1)
+        item(base, a, c, True)
+        item(base + 1, a_two, c_two, real)
+        return a, a_two, a_three, c_three
+
+    ready(0, 0)
+    ready(following(0, 0)[0], 1)
+    before, between, _, _ = lax.fori_loop(0, (total + 1) // 2, turn, (0, 0, 0, 0))
+    finish(before)
+    finish(between)
+
+
+def forward_kernel(group, n_ref, list_ref, total_ref, q_ref, k_ref, v_ref, segc_ref, segr_ref,
                    o_ref, lse_ref, vt_ref, qst_ref, m_ref, l_ref, acc_ref):
     row = pl.program_id(0)
     width = q_ref.shape[2]
     nb = q_ref.shape[1] // BLK
     groups, halves = width // group, group // 128
+    tiles = width // 128
     turn_all(v_ref, vt_ref, nb, width)
     qst_ref[...] = jnp.zeros_like(qst_ref)
-
-    def per_query(a, _):
+    l_ref[...] = jnp.ones_like(l_ref)
+    acc_ref[...] = jnp.zeros_like(acc_ref)
+    m_ref[...] = jnp.zeros_like(m_ref)
+
+    def ready(a, slot):
         start = pl.multiple_of(a * BLK, BLK)
-        for t in range(width // 128):
+        for t in range(tiles):
             tile = q_ref[0, pl.ds(start, BLK), t * 128 : t * 128 + 128] * 0.125
-            g, u = t // halves, t % halves
-            qst_ref[g, u * 128 : u * 128 + 128, u * 128 : u * 128 + 128] = diag128(
+            square = slice(t % halves * 128, t % halves * 128 + 128)
+            qst_ref[slot, t // halves, square, square] = diag128(
                 transposed_twice(tile.astype(jnp.bfloat16))
             )
-        seg_q = segr_ref[0, a]
-        m_ref[...] = jnp.full_like(m_ref, NEG)
-        l_ref[...] = jnp.zeros_like(l_ref)
-        acc_ref[...] = jnp.zeros_like(acc_ref)
-
-        def per_chunk(c, _):
-            ids, safe = chunk_ids(list_ref, row, a * nb + c * CHUNK, nb)
-            seg_k = block_rows(segc_ref, ids, slice(0, 128))
-            allowed = seg_k == seg_q
-            for g in range(groups):
-                lanes = slice(g * group, g * group + group)
-                s_t = dot_f32(block_rows(k_ref, safe, lanes), qst_ref[g])
-                weights, alphas = [], []
-                for u in range(halves):
-                    t = g * halves + u
-                    s = jnp.where(allowed, s_t[:, u * 128 : u * 128 + 128], NEG)
-                    m_old = m_ref[t]
-                    m_new = jnp.maximum(m_old, jnp.max(s, axis=0, keepdims=True))
-                    p = jnp.exp(s - m_new)
-                    alpha = jnp.exp(m_old - m_new)
-                    l_ref[t] = alpha * l_ref[t] + jnp.sum(p, axis=0, keepdims=True)
-                    m_ref[t] = m_new
-                    weights.append(p.astype(jnp.bfloat16))
-                    alphas.append(alpha)
-                p_t = jnp.concatenate(weights, axis=1) if halves > 1 else weights[0]
-                o_t = dot_f32(turned_blocks(vt_ref, safe, lanes), p_t)
-                for u in range(halves):
-                    t = g * halves + u
-                    acc_ref[t] = alphas[u] * acc_ref[t] + pick_diag(o_t, u)
-            return 0
-
-        lax.fori_loop(0, n_ref[row, a], per_chunk, 0)
-        for t in range(width // 128):
-            total = l_ref[t]
-            out = acc_ref[t] / total
-            o_ref[0, pl.ds(start, BLK), t * 128 : t * 128 + 128] = head_rows(out).astype(
+
+    def finish(a):
+        even = lax.rem(a, 2)
+        start = pl.multiple_of(a * BLK, BLK)
+        for t in range(tiles):
+            lanes = slice(t * 128, t * 128 + 128)
+            total = l_ref[even, t]
+            o_ref[0, pl.ds(start, BLK), lanes] = head_rows(acc_ref[even, t] / total).astype(
                 jnp.bfloat16
             )
-            lse_ref[0, a, :, t * 128 : t * 128 + 128] = m_ref[t] + jnp.log(total)
-        return 0
-
-    lax.fori_loop(0, nb, per_query, 0)
+            lse_ref[0, a, :, lanes] = m_ref[even, t] + jnp.log(total)
+
+    def item(slot, a, c, real):
+        ids, safe = chunk_ids(list_ref, row, a * nb + c * CHUNK, nb, real)
+        even = lax.rem(a, 2)
+        allowed = block_rows(segc_ref, ids, slice(0, 128)) == segr_ref[0, a]
+        first = c == 0
+        for g in range(groups):
+            lanes = slice(g * group, g * group + group)
+            s_t = dot_f32(block_rows(k_ref, safe, lanes), qst_ref[slot, g])
+            weights, alphas = [], []
+            for u in range(halves):
+                t = g * halves + u
+                s = jnp.where(allowed, s_t[:, u * 128 : u * 128 + 128], NEG)
+                m_old = jnp.where(first, NEG, m_ref[even, t])
+                m_new = jnp.maximum(m_old, jnp.max(s, axis=0, keepdims=True))
+                p = jnp.exp(s - m_new)
+                alpha = jnp.exp(m_old - m_new)
+                l_ref[even, t] = alpha * l_ref[even, t] + jnp.sum(p, axis=0, keepdims=True)
+                m_ref[even, t] = m_new
+                weights.append(p.astype(jnp.bfloat16))
+                alphas.append(alpha)
+            p_t = jnp.concatenate(weights, axis=1) if halves > 1 else weights[0]
+            o_t = dot_f32(turned_blocks(vt_ref, safe, lanes), p_t)
+            for u in range(halves):
+                t = g * halves + u
+                acc_ref[even, t] = alphas[u] * acc_ref[even, t] + pick_diag(o_t, u)
+
+    run_items(n_ref, total_ref, row, nb, ready, item, finish)
 
 
 def group_of(width):
@@ -180,7 +217,7 @@
 
 
 def attention_forward(q, k, v, plan):
-    chunks, listed, seg_cols, seg_rows = plan
+    *tables, seg_cols, seg_rows = plan
     rows, full_len, width = q.shape
     nb, group = full_len // BLK, group_of(width)
     tiles = width // 128
@@ -193,42 +230,43 @@
             jax.ShapeDtypeStruct((rows, nb, 1, width), jnp.float32),
         ),
         grid_spec=pltpu.PrefetchScalarGridSpec(
-            num_scalar_prefetch=2,
+            num_scalar_prefetch=3,
             grid=(rows,),
             in_specs=[one_spec(x.shape) for x in args],
             out_specs=(one_spec((rows, full_len, width)), one_spec((rows, nb, 1, width))),
             scratch_shapes=[
                 pltpu.VMEM((nb, width, 128), jnp.bfloat16),
-                pltpu.VMEM((width // group, group, group), jnp.bfloat16),
-                pltpu.VMEM((tiles, 1, 128), jnp.float32),
-                pltpu.VMEM((tiles, 1, 128), jnp.float32),
-                pltpu.VMEM((tiles, HD, 128), jnp.float32),
+                pltpu.VMEM((4, width // group, group, group), jnp.bfloat16),
+                pltpu.VMEM((2, tiles, 1, 128), jnp.float32),
+                pltpu.VMEM((2, tiles, 1, 128), jnp.float32),
+                pltpu.VMEM((2, tiles, HD, 128), jnp.float32),
             ],
         ),
-        compiler_params=pltpu.CompilerParams(vmem_limit_bytes=48 << 20),
+        compiler_params=pltpu.CompilerParams(vmem_limit_bytes=62 << 20),
         cost_estimate=pl.CostEstimate(
-            flops=64 * pairs, transcendentals=pairs // HD, bytes_accessed=8 * q.size
+            flops=4 * pairs, transcendentals=pairs // HD, bytes_accessed=8 * q.size
         ),
         name="attention_forward",
-    )(chunks, listed, *args)
-
-
-def backward_kernel(group, n_ref, list_ref, q_ref, k_ref, v_ref, o_ref, do_ref, lse_ref,
-                    segc_ref, segr_ref, dq_ref, dk_ref, dv_ref,
+    )(*tables, *args)
+
+
+def backward_kernel(group, n_ref, list_ref, total_ref, q_ref, k_ref, v_ref, o_ref, do_ref,
+                    lse_ref, segc_ref, segr_ref, dq_ref, dk_ref, dv_ref,
                     kt_ref, qst_ref, qs_ref, dost_ref, dos_ref, delta_ref, acc_ref,
                     dk_acc, dv_acc):
     row = pl.program_id(0)
     full_len, width = q_ref.shape[1], q_ref.shape[2]
     nb = full_len // BLK
     groups, halves = width // group, group // 128
+    tiles = width // 128
     turn_all(k_ref, kt_ref, nb, width)
-    for ref in (qst_ref, qs_ref, dost_ref, dos_ref, dk_acc, dv_acc):
+    for ref in (qst_ref, qs_ref, dost_ref, dos_ref, dk_acc, dv_acc, acc_ref):
         ref[...] = jnp.zeros_like(ref)
-    low = lane_low(HD)
-
-    def per_query(a, _):
+    low = lane_low(1)
+
+    def ready(a, slot):
         start = pl.multiple_of(a * BLK, BLK)
-        for t in range(width // 128):
+        for t in range(tiles):
             g, u = t // halves, t % halves
             lanes = slice(t * 128, t * 128 + 128)
             square = slice(u * 128, u * 128 + 128)
@@ -236,58 +274,60 @@
             g_tile = do_ref[0, pl.ds(start, BLK), lanes]
             o_tile = o_ref[0, pl.ds(start, BLK), lanes]
             g_turn = transposed_twice(g_tile)
-            qst_ref[g, square, square] = diag128(transposed_twice(q_tile))
-            dost_ref[g, square, square] = diag128(g_turn)
-            qs_ref[g, square, square] = diag128(jnp.concatenate([q_tile, q_tile], axis=0))
-            dos_ref[g, square, square] = diag128(jnp.concatenate([g_tile, g_tile], axis=0))
+            qst_ref[slot, g, square, square] = diag128(transposed_twice(q_tile))
+            dost_ref[slot, g, square, square] = diag128(g_turn)
+            qs_ref[slot, g, square, square] = diag128(jnp.concatenate([q_tile, q_tile], axis=0))
+            dos_ref[slot, g, square, square] = diag128(
+                jnp.concatenate([g_tile, g_tile], axis=0)
+            )
             product = g_turn.astype(jnp.float32) * transposed_twice(o_tile).astype(jnp.float32)
-            delta_ref[t] = jnp.where(
-                low[:1],
+            delta_ref[slot, t] = jnp.where(
+                low,
                 jnp.sum(product[:HD], axis=0, keepdims=True),
                 jnp.sum(product[HD:], axis=0, keepdims=True),
             )
-        seg_q = segr_ref[0, a]
-        acc_ref[...] = jnp.zeros_like(acc_ref)
-
-        def per_chunk(c, _):
-            ids, safe = chunk_ids(list_ref, row, a * nb + c * CHUNK, nb)
-            seg_k = block_rows(segc_ref, ids, slice(0, 128))
-            allowed = seg_k == seg_q
-            for g in range(groups):
-                lanes = slice(g * group, g * group + group)
-                s_t = dot_f32(block_rows(k_ref, safe, lanes), qst_ref[g])
-                dp_t = dot_f32(block_rows(v_ref, safe, lanes), dost_ref[g])
-                p_parts, ds_parts = [], []
-                for u in range(halves):
-                    t = g * halves + u
-                    half = slice(u * 128, u * 128 + 128)
-                    lse = lse_ref[0, a, :, t * 128 : t * 128 + 128]
-                    p = jnp.exp(jnp.where(allowed, s_t[:, half], NEG) - lse)
-                    ds = p * (dp_t[:, half] - delta_ref[t])
-                    p_parts.append(p.astype(jnp.bfloat16))
-                    ds_parts.append(ds.astype(jnp.bfloat16))
-                p_t = jnp.concatenate(p_parts, axis=1) if halves > 1 else p_parts[0]
-                ds_t = jnp.concatenate(ds_parts, axis=1) if halves > 1 else ds_parts[0]
-                dv = dot_f32(p_t, dos_ref[g])
-                dk = dot_f32(ds_t, qs_ref[g])
-                dq_t = dot_f32(turned_blocks(kt_ref, safe, lanes), ds_t)
-                for j in range(CHUNK):
-                    where = pl.ds(pl.multiple_of(safe[j] * BLK, BLK), BLK)
-                    part = slice(j * BLK, j * BLK + BLK)
-                    dv_acc[where, lanes] += dv[part]
-                    dk_acc[where, lanes] += dk[part]
-                for u in range(halves):
-                    acc_ref[g * halves + u] += pick_diag(dq_t, u)
-            return 0
-
-        lax.fori_loop(0, n_ref[row, a], per_chunk, 0)
-        for t in range(width // 128):
+
+    def finish(a):
+        even = lax.rem(a, 2)
+        start = pl.multiple_of(a * BLK, BLK)
+        for t in range(tiles):
             dq_ref[0, pl.ds(start, BLK), t * 128 : t * 128 + 128] = (
-                head_rows(acc_ref[t]) * 0.125
+                head_rows(acc_ref[even, t]) * 0.125
             ).astype(jnp.bfloat16)
-        return 0
-
-    lax.fori_loop(0, nb, per_query, 0)
+
+    def item(slot, a, c, real):
+        ids, safe = chunk_ids(list_ref, row, a * nb + c * CHUNK, nb, real)
+        even = lax.rem(a, 2)
+        allowed = block_rows(segc_ref, ids, slice(0, 128)) == segr_ref[0, a]
+        first = c == 0
+        for g in range(groups):
+            lanes = slice(g * group, g * group + group)
+            s_t = dot_f32(block_rows(k_ref, safe, lanes), qst_ref[slot, g])
+            dp_t = dot_f32(block_rows(v_ref, safe, lanes), dost_ref[slot, g])
+            p_parts, ds_parts = [], []
+            for u in range(halves):
+                t = g * halves + u
+                half = slice(u * 128, u * 128 + 128)
+                lse = lse_ref[0, a, :, t * 128 : t * 128 + 128]
+                p = jnp.exp(jnp.where(allowed, s_t[:, half], NEG) - lse)
+                ds = p * (dp_t[:, half] - delta_ref[slot, t])
+                p_parts.append(p.astype(jnp.bfloat16))
+                ds_parts.append(ds.astype(jnp.bfloat16))
+            p_t = jnp.concatenate(p_parts, axis=1) if halves > 1 else p_parts[0]
+            ds_t = jnp.concatenate(ds_parts, axis=1) if halves > 1 else ds_parts[0]
+            dv = dot_f32(p_t, dos_ref[slot, g])
+            dk = dot_f32(ds_t, qs_ref[slot, g])
+            dq_t = dot_f32(turned_blocks(kt_ref, safe, lanes), ds_t)
+            for j in range(CHUNK):
+                where = pl.ds(pl.multiple_of(safe[j] * BLK, BLK), BLK)
+                part = slice(j * BLK, j * BLK + BLK)
+                dv_acc[where, lanes] += dv[part]
+                dk_acc[where, lanes] += dk[part]
+            for u in range(halves):
+                t = g * halves + u
+                acc_ref[even, t] = jnp.where(first, 0.0, acc_ref[even, t]) + pick_diag(dq_t, u)
+
+    run_items(n_ref, total_ref, row, nb, ready, item, finish)
 
     def flush(a, _):
         where = pl.ds(pl.multiple_of(a * BLK, BLK), BLK)
@@ -295,41 +335,41 @@
         dv_ref[0, where, :] = dv_acc[where, :].astype(jnp.bfloat16)
         return 0
 
-    lax.fori_loop(0, nb, flush, 0)
+    lax.fori_loop(0, nb, flush, 0, unroll=2)
 
 
 def attention_backward(q, k, v, o, do, lse, plan):
-    chunks, listed, seg_cols, seg_rows = plan
+    *tables, seg_cols, seg_rows = plan
     rows, full_len, width = q.shape
     nb, group = full_len // BLK, group_of(width)
     tiles, groups = width // 128, width // group
     pairs = rows * full_len * full_len // 4 * width
     args = (q, k, v, o, do, lse, seg_cols, seg_rows)
     like = jax.ShapeDtypeStruct((rows, full_len, width), jnp.bfloat16)
-    square = pltpu.VMEM((groups, group, group), jnp.bfloat16)
+    square = pltpu.VMEM((4, groups, group, group), jnp.bfloat16)
     return pl.pallas_call(
         functools.partial(backward_kernel, group),
         out_shape=(like, like, like),
         grid_spec=pltpu.PrefetchScalarGridSpec(
-            num_scalar_prefetch=2,
+            num_scalar_prefetch=3,
             grid=(rows,),
             in_specs=[one_spec(x.shape) for x in args],
             out_specs=tuple(one_spec(like.shape) for _ in range(3)),
             scratch_shapes=[
                 pltpu.VMEM((nb, width, 128), jnp.bfloat16),
                 square, square, square, square,
-                pltpu.VMEM((tiles, 1, 128), jnp.float32),
-                pltpu.VMEM((tiles, HD, 128), jnp.float32),
+                pltpu.VMEM((4, tiles, 1, 128), jnp.float32),
+                pltpu.VMEM((2, tiles, HD, 128), jnp.float32),
                 pltpu.VMEM((full_len, width), jnp.float32),
                 pltpu.VMEM((full_len, width), jnp.float32),
             ],
         ),
-        compiler_params=pltpu.CompilerParams(vmem_limit_bytes=58 << 20),
+        compiler_params=pltpu.CompilerParams(vmem_limit_bytes=62 << 20),
         cost_estimate=pl.CostEstimate(
-            flops=100 * pairs, transcendentals=pairs // HD, bytes_accessed=16 * q.size
+            flops=10 * pairs, transcendentals=pairs // HD, bytes_accessed=16 * q.size
         ),
         name="attention_backward",
-    )(chunks, listed, *args)
+    )(*tables, *args)
 
 
 def pair_bit(index, bit):
@@ -356,9 +396,9 @@
 
 
 def qkv_backward_kernel(
-    bits, x_in, dq_in, dk_in, dv_in, w_in, res_in, small_in,
+    bits, xt_in, dq_in, dk_in, dv_in, wt_in, res_in, small_in,
     wq_out, wk_out, wv_out, small_out, tok_out,
-    x, xt, grads, w, wt, res, tok, kept, sends, lands, final, small, small_land, result,
+    xt, grads, wt, res, tok, kept, sends, lands, final, small, small_land, result,
     in_sem, tok_send, tok_land, own_sem, send_sem, land_sem, x_send, x_land,
     small_send, small_recv, out_sem,
 ):
@@ -369,33 +409,20 @@
     owners = 1 << bits
     sources = (dq_in, dk_in, dv_in)
     loads = [
-        pltpu.make_async_copy(w_in, w, in_sem.at[0]),
+        pltpu.make_async_copy(wt_in, wt, in_sem.at[0]),
         pltpu.make_async_copy(res_in, res, in_sem.at[1]),
         pltpu.make_async_copy(small_in, small.at[0], in_sem.at[2]),
-        pltpu.make_async_copy(x_in, x, in_sem.at[3]),
+        pltpu.make_async_copy(xt_in, xt, in_sem.at[3]),
     ] + [pltpu.make_async_copy(sources[i], grads.at[i], in_sem.at[4 + i]) for i in range(3)]
-    for i in (0, 3, 4, 5, 6, 1, 2):
+    for i in (3, 4, 5, 6, 0, 1, 2):
         loads[i].start()
     all_arrived(bits)
-    loads[0].wait()
-    for i in range(3):
-        first = part_start(width, i)
-        wt[i * width : (i + 1) * width, :] = w[:, first : first + width].T
-    loads[3].wait()
-
-    def turn(r, _):
-        xt[r] = x[pl.ds(pl.multiple_of(r * piece, piece), piece), :].T
-        return 0
-
-    lax.fori_loop(0, 2 * pieces, turn, 0)
-    for i in (4, 5, 6, 1):
-        loads[i].wait()
 
     def token_rows(start):
         total = res[pl.ds(start, piece), :].astype(jnp.float32)
         for i in range(3):
             total = total + dot_f32(
-                grads[i, pl.ds(start, piece), :], wt[i * width : (i + 1) * width, :]
+                grads[i, pl.ds(start, piece), :], wt[i]
             )
         return total.astype(jnp.bfloat16)
 
@@ -428,8 +455,6 @@
         sent(i).start()
         return 0
 
-    lax.fori_loop(0, pieces, send_piece, 0)
-
     def keep_piece(i, _):
         start = pl.multiple_of(side * half + i * piece, piece)
         tok[1, i] = token_rows(start)
@@ -446,7 +471,10 @@
         def rows(m, _):
             rows_here = pl.ds(pl.multiple_of(m * tile * own, tile * own), tile * own)
             block = dot_f32(
-                jnp.concatenate([xt[r, rows_here, :] for r in range(2 * pieces)], axis=1), grads[i]
+                jnp.concatenate(
+                    [xt[h, r, rows_here, :] for h in range(2) for r in range(pieces)], axis=1
+                ),
+                grads[i],
             ).reshape(tile // 2, 2, own, width)
             even, odd = block[:, 0], block[:, 1]
             spot = pl.ds(m * (tile // 2), tile // 2)
@@ -519,9 +547,17 @@
         if bit < bits:
             small_hop(bit + 1).start()
 
-    loads[2].wait()
+    for i in (3, 4):
+        loads[i].wait()
     weights(0)
     hop(0, 0).start()
+    for i in (5, 6, 0, 1):
+        loads[i].wait()
+    lax.fori_loop(0, pieces, send_piece, 0)
+    advance(0, 0)
+    weights(1)
+    hop(1, 0).start()
+    loads[2].wait()
     for spot, i in ((0, 0), (1, 2)):
         def column_sums(c, total):
             block = grads[i, pl.ds(pl.multiple_of(c * 128, 128), 128), :].astype(jnp.float32)
@@ -532,12 +568,9 @@
         )
         small[0, spot : spot + 1] = jnp.sum(total, axis=0, keepdims=True)
     small_hop(0).start()
-    weights(1)
-    hop(1, 0).start()
-    advance(0, 0)
-    small_advance(0)
     weights(2)
     hop(2, 0).start()
+    small_advance(0)
     plan = []
     for step in range(1, bits + 2):
         todo = []
@@ -576,7 +609,7 @@
         landed(i).wait_recv()
 
 
-def qkv_backward(x, dq, dk, dv, w, resid, small, own):
+def qkv_backward(xt, dq, dk, dv, wt, resid, small, own):
     tokens, width = dq.shape
     bits = lax.axis_size("fsdp").bit_length() - 1
     owners = 1 << bits
@@ -585,7 +618,7 @@
     dma = pltpu.SemaphoreType.DMA
     f32, bf16 = jnp.float32, jnp.bfloat16
     shard = jax.ShapeDtypeStruct((own, width), f32)
-    anywhere = pl.BlockSpec(memory_space=pl.ANY)
+    anywhere = pl.BlockSpec(memory_space=pltpu.HBM)
     return pl.pallas_call(
         functools.partial(qkv_backward_kernel, bits),
         out_shape=(
@@ -596,11 +629,9 @@
         in_specs=[anywhere] * 7,
         out_specs=(anywhere,) * 5,
         scratch_shapes=[
-            pltpu.VMEM((tokens, width), bf16),
-            pltpu.VMEM((2 * pieces, width, piece), bf16),
+            pltpu.VMEM(xt.shape, bf16),
             pltpu.VMEM((3, tokens, width), bf16),
-            pltpu.VMEM(w.shape, bf16),
-            pltpu.VMEM((3 * width, width), bf16),
+            pltpu.VMEM(wt.shape, bf16),
             pltpu.VMEM((tokens, width), bf16),
             pltpu.VMEM((2, pieces, piece, width), bf16),
             pltpu.VMEM((3, owners - 1, own, width), f32),
@@ -615,21 +646,22 @@
             dma((bits + 1,)), dma((bits + 1,)), dma((4,)),
         ],
         compiler_params=pltpu.CompilerParams(
-            collective_id=1, has_side_effects=True, vmem_limit_bytes=60 << 20
+            collective_id=1, has_side_effects=True, vmem_limit_bytes=62 << 20
         ),
         cost_estimate=pl.CostEstimate(
             flops=40 * tokens * width * width, transcendentals=0,
             bytes_accessed=16 * tokens * width,
         ),
         name="qkv_backward",
-    )(x, dq, dk, dv, w, resid, small)
+    )(xt, dq, dk, dv, wt, resid, small)
 
 
 def qkv_forward_kernel(
     bits, tokens_in, own_in,
-    x_out, q_out, k_out, v_out, w_out, small_out,
-    x, w, qkv, small,
-    own_sem, tok_send, tok_land, load_sem, send_sem, land_sem, x_sem, out_sem, w_sem, small_sem,
+    x_out, xt_out, q_out, k_out, v_out, wt_out, small_out,
+    x, xt, w, wt, qkv, small,
+    own_sem, tok_send, tok_land, load_sem, send_sem, land_sem, x_sem, xt_sem, out_sem, w_sem,
+    small_sem,
 ):
     me, side = lax.axis_index("fsdp"), lax.axis_index("seq")
     pieces, piece, width = x.shape[1], x.shape[2], x.shape[3]
@@ -690,14 +722,24 @@
             qkv.at[part, half, i], outs[part].at[half, i], out_sem.at[part, half, i]
         )
 
+    def xt_copy(half, i):
+        return pltpu.make_async_copy(xt.at[half, i], xt_out.at[half, i], xt_sem.at[half, i])
+
     def w_copy(part):
-        spot = (slice(None),) * (bits + 1) + (columns[part],)
-        return pltpu.make_async_copy(w.at[spot], w_out.at[spot], w_sem.at[part])
-
-    def project(part, half, i):
+        return pltpu.make_async_copy(wt.at[part], wt_out.at[part], w_sem.at[part])
+
+    def whole(part):
         first = part_start(width, part)
         spot = (slice(None),) * (bits + 1) + (slice(first, first + width),)
-        total = dot_f32(x[half, i], w[spot].reshape(width, width))
+        return w[spot].reshape(width, width)
+
+    def turn(half, i):
+        x_copy(half, i).start()
+        xt[half, i] = x[half, i].T
+        xt_copy(half, i).start()
+
+    def project(part, half, i):
+        total = dot_f32(x[half, i], whole(part))
         if part == 0:
             total = total + small[0:1, :]
         if part == 2:
@@ -705,56 +747,60 @@
         qkv[part, half, i] = total.astype(jnp.bfloat16)
         out_copy(part, half, i).start()
 
-    def each_own(part):
+    def over(body):
         def one(i, _):
-            project(part, side, i)
+            body(i)
             return 0
 
         lax.fori_loop(0, pieces, one, 0)
 
-    def arrived(part):
+    def turn_weights(part):
+        wt[part] = whole(part).T
         w_copy(part).start()
-        if part == 0:
+
+    def other(i):
+        landed(i).wait_recv()
+        turn(1 - side, i)
+        project(0, 1 - side, i)
+        project(1, 1 - side, i)
+
+    own_tokens.wait()
+    over(lambda i: turn(side, i))
+    for step in range(bits + 2):
+        full = None
+        for part in range(3):
+            hops = step - part
+            if 0 <= hops < bits:
+                hop(part, hops).wait_recv()
+                if hops + 1 < bits:
+                    hop(part, hops + 1).start()
+                else:
+                    full = part
+        if full == 0:
             spot = (slice(None),) * (bits + 1) + (slice(width, width + 128),)
             turned = w[spot].reshape(width, 128).astype(jnp.float32).T
             small[...] = turned[: small.shape[0]]
             pltpu.make_async_copy(small, small_out, small_sem.at[0]).start()
-            own_tokens.wait()
-        each_own(part)
-
-    for step in range(bits + 2):
-        full = None
-        for part in range(3):
-            turn = step - part
-            if 0 <= turn < bits:
-                hop(part, turn).wait_recv()
-                if turn + 1 < bits:
-                    hop(part, turn + 1).start()
-                else:
-                    full = part
         if full is not None:
-            arrived(full)
-    for i in range(pieces):
-        x_copy(side, i).start()
-
-    def other(i, _):
-        landed(i).wait_recv()
-        x_copy(1 - side, i).start()
-        for part in range(3):
-            project(part, 1 - side, i)
-        return 0
-
-    lax.fori_loop(0, pieces, other, 0)
+            over(lambda i: project(full, side, i))
+        if full == 1:
+            turn_weights(0)
+            turn_weights(1)
+            over(other)
+        if full == 2:
+            over(lambda i: project(2, 1 - side, i))
+            turn_weights(2)
     for i in range(pieces):
         sent(i).wait_send()
     for part in range(3):
         w_copy(part).wait()
-        for turn in range(bits):
-            hop(part, turn).wait_send()
+        for hops in range(bits):
+            hop(part, hops).wait_send()
     pltpu.make_async_copy(small, small_out, small_sem.at[0]).wait()
     for half in range(2):
         for i in range(pieces):
             x_copy(half, i).wait()
+            xt_copy(half, i).wait()
             for part in range(3):
                 out_copy(part, half, i).wait()
 
@@ -781,28 +827,31 @@
     bf16 = jnp.bfloat16
     halves = (2, pieces, piece, width)
     gathered = (2,) * bits + (own, columns)
-    anywhere = pl.BlockSpec(memory_space=pl.ANY)
+    anywhere = pl.BlockSpec(memory_space=pltpu.HBM)
     like = jax.ShapeDtypeStruct(halves, bf16)
-    x, q, k, v, weights, small = pl.pallas_call(
+    turned = (2, pieces, width, piece)
+    x, xt, q, k, v, weights_t, small = pl.pallas_call(
         functools.partial(qkv_forward_kernel, bits),
         out_shape=(
-            like, like, like, like,
-            jax.ShapeDtypeStruct(gathered, bf16),
+            like, jax.ShapeDtypeStruct(turned, bf16), like, like, like,
+            jax.ShapeDtypeStruct((3, width, width), bf16),
             jax.ShapeDtypeStruct((SMALL_ROWS, width), jnp.float32),
         ),
         in_specs=[anywhere] * 2,
-        out_specs=(anywhere,) * 6,
+        out_specs=(anywhere,) * 7,
         scratch_shapes=[
             pltpu.VMEM(halves, bf16),
+            pltpu.VMEM(turned, bf16),
             pltpu.VMEM(gathered, bf16),
+            pltpu.VMEM((3, width, width), bf16),
             pltpu.VMEM((3,) + halves, bf16),
             pltpu.VMEM((SMALL_ROWS, width), jnp.float32),
             dma((1,)), dma((pieces,)), dma((pieces,)), dma((3,)),
-            dma((3, bits)), dma((3, bits)), dma((2, pieces)), dma((3, 2, pieces)),
-            dma((3,)), dma((1,)),
+            dma((3, bits)), dma((3, bits)), dma((2, pieces)), dma((2, pieces)),
+            dma((3, 2, pieces)), dma((3,)), dma((1,)),
         ],
         compiler_params=pltpu.CompilerParams(
-            collective_id=2, has_side_effects=True, vmem_limit_bytes=30 << 20
+            collective_id=2, has_side_effects=True, vmem_limit_bytes=62 << 20
         ),
         cost_estimate=pl.CostEstimate(
             flops=18 * rows * local * width * width, transcendentals=0,
@@ -811,10 +860,7 @@
         name="qkv_forward",
     )(tokens_in.reshape(halves), own_pack)
     flat = rows * local, width
-    return (
-        x.reshape(flat), q.reshape(flat), k.reshape(flat), v.reshape(flat),
-        weights.reshape(-1, columns), small,
-    )
+    return x.reshape(flat), q.reshape(flat), k.reshape(flat), v.reshape(flat), xt, weights_t, small
 
 
 eps_norm = 1e-06
@@ -849,14 +895,14 @@
 
 
 OUT_B, GAIN_1, BIAS_1, OUTER_B, GAIN_2, BIAS_2, INNER_B = 2, 3, 4, 5, 6, 7, 8
-STEP_ROWS = 64
+STEP_ROWS = 512
 SMALL_ROWS = 16
 
 
 def middle_kernel(
     chunks, weights_in, small, att, tokens, cotangent,
     out, d_attn, d_att, d_weights, sums,
-    w, acc, act, slope, z_one, flow, rs_one, normed, normed_t, d_mlp, load_sem, store_sem,
+    w, acc, act, slope, z_one, flow, rs_one, normed, normed_t, d_mlp, part, load_sem, store_sem,
 ):
     step, steps = pl.program_id(0), pl.num_programs(0)
     rows, width = att.shape
@@ -877,7 +923,7 @@
     def _():
         for i in range(count):
             load(i).start()
-        sums[...] = jnp.zeros_like(sums)
+        part[...] = jnp.zeros_like(part)
 
         def clear(i, _):
             acc[i] = jnp.zeros_like(acc[i])
@@ -890,8 +936,11 @@
     def vector(i):
         return small[i : i + 1, :]
 
+    def eights(values):
+        return jnp.sum(values.reshape(-1, 8, values.shape[-1]), axis=0)
+
     def add_sum(i, values):
-        sums[pl.ds(i, 1), :] += jnp.sum(values, axis=0, keepdims=True)
+        part[i] += eights(values)
 
     def by_rows(body):
         def one(r, _):
@@ -960,9 +1009,7 @@
             cols = slice(n * 256, n * 256 + 256)
             d_act = dot_nt(d_mlp[...], w[1 + chunks + c, cols, :])
             d_pre = (slope[c, :, cols].astype(f32) * d_act).astype(bf16)
-            sums[pl.ds(INNER_B + c, 1), cols] += jnp.sum(
-                d_pre.astype(f32), axis=0, keepdims=True
-            )
+            part[INNER_B + c, :, cols] += eights(d_pre.astype(f32))
             slope[c, :, cols] = d_pre
         acc[1 + chunks + c] += dot_rows(act[c], d_mlp[...])
         acc[1 + c] += dot_f32(normed_t[...], slope[c])
@@ -997,6 +1044,7 @@
     def _():
         w[0] = acc[0].astype(bf16)
         store(0).start()
+        sums[...] = jnp.sum(part[...], axis=1)
         for i in range(count):
             store(i).wait()
 
@@ -1033,6 +1081,7 @@
             pltpu.VMEM((rows, width), bf16),
             pltpu.VMEM((width, rows), bf16),
             pltpu.VMEM((rows, width), bf16),
+            pltpu.VMEM((small.shape[0], 8, width), f32),
             pltpu.SemaphoreType.DMA((count,)),
             pltpu.SemaphoreType.DMA((count,)),
         ],
@@ -1198,7 +1247,7 @@
         return values[:, part_start(width, i) : part_start(width, i) + width]
 
     if paired:
-        flat_in, *qkv, first, small = qkv_forward(tokens_in, first)
+        flat_in, *qkv, turned_in, turned_w, small = qkv_forward(tokens_in, first)
     else:
         first = lax.all_gather(first, "fsdp", axis=0, tiled=True)
         small = first[:, width : width + SMALL_ROWS].astype(jnp.float32).T
@@ -1231,7 +1280,7 @@
     dq, out_tokens = lax.optimization_barrier((dq, out_tokens))
     if paired:
         d_query_w, d_key_w, d_value_w, sums, d_tokens_in = qkv_backward(
-            flat_in, dq, dk, dv, first, d_attn, sums, own
+            turned_in, dq, dk, dv, turned_w, d_attn, sums, own
         )
         d_second, sums = lax.optimization_barrier((d_second, sums))
     else:

time: 469 us -> 427 us (0.910)
  Pallas kernels: 383 us -> 345 us
  local copies, waits for them, and re-layouts: 48.6 us -> 36.6 us
  starting transfers between devices: 5.21 us -> 13.7 us
    pallas_call x1, Pallas kernels: 77 us -> 57 us  [attention_backward(): pl.pallas_call(functools.partial(backward_kernel, group), out_shape=(like...]
    pallas_call x1, Pallas kernels: 122 us -> 109 us  [middle(): pl.pallas_call(functools.partial(middle_kernel, chunks), grid=(tok_count...]
    pallas_call x1, Pallas kernels: 47.7 us -> 35 us  [attention_forward(): pl.pallas_call(functools.partial(forward_kernel, group), out_shape=(jax.S...]
    pallas_call x1, Pallas kernels: 67.7 us -> 78.8 us  [qkv_backward(): pl.pallas_call(functools.partial(qkv_backward_kernel, bits), out_shape=(s...]
    unnamed x80 -> x56, local copies, waits for them, and re-layouts: 25 us -> 13.8 us
    ppermute x2, starting transfers between devices: 4.82 us -> 13.5 us  [move(): return lax.ppermute(values, 'seq', pairs)]
  transfers between devices with their start and end apart: 5 -> 5, of which waited for: 1 -> 1; matrix products, arithmetic and copies ran while one was open for 5% -> 5% of each run, Pallas kernels for 56% -> 55%
where the time goes in v2:
time: 427 us; the launch traced here: 428 us
  Pallas kernels  345 us (81%)
  local copies, waits for them, and re-layouts  36.6 us (9%)
  between operations  14.5 us (3%)
  starting transfers between devices  13.7 us (3%)
  waiting for transfers between devices  10.5 us (2%)
  other arithmetic  7.05 us (2%)
    pallas_call x1, Pallas kernels, middle(): pl.pallas_call(functools.partial(middle_kernel, chunks), grid=(tok_count...  109 us
    pallas_call x1, Pallas kernels, qkv_backward(): pl.pallas_call(functools.partial(qkv_backward_kernel, bits), out_shape=(s...  78.8 us
    pallas_call x1, Pallas kernels, qkv_forward(): pl.pallas_call(functools.partial(qkv_forward_kernel, bits), out_shape=(li...  65.7 us
    pallas_call x1, Pallas kernels, attention_backward(): pl.pallas_call(functools.partial(backward_kernel, group), out_shape=(like...  57 us
    pallas_call x1, Pallas kernels, attention_forward(): pl.pallas_call(functools.partial(forward_kernel, group), out_shape=(jax.S...  35 us
    unnamed x56, local copies, waits for them, and re-layouts  13.8 us
    ppermute x2, starting transfers between devices, move(): return lax.ppermute(values, 'seq', pairs)  13.5 us
    ppermute x1, waiting for transfers between devices, sum_seq(): other = lax.ppermute(values, 'seq', [(0, 1), (1, 0)])  10.4 us
  transfers between devices with their start and end apart: 5, of which 1 were waited for; matrix products, arithmetic and copies ran while one was open for 5% of the time, Pallas kernels for 55%

profile of v2, /device:TPU:0, one launch (start us, length us, event | category | flops | bytes accessed | tf_op | source)
XLA Modules:
  0.0 427.8 jit_solution(15792783522468568386)
XLA Ops:
  7.4 1.4 copy.71
  8.8 0.6 copy.72
  9.5 1.1 reshape.736
  10.6 0.9 pad_maximum_fusion
  12.7 0.8 concatenate.12.own_in
  13.5 65.7 %qkv_forward.1 = (bf16[2,4,256,768]{3,2,1,0:T(8,128)(2,1)}, bf16[2,4,768,256]{3,2,1,0:T(8,128)(2,1)}, bf16[2,4,256,768]{3,2,1,0:T(8,128)(2,1)}, bf16[2,4,256,768...) custom-call(bf16[2,4,256,768]{3,2,1,0:T(8,128)(2,1)} %bitcast.94, ...), custom_call_target="tpu_custom_call" | custom-call | flops 21743271936 | bytes 25165824 | tf_op jit(solution)/shard_map/qkv_forward/pallas_call | solution.py:833
  79.2 2.8 constant_dynamic-slice_fusion.1
  82.1 1.3 collective-permute-start
  83.4 0.5 broadcast.485
  83.9 0.7 fusion.16
  85.1 0.2 multiply_reduce_fusion
  85.4 0.4 select_reduce_fusion
  85.8 0.2 convert_reduce_fusion
  86.3 0.7 pad_add_fusion
  87.0 0.6 fusion.14
  87.6 0.2 broadcast_in_dim.101
  87.8 0.2 bitcast_dynamic-update-slice_fusion.2
  88.0 1.7 copy-done.5
  89.7 0.5 and_select_fusion.1.n_ref
  90.2 0.6 compare_select_fusion.list_ref
  90.8 1.3 broadcast_in_dim.99.segc_ref
  92.1 35.0 %attention_forward.1 = (bf16[1,2048,768]{2,1,0:T(8,128)(2,1)}, f32[1,32,1,768]{3,2,1,0:T(1,128)}) custom-call(s32[1,32]{1,0:T(1,128)} %and_select_fusion.1.n_ref, s32[1,1024]{1,0:T(1,128)} %compare_select_fusion.list_ref, s32[1]{0:T(128)} %bitcast.3.total_ref, bf16[1,2048,768]{2,1,0:T(8,128)(2,1)} %bitcast.95, bf16[1,2048,768]{2,1,0:T(8,128)(2,1)} %bitcast.97, ...), custom_call_target="tpu_custom_call" | custom-call | flops 3221225472 | bytes 12582912 | tf_op jit(solution)/shard_map/attention_forward/pallas_call | solution.py:226
  127.1 2.7 bitcast_dynamic-update-slice_fusion.1
  129.8 108.9 %middle.1 = (bf16[2048,768]{1,0:T(8,128)(2,1)}, bf16[2048,768]{1,0:T(8,128)(2,1)}, bf16[2048,768]{1,0:T(8,128)(2,1)}, bf16[768,6912]{1,0:T(8,128)(2,1)}, f32[16,768]{1,0:T(8,128)}) custom-call(bf16[768,6912]{1,0:T(8,128)(2,1)} %all-gather.2.cloned.1.call-done.weights_in, f32[16,768]{1,0:T(8,128)} %get-tuple-element.51.small, bf16[2048,768]{1,0:T(8,128)(2,1)} %bitcast.102, ...), custom_call_target="tpu_custom_call" | custom-call | flops 130459631616 | bytes 40108032 | tf_op jit(solution)/shard_map/middle/pallas_call | solution.py:1063
  238.7 1.9 copy-done.3
  240.6 1.3 dynamic-slice_bitcast_fusion
  241.9 12.3 %collective-permute-start.1 = (bf16[1,1024,768]{2,1,0:T(8,128)(2,1)}, bf16[1,1024,768]{2,1,0:T(8,128)(2,1)}, u32[]{:S(2)}, u32[]{:S(2)}) collective-permute-start(bf16[1,1024,768]{2,1,0:T(8,128)(2,1)} %dynamic-slice_bitcast_fusion), channel_id=1, source_target_pairs={{16,0},{0,16},{17,1},{1,17},{18,2},{2,18},{19,3},{3,19},{20,4},{4,... | collective-permute-start | bytes 4718600 | tf_op jit(solution)/shard_map/ppermute | solution.py:1147
  254.1 0.2 broadcast_in_dim.104
  254.5 1.7 copy-done.4
  256.2 57.0 %attention_backward.1 = (bf16[1,2048,768]{2,1,0:T(8,128)(2,1)}, bf16[1,2048,768]{2,1,0:T(8,128)(2,1)}, bf16[1,2048,768]{2,1,0:T(8,128)(2,1)}) custom-call(s32[1,32]{1,0:T(1,128)} %and_select_fusion.1.n_ref, s32[1,1024]{1,0:T(1,128)} %compare_select_fusion.list_ref, s32[1]{0:T(128)} %bitcast.3.total_ref, bf16[1,2048,768]{2,1,0:T(8,128)(2,1)} %bitcast.96, ...), custom_call_target="tpu_custom_call" | custom-call | flops 8053063680 | bytes 25165824 | tf_op jit(solution)/shard_map/attention_backward/pallas_call | solution.py:350
  313.2 2.7 constant_dynamic-update-slice_fusion
  315.9 78.8 %qkv_backward.1 = (f32[48,768]{1,0:T(8,128)}, f32[48,768]{1,0:T(8,128)}, f32[48,768]{1,0:T(8,128)}, f32[16,768]{1,0:T(8,128)}, bf16[2,1024,768]{2,1,0:T(8,128)(2,1)}) custom-call(bf16[2,4,768,256]{3,2,1,0:T(8,128)(2,1)} %get-tuple-element.59.xt_in, bf16[2048,768]{1,0:T(8,128)(2,1)} %bitcast.104, bf16[2048,768]{1,0:T(8,128)(2,1)} %bitcast.105, ...), custom_call_target="tpu_custom_call" | custom-call | flops 48318382080 | bytes 25165824 | tf_op jit(solution)/shard_map/qkv_backward/pallas_call | solution.py:622
  394.9 0.8 dynamic-slice_bitcast_fusion.1
  395.7 0.7 reshape.745
  396.4 1.6 dynamic-slice_bitcast_fusion.2
  398.0 0.9 slice_reduce_fusion.2
  398.9 0.5 multiply_sqrt_fusion
  399.4 10.4 %collective-permute-done.2 = bf16[48,6912]{1,0:T(8,128)(2,1)S(1)} collective-permute-done((bf16[48,6912]{1,0:T(8,128)(2,1)}, bf16[48,6912]{1,0:T(8,128)(2,1)S(1)}, u32[]{:S(2)}, u32[]{:S(2)}) %collective-permute-start.2) | collective-permute-done | bytes 663584 | tf_op jit(solution)/shard_map/ppermute | solution.py:1123
  409.8 1.3 convert_add_fusion
  411.2 0.7 slice.62
  411.9 0.3 reshape.743
  412.1 0.7 copy.73
  412.9 1.3 copy.75
  414.2 1.0 reshape.746
  415.1 3.8 copy.88
  419.0 0.7 copy.89
  419.6 0.7 copy.90
  420.3 0.7 copy.91
  (83 shorter events, 2.6 us)
Async XLA Ops:
  7.2 77.4 %copy-start = (s32[2,32,3]{1,0,2:T(2,128)S(1)}, s32[2,32,3]{1,0,2:T(2,128)}, u32[]{:S(2)}) copy-start(s32[2,32,3]{1,0,2:T(2,128)} %param.22) | copy-start | bytes 2308
  7.2 3.4 copy-start.12
  7.2 4.4 %copy-start.14 = (bf16[48]{0:T(256)(128)(2,1)S(1)}, bf16[48]{0:T(256)(128)(2,1)}, u32[]{:S(2)}) copy-start(bf16[48]{0:T(256)(128)(2,1)} %param.25) | copy-start | bytes 292
  7.2 4.5 %copy-start.15 = (bf16[48]{0:T(256)(128)(2,1)S(1)}, bf16[48]{0:T(256)(128)(2,1)}, u32[]{:S(2)}) copy-start(bf16[48]{0:T(256)(128)(2,1)} %param.28) | copy-start | bytes 292
  7.2 4.6 %copy-start.16 = (bf16[48]{0:T(256)(128)(2,1)S(1)}, bf16[48]{0:T(256)(128)(2,1)}, u32[]{:S(2)}) copy-start(bf16[48]{0:T(256)(128)(2,1)} %param.30) | copy-start | bytes 292
  7.3 4.7 %copy-start.17 = (bf16[48]{0:T(256)(128)(2,1)S(1)}, bf16[48]{0:T(256)(128)(2,1)}, u32[]{:S(2)}) copy-start(bf16[48]{0:T(256)(128)(2,1)} %param.31) | copy-start | bytes 292
  7.3 4.8 %copy-start.18 = (bf16[48]{0:T(256)(128)(2,1)S(1)}, bf16[48]{0:T(256)(128)(2,1)}, u32[]{:S(2)}) copy-start(bf16[48]{0:T(256)(128)(2,1)} %param.32) | copy-start | bytes 292
  7.3 4.9 %copy-start.19 = (bf16[48]{0:T(256)(128)(2,1)S(1)}, bf16[48]{0:T(256)(128)(2,1)}, u32[]{:S(2)}) copy-start(bf16[48]{0:T(256)(128)(2,1)} %param.36) | copy-start | bytes 292
  7.3 5.0 %copy-start.20 = (bf16[48]{0:T(256)(128)(2,1)S(1)}, bf16[48]{0:T(256)(128)(2,1)}, u32[]{:S(2)}) copy-start(bf16[48]{0:T(256)(128)(2,1)} %param.37) | copy-start | bytes 292
  7.3 5.1 %copy-start.21 = (bf16[48]{0:T(256)(128)(2,1)S(1)}, bf16[48]{0:T(256)(128)(2,1)}, u32[]{:S(2)}) copy-start(bf16[48]{0:T(256)(128)(2,1)} %param.38) | copy-start | bytes 292
  7.3 5.2 %copy-start.22 = (bf16[192]{0:T(256)(128)(2,1)S(1)}, bf16[192]{0:T(256)(128)(2,1)}, u32[]{:S(2)}) copy-start(bf16[192]{0:T(256)(128)(2,1)} %param.34) | copy-start | bytes 1156
  7.3 5.3 %copy-start.9 = (bf16[48,768]{1,0:T(8,128)(2,1)S(1)}, bf16[48,768]{1,0:T(8,128)(2,1)}, u32[]{:S(2)}) copy-start(bf16[48,768]{1,0:T(8,128)(2,1)} %param.24) | copy-start | bytes 221188
  7.3 5.3 %copy-start.10 = (bf16[48,768]{1,0:T(8,128)(2,1)S(1)}, bf16[48,768]{1,0:T(8,128)(2,1)}, u32[]{:S(2)}) copy-start(bf16[48,768]{1,0:T(8,128)(2,1)} %param.26) | copy-start | bytes 221188
  7.3 5.3 %copy-start.11 = (bf16[48,768]{1,0:T(8,128)(2,1)S(1)}, bf16[48,768]{1,0:T(8,128)(2,1)}, u32[]{:S(2)}) copy-start(bf16[48,768]{1,0:T(8,128)(2,1)} %param.27) | copy-start | bytes 221188
  7.3 122.4 %all-gather.2.cloned.1.call-start = ((), (), s32[]{:S(2)}) async-start(), calls=%async_computation.1 | async-start | bytes 11280384 | tf_op jit(solution)/shard_map/all_gather | solution.py:1236
  11.5 383.2 %reduce-scatter.2.cloned.1.call-start = ((), (), s32[]{:S(2)}) async-start(), calls=%async_computation.2 | async-start | bytes 11280384 | tf_op jit(solution)/shard_map/reduce_scatter | solution.py:1272
  79.2 4.7 %copy-start.13 = (s32[2,2048]{1,0:T(2,128)S(1)}, s32[2,2048]{1,0:T(2,128)}, u32[]{:S(2)}) copy-start(s32[2,2048]{1,0:T(2,128)} %param.21) | copy-start | bytes 49156
  79.2 5.5 %copy-start.23 = (s32[2,2]{1,0:T(2,128)S(1)}, s32[2,2]{1,0:T(2,128)}, u32[]{:S(2)}) copy-start(s32[2,2]{1,0:T(2,128)} %param.23) | copy-start | bytes 52
  79.2 8.6 %copy-start.2 = (bf16[2,1024,768]{2,1,0:T(8,128)(2,1)S(1)}, bf16[2,1024,768]{2,1,0:T(8,128)(2,1)}, u32[]{:S(2)}) copy-start(bf16[2,1024,768]{2,1,0:T(8,128)(2,1)} %param.39) | copy-start | bytes 9437188
  82.1 45.1 %collective-permute-start = (bf16[1,1024,768]{2,1,0:T(8,128)(2,1)}, bf16[1,1024,768]{2,1,0:T(8,128)(2,1)}, u32[]{:S(2)}, u32[]{:S(2)}) collective-permute-start(bf16[1,1024,768]{2,1,0:T(8,128)(2,1)} %constant_dynamic-slice_fusion.1), channel_id=1, source_target_pairs={{0,16},{16,0},{1,17},{17,1},{2,18},{18,2},{3,19},{19,3},{4,20},{20... | collective-permute-start | bytes 4718600 | tf_op jit(solution)/shard_map/ppermute | solution.py:1147
  88.0 1.7 copy-start.5
  238.7 1.9 copy-start.3
  241.9 71.3 %collective-permute-start.1 = (bf16[1,1024,768]{2,1,0:T(8,128)(2,1)}, bf16[1,1024,768]{2,1,0:T(8,128)(2,1)}, u32[]{:S(2)}, u32[]{:S(2)}) collective-permute-start(bf16[1,1024,768]{2,1,0:T(8,128)(2,1)} %dynamic-slice_bitcast_fusion), channel_id=1, source_target_pairs={{16,0},{0,16},{17,1},{1,17},{18,2},{2,18},{19,3},{3,19},{20,4},{4,... | collective-permute-start | bytes 4718600 | tf_op jit(solution)/shard_map/ppermute | solution.py:1147
  254.5 1.7 copy-start.4
  394.8 15.0 %collective-permute-start.2 = (bf16[48,6912]{1,0:T(8,128)(2,1)}, bf16[48,6912]{1,0:T(8,128)(2,1)S(1)}, u32[]{:S(2)}, u32[]{:S(2)}) collective-permute-start(bf16[48,6912]{1,0:T(8,128)(2,1)} %reduce-scatter.2.cloned.1.call-done), channel_id=1, source_target_pairs={{0,16},{16,0},{1,17},{17,1},{2,18},{18,2},{3,19},{19,3},{4,20},{20... | collective-permute-start | bytes 1990664 | tf_op jit(solution)/shard_map/ppermute | solution.py:1123
  415.1 5.8 %copy-start.1 = (s32[2,32,3]{1,0,2:T(2,128)S(1)}, s32[2,32,3]{1,0,2:T(2,128)}, u32[]{:S(2)}) copy-start(s32[2,32,3]{1,0,2:T(2,128)} %param.22) | copy-start | bytes 2308
  415.1 3.8 copy-start.8
  415.1 4.5 %copy-start.7 = (f32[48,768]{1,0:T(8,128)S(1)}, f32[48,768]{1,0:T(8,128)}, u32[]{:S(2)}) copy-start(f32[48,768]{1,0:T(8,128)} %get-tuple-element.149) | copy-start | bytes 442372
  415.1 5.1 %copy-start.6 = (f32[48,768]{1,0:T(8,128)S(1)}, f32[48,768]{1,0:T(8,128)}, u32[]{:S(2)}) copy-start(f32[48,768]{1,0:T(8,128)} %get-tuple-element.150) | copy-start | bytes 442372
Sparse Core Ops, SparseCore 0:
  11.7 103.7 all-gather.1
  238.9 139.3 reduce-scatter.1

commit v3 on v2

--- a/solution.py
+++ b/solution.py
@@ -408,13 +408,21 @@
     own, width = wq_out.shape
     owners = 1 << bits
     sources = (dq_in, dk_in, dv_in)
-    loads = [
-        pltpu.make_async_copy(wt_in, wt, in_sem.at[0]),
-        pltpu.make_async_copy(res_in, res, in_sem.at[1]),
-        pltpu.make_async_copy(small_in, small.at[0], in_sem.at[2]),
-        pltpu.make_async_copy(xt_in, xt, in_sem.at[3]),
-    ] + [pltpu.make_async_copy(sources[i], grads.at[i], in_sem.at[4 + i]) for i in range(3)]
-    for i in (3, 4, 5, 6, 0, 1, 2):
+    rows_of = [pl.ds(pl.multiple_of(p * half, half), half) for p in (1 - side, side)]
+    loads = [pltpu.make_async_copy(wt_in, wt, in_sem.at[0])]
+    for p in range(2):
+        for i in range(3):
+            loads.append(
+                pltpu.make_async_copy(
+                    sources[i].at[rows_of[p]], grads.at[i, rows_of[p]], in_sem.at[1 + 4 * p + i]
+                )
+            )
+        loads.append(
+            pltpu.make_async_copy(res_in.at[rows_of[p]], res.at[rows_of[p]], in_sem.at[4 + 4 * p])
+        )
+    loads.append(pltpu.make_async_copy(xt_in, xt, in_sem.at[9]))
+    loads.append(pltpu.make_async_copy(small_in, small.at[0], in_sem.at[10]))
+    for i in (0, 1, 2, 3, 4, 9, 5, 6, 7, 8, 10):
         loads[i].start()
     all_arrived(bits)
 
@@ -547,54 +555,52 @@
         if bit < bits:
             small_hop(bit + 1).start()
 
-    for i in (3, 4):
+    def column_sums(i, spot):
+        def one(c, total):
+            block = grads[i, pl.ds(pl.multiple_of(c * 256, 256), 256), :].astype(jnp.float32)
+            return total + jnp.sum(block.reshape(32, 8, width), axis=0)
+
+        total = lax.fori_loop(
+            0, grads.shape[1] // 256, one, jnp.zeros((8, width), jnp.float32)
+        )
+        small[0, spot : spot + 1] = jnp.sum(total, axis=0, keepdims=True)
+
+    for i in range(5):
         loads[i].wait()
-    weights(0)
-    hop(0, 0).start()
-    for i in (5, 6, 0, 1):
+    send_piece(0, 0)
+    for i in range(5, 11):
         loads[i].wait()
-    lax.fori_loop(0, pieces, send_piece, 0)
-    advance(0, 0)
-    weights(1)
-    hop(1, 0).start()
-    loads[2].wait()
-    for spot, i in ((0, 0), (1, 2)):
-        def column_sums(c, total):
-            block = grads[i, pl.ds(pl.multiple_of(c * 128, 128), 128), :].astype(jnp.float32)
-            return total + jnp.sum(block.reshape(16, 8, width), axis=0)
-
-        total = lax.fori_loop(
-            0, grads.shape[1] // 128, column_sums, jnp.zeros((8, width), jnp.float32)
-        )
-        small[0, spot : spot + 1] = jnp.sum(total, axis=0, keepdims=True)
+
+    def begin(i, _):
+        weights(i)
+        hop(i, 0).start()
+        send_piece(i + 1, 0)
+        advance(i, 0)
+        return 0
+
+    lax.fori_loop(0, 3, begin, 0)
+    column_sums(0, 0)
+    column_sums(2, 1)
     small_hop(0).start()
-    weights(2)
-    hop(2, 0).start()
+
+    def second(i, _):
+        keep_piece(i, 0)
+        advance(i, 1)
+        return 0
+
+    lax.fori_loop(0, 3, second, 0)
     small_advance(0)
-    plan = []
-    for step in range(1, bits + 2):
-        todo = []
+    keep_piece(3, 0)
+    for bit in range(2, bits):
         for i in range(3):
-            bit = step - i
-            if 0 <= bit < bits:
-                todo.append((i, bit))
-        plan.append((todo, step))
-    done = 0
-    for todo, step in plan:
-        for i, bit in todo:
             advance(i, bit)
-        if step <= bits:
-            small_advance(step)
-        if done < pieces:
-            keep_piece(done, 0)
-            done += 1
+        small_advance(bit - 1)
+    for bit in range(bits - 1, bits + 1):
+        small_advance(bit)
     for i in range(3):
         finish(i)
     small_copy = pltpu.make_async_copy(small.at[bits + 1], small_out, out_sem.at[3])
     small_copy.start()
-    while done < pieces:
-        keep_piece(done, 0)
-        done += 1
     for i in range(3):
         written(i).wait()
         cross(i).wait_send()
@@ -641,7 +647,7 @@
             pltpu.VMEM((bits + 2,) + small.shape, f32),
             pltpu.VMEM((bits + 1,) + small.shape, f32),
             pltpu.VMEM((3, own, width), f32),
-            dma((7,)), dma((pieces,)), dma((pieces,)), dma((pieces,)),
+            dma((11,)), dma((pieces,)), dma((pieces,)), dma((pieces,)),
             dma((3, bits)), dma((3, bits)), dma((3,)), dma((3,)),
             dma((bits + 1,)), dma((bits + 1,)), dma((4,)),
         ],
@@ -657,8 +663,8 @@
 
 
 def qkv_forward_kernel(
-    bits, tokens_in, own_in,
-    x_out, xt_out, q_out, k_out, v_out, wt_out, small_out,
+    bits, tokens_in, own_in, grad_in,
+    grad_out, x_out, xt_out, q_out, k_out, v_out, wt_out, small_out,
     x, xt, w, wt, qkv, small,
     own_sem, tok_send, tok_land, load_sem, send_sem, land_sem, x_sem, xt_sem, out_sem, w_sem,
     small_sem,
@@ -675,6 +681,8 @@
 
     own_tokens = pltpu.make_async_copy(tokens_in.at[side], x.at[side], own_sem.at[0])
     own_tokens.start()
+    grad_rows = pltpu.make_async_copy(grad_in.at[1 - side], grad_out, own_sem.at[1])
+    grad_rows.start()
 
     def load(part):
         spot = tuple(mine[b] for b in range(bits - 1, -1, -1)) + (slice(None), columns[part])
@@ -796,6 +804,7 @@
         w_copy(part).wait()
         for hops in range(bits):
             hop(part, hops).wait_send()
+    grad_rows.wait()
     pltpu.make_async_copy(small, small_out, small_sem.at[0]).wait()
     for half in range(2):
         for i in range(pieces):
@@ -817,7 +826,7 @@
     )
 
 
-def qkv_forward(tokens_in, own_pack):
+def qkv_forward(tokens_in, own_pack, out_grad):
     rows, local, width = tokens_in.shape
     own, columns = own_pack.shape
     bits = lax.axis_size("fsdp").bit_length() - 1
@@ -830,15 +839,16 @@
     anywhere = pl.BlockSpec(memory_space=pltpu.HBM)
     like = jax.ShapeDtypeStruct(halves, bf16)
     turned = (2, pieces, width, piece)
-    x, xt, q, k, v, weights_t, small = pl.pallas_call(
+    grad, x, xt, q, k, v, weights_t, small = pl.pallas_call(
         functools.partial(qkv_forward_kernel, bits),
         out_shape=(
+            jax.ShapeDtypeStruct((local, width), bf16),
             like, jax.ShapeDtypeStruct(turned, bf16), like, like, like,
             jax.ShapeDtypeStruct((3, width, width), bf16),
             jax.ShapeDtypeStruct((SMALL_ROWS, width), jnp.float32),
         ),
-        in_specs=[anywhere] * 2,
-        out_specs=(anywhere,) * 7,
+        in_specs=[anywhere] * 3,
+        out_specs=(anywhere,) * 8,
         scratch_shapes=[
             pltpu.VMEM(halves, bf16),
             pltpu.VMEM(turned, bf16),
@@ -846,7 +856,7 @@
             pltpu.VMEM((3, width, width), bf16),
             pltpu.VMEM((3,) + halves, bf16),
             pltpu.VMEM((SMALL_ROWS, width), jnp.float32),
-            dma((1,)), dma((pieces,)), dma((pieces,)), dma((3,)),
+            dma((2,)), dma((pieces,)), dma((pieces,)), dma((3,)),
             dma((3, bits)), dma((3, bits)), dma((2, pieces)), dma((2, pieces)),
             dma((3, 2, pieces)), dma((3,)), dma((1,)),
         ],
@@ -858,9 +868,11 @@
             bytes_accessed=16 * rows * local * width,
         ),
         name="qkv_forward",
-    )(tokens_in.reshape(halves), own_pack)
+    )(tokens_in.reshape(halves), own_pack, out_grad)
     flat = rows * local, width
-    return x.reshape(flat), q.reshape(flat), k.reshape(flat), v.reshape(flat), xt, weights_t, small
+    return (
+        x.reshape(flat), q.reshape(flat), k.reshape(flat), v.reshape(flat), xt, weights_t, small, grad
+    )
 
 
 eps_norm = 1e-06
@@ -900,14 +912,15 @@
 
 
 def middle_kernel(
-    chunks, weights_in, small, att, tokens, cotangent,
-    out, d_attn, d_att, d_weights, sums,
+    chunks, side, weights_in, small, att, tokens, grad_own, grad_other,
+    out_keep, out_send, d_attn, d_att, d_weights, sums,
     w, acc, act, slope, z_one, flow, rs_one, normed, normed_t, d_mlp, part, load_sem, store_sem,
 ):
     step, steps = pl.program_id(0), pl.num_programs(0)
     rows, width = att.shape
     f32, bf16 = jnp.float32, jnp.bfloat16
     count = 2 * chunks + 1
+    staying = step // (steps // 2) == side[0]
 
     def load(i):
         return pltpu.make_async_copy(
@@ -930,8 +943,7 @@
             return 0
 
         lax.fori_loop(0, count, clear, 0)
-        for i in range(count):
-            load(i).wait()
+        load(0).wait()
 
     def vector(i):
         return small[i : i + 1, :]
@@ -967,6 +979,10 @@
     normed_t[...] = normed[...].T
 
     def inner(c, _):
+        @pl.when(step == 0)
+        def _():
+            load(1 + c).wait()
+
         for n in range(width // 256):
             cols = slice(n * 256, n * 256 + 256)
             pre = dot_f32(normed[...], w[1 + c, :, cols]) + small[pl.ds(INNER_B + c, 1), cols]
@@ -976,6 +992,12 @@
         return 0
 
     lax.fori_loop(0, chunks, inner, 0)
+
+    @pl.when(step == 0)
+    def _():
+        for i in range(1 + chunks, count):
+            load(i).wait()
+
     flow[...] = dot_f32(act[0], w[1 + chunks])
 
     def outer(c, _):
@@ -991,8 +1013,17 @@
         centred = resid - row_mean(resid)
         scale = lax.rsqrt(row_mean(centred * centred) + eps_norm)
         z = centred * scale
-        out[r, :] = (z * vector(GAIN_2) + vector(BIAS_2)).astype(bf16)
-        grad = cotangent[r, :].astype(f32)
+        result = (z * vector(GAIN_2) + vector(BIAS_2)).astype(bf16)
+
+        @pl.when(staying)
+        def _():
+            out_keep[r, :] = result
+
+        @pl.when(jnp.logical_not(staying))
+        def _():
+            out_send[r, :] = result
+
+        grad = jnp.where(staying, grad_own[r, :], grad_other[r, :]).astype(f32)
         add_sum(GAIN_2, grad * z)
         add_sum(BIAS_2, grad)
         grad = grad * vector(GAIN_2)
@@ -1049,28 +1080,43 @@
             store(i).wait()
 
 
-def middle(weights, small, att, tokens, cotangent):
+def middle(side, weights, small, att, tokens, grad_own, grad_other):
     tok_count, width = att.shape
     chunks = (weights.shape[1] // width - 1) // 2
     count = 2 * chunks + 1
     rows = 512
     f32, bf16 = jnp.float32, jnp.bfloat16
-    tile = pl.BlockSpec((rows, width), lambda i: (i, 0))
-    fixed = pl.BlockSpec(small.shape, lambda i: (0, 0), pipeline_mode=pl.Buffered(1))
+    half = tok_count // rows // 2
+
+    def early(i):
+        return jnp.minimum(i, half - 1)
+
+    def late(i):
+        return jnp.maximum(i - half, 0)
+
+    tile = pl.BlockSpec((rows, width), lambda i, s: (i, 0))
+    keep = pl.BlockSpec((rows, width), lambda i, s: (jnp.where(s[0] == 0, early(i), late(i)), 0))
+    send = pl.BlockSpec((rows, width), lambda i, s: (jnp.where(s[0] == 0, late(i), early(i)), 0))
+    fixed = pl.BlockSpec(small.shape, lambda i, s: (0, 0), pipeline_mode=pl.Buffered(1))
     anywhere = pl.BlockSpec(memory_space=pl.ANY)
     like = jax.ShapeDtypeStruct((tok_count, width), bf16)
+    part = jax.ShapeDtypeStruct((tok_count // 2, width), bf16)
     flops = 6 * tok_count * width * width * count
     return pl.pallas_call(
         functools.partial(middle_kernel, chunks),
-        grid=(tok_count // rows,),
         out_shape=(
-            like, like, like,
+            part, part, like, like,
             jax.ShapeDtypeStruct(weights.shape, bf16),
             jax.ShapeDtypeStruct(small.shape, f32),
         ),
-        in_specs=[anywhere, fixed, tile, tile, tile],
-        out_specs=(tile, tile, tile, anywhere, pl.BlockSpec(small.shape, lambda i: (0, 0))),
-        scratch_shapes=[
+        grid_spec=pltpu.PrefetchScalarGridSpec(
+          num_scalar_prefetch=1,
+          grid=(tok_count // rows,),
+          in_specs=[anywhere, fixed, tile, tile, keep, send],
+          out_specs=(
+            keep, send, tile, tile, anywhere, pl.BlockSpec(small.shape, lambda i, s: (0, 0))
+          ),
+          scratch_shapes=[
             pltpu.VMEM((count, width, width), bf16),
             pltpu.VMEM((count, width, width), f32),
             pltpu.VMEM((chunks, rows, width), bf16),
@@ -1084,14 +1130,15 @@
             pltpu.VMEM((small.shape[0], 8, width), f32),
             pltpu.SemaphoreType.DMA((count,)),
             pltpu.SemaphoreType.DMA((count,)),
-        ],
+          ],
+        ),
         compiler_params=pltpu.CompilerParams(vmem_limit_bytes=62 << 20),
         cost_estimate=pl.CostEstimate(
             flops=2 * flops, transcendentals=tok_count * width * chunks,
             bytes_accessed=12 * tok_count * width + 4 * weights.size,
         ),
         name="middle",
-    )(weights, small, att, tokens, cotangent)
+    )(side.reshape(1), weights, small, att, tokens, grad_own, grad_other)
 
 
 def contract_rows(left, right):
@@ -1224,7 +1271,7 @@
     own = w_query.shape[0]
     chunks = b_inner.shape[0] // own
     regroup = Regroup(row_count)
-    paired = row_count == 2 and seq_count == 2 and fsdp_count & (fsdp_count - 1) == 0
+    paired = row_count == 2 and seq_count == 2 and fsdp_count in (4, 8, 16, 32)
 
     vectors = [b_query, b_value, b_attn_out, ln1_gain, ln1_bias, b_outer, ln2_gain, ln2_bias]
     columns = [x[:, None] for x in vectors] + [b_inner.reshape(own, chunks)]
@@ -1246,8 +1293,14 @@
     def part_of(values, i):
         return values[:, part_start(width, i) : part_start(width, i) + width]
 
+    side = lax.axis_index("seq") if paired else jnp.int32(0)
+    swap = [(0, 1), (1, 0)]
     if paired:
-        flat_in, *qkv, turned_in, turned_w, small = qkv_forward(tokens_in, first)
+        flat_in, *qkv, turned_in, turned_w, small, leaving = qkv_forward(
+            tokens_in, first, out_grad
+        )
+        grad_other = lax.ppermute(leaving, "seq", swap)
+        grad_own = lax.dynamic_index_in_dim(out_grad, side, 0, keepdims=False)
     else:
         first = lax.all_gather(first, "fsdp", axis=0, tiled=True)
         small = first[:, width : width + SMALL_ROWS].astype(jnp.float32).T
@@ -1258,15 +1311,16 @@
              + biases[i]).astype(jnp.bfloat16)
             for i in range(3)
         ]
-    q, out_grad = lax.optimization_barrier((qkv[0], out_grad))
-    flat_grad = regroup.gather(out_grad).reshape(tok_count, width)
-    q, k, v = (regroup.to_heads(split_rows(x)) for x in (q, qkv[1], qkv[2]))
+        flat_grad = regroup.gather(out_grad).reshape(tok_count, width)
+        grad_own, grad_other = flat_grad[: tok_count // 2], flat_grad[tok_count // 2 :]
+    q, k, v = (regroup.to_heads(split_rows(x)) for x in qkv)
     att, lse = attention_forward(q, k, v, plan)
     att_flat = regroup.from_heads(att).reshape(tok_count, width)
-    out_tokens, d_attn, d_att, d_second, sums = middle(
-        second, small, att_flat, flat_in, flat_grad
-    )
-    out_tokens = regroup.scatter(split_rows(out_tokens))
+    kept, sent, d_attn, d_att, d_second, sums = middle(
+        side, second, small, att_flat, flat_in, grad_own, grad_other
+    )
+    if paired:
+        sent = lax.ppermute(sent, "seq", swap)
 
     def scattered(values):
         return lax.psum_scatter(values, "fsdp", scatter_dimension=0, tiled=True)
@@ -1277,12 +1331,15 @@
     )
     dq, dk, dv = (regroup.from_heads(x).reshape(tok_count, width) for x in (dq, dk, dv))
     mine = lax.axis_index("fsdp")
-    dq, out_tokens = lax.optimization_barrier((dq, out_tokens))
+    dq, sent = lax.optimization_barrier((dq, sent))
     if paired:
         d_query_w, d_key_w, d_value_w, sums, d_tokens_in = qkv_backward(
             turned_in, dq, dk, dv, turned_w, d_attn, sums, own
         )
         d_second, sums = lax.optimization_barrier((d_second, sums))
+        place = jnp.arange(2, dtype=jnp.int32)[:, None, None]
+        out_tokens = jnp.where(place == side, kept[None], sent[None])
+        d_tokens_in = jnp.where(place >= -side, d_tokens_in, jnp.zeros_like(d_tokens_in))
     else:
         for spot, part in ((0, dq), (1, dv)):
             sums = sums.at[spot].set(jnp.sum(part.astype(jnp.float32), axis=0))
@@ -1295,6 +1352,7 @@
         for i, part in enumerate((dq, dk, dv)):
             d_tokens = d_tokens + times_transpose(part, part_of(first, i))
         d_tokens_in = regroup.scatter(split_rows(d_tokens.astype(jnp.bfloat16)))
+        out_tokens = regroup.scatter(split_rows(jnp.concatenate([kept, sent])))
     d_second = sum_seq(d_second)
     d_inner_w = (
         d_second[:, width : (1 + chunks) * width]

time: 427 us -> 420 us (0.984)
  local copies, waits for them, and re-layouts: 36.6 us -> 21.2 us
  other arithmetic: 7.05 us -> 13.1 us
    unnamed x56 -> x51, local copies, waits for them, and re-layouts: 13.8 us -> 5.94 us
    select_n x0 -> x2, other arithmetic: none -> 5.98 us  [the longest x1 3.95 us: shards(): jnp.where(place >= -side, d_tokens_in, jnp.zeros_like(d_tokens_in))]
    dynamic_update_slice x4 -> x0, local copies, waits for them, and re-layouts: 5.71 us -> none  [the longest x2 2.87 us: scatter(): out = lax.dynamic_update_slice_in_dim(out, chunk, pick * rows, 0)]
    pallas_call x1, Pallas kernels: 78.8 us -> 83.7 us  [qkv_backward(): pl.pallas_call(functools.partial(qkv_backward_kernel, bits), out_shape=(s...]
  transfers between devices with their start and end apart: 5 -> 5, of which waited for: 1 -> 1; matrix products, arithmetic and copies ran while one was open for 5% -> 5% of each run, Pallas kernels for 55% -> 57%
where the time goes in v3:
time: 420 us
  Pallas kernels  346 us (82%)
  local copies, waits for them, and re-layouts  21.2 us (5%)
  starting transfers between devices  15.4 us (4%)
  between operations  14.5 us (3%)
  other arithmetic  13.1 us (3%)
  waiting for transfers between devices  9.83 us (2%)
    pallas_call x1, Pallas kernels, middle(): pl.pallas_call(functools.partial(middle_kernel, chunks), out_shape=(part,...  107 us
    pallas_call x1, Pallas kernels, qkv_backward(): pl.pallas_call(functools.partial(qkv_backward_kernel, bits), out_shape=(s...  83.7 us
    pallas_call x1, Pallas kernels, qkv_forward(): pl.pallas_call(functools.partial(qkv_forward_kernel, bits), out_shape=(ja...  66.5 us
    pallas_call x1, Pallas kernels, attention_backward(): pl.pallas_call(functools.partial(backward_kernel, group), out_shape=(like...  54.7 us
    pallas_call x1, Pallas kernels, attention_forward(): pl.pallas_call(functools.partial(forward_kernel, group), out_shape=(jax.S...  33.4 us
    ppermute x1, starting transfers between devices, shards(): sent = lax.ppermute(sent, 'seq', swap)  14 us
    ppermute x1, waiting for transfers between devices, sum_seq(): other = lax.ppermute(values, 'seq', [(0, 1), (1, 0)])  9.76 us
  transfers between devices with their start and end apart: 5, of which 1 were waited for; matrix products, arithmetic and copies ran while one was open for 5% of the time, Pallas kernels for 57%

profile of v3, /device:TPU:0, one launch (start us, length us, event | category | flops | bytes accessed | tf_op | source)
XLA Modules:
  0.0 419.5 jit_solution(15458598230223538815)
XLA Ops:
  7.4 1.4 copy.63
  8.8 0.6 copy.64
  9.5 1.1 reshape.741
  10.6 0.9 pad_maximum_fusion
  11.6 0.1 copy.65
  12.0 0.1 copy.69
  12.1 0.1 copy.70
  12.2 0.1 copy.71
  12.4 0.1 copy.72
  12.5 0.1 reshape.743
  12.6 0.8 concatenate.13.own_in
  13.4 66.5 %qkv_forward.1 = (bf16[1024,768]{1,0:T(8,128)(2,1)}, bf16[2,4,256,768]{3,2,1,0:T(8,128)(2,1)}, bf16[2,4,768,256]{3,2,1,0:T(8,128)(2,1)}, bf16[2,4,256,768]{3,2,1...) custom-call(bf16[2,4,256,768]{3,2,1,0:T(8,128)(2,1)} %bitcast.83, ...), custom_call_target="tpu_custom_call" | custom-call | flops 21743271936 | bytes 25165824 | tf_op jit(solution)/shard_map/qkv_forward/pallas_call | solution.py:842
  79.9 1.3 collective-permute-start
  81.2 0.5 broadcast.492
  81.7 0.7 fusion.16
  82.5 0.2 slice_reduce_fusion
  83.0 0.2 multiply_reduce_fusion
  83.2 0.4 select_reduce_fusion
  83.7 0.2 convert_reduce_fusion
  84.1 0.7 pad_add_fusion
  84.8 0.6 fusion.14
  85.5 2.7 dynamic-slice_bitcast_fusion.grad_own
  88.2 0.5 and_select_fusion.1.n_ref
  88.7 0.6 compare_select_fusion.list_ref
  89.3 1.3 broadcast_in_dim.126.segc_ref
  90.6 33.4 %attention_forward.1 = (bf16[1,2048,768]{2,1,0:T(8,128)(2,1)}, f32[1,32,1,768]{3,2,1,0:T(1,128)}) custom-call(s32[1,32]{1,0:T(1,128)} %and_select_fusion.1.n_ref, s32[1,1024]{1,0:T(1,128)} %compare_select_fusion.list_ref, s32[1]{0:T(128)} %bitcast.15.total_ref, bf16[1,2048,768]{2,1,0:T(8,128)(2,1)} %bitcast.84, bf16[1,2048,768]{2,1,0:T(8,128)(2,1)} %bitcast.86, ...), custom_call_target="tpu_custom_call" | custom-call | flops 3221225472 | bytes 12582912 | tf_op jit(solution)/shard_map/attention_forward/pallas_call | solution.py:226
  124.0 1.1 copy-done.20
  125.2 107.3 %middle.1 = (bf16[1024,768]{1,0:T(8,128)(2,1)}, bf16[1024,768]{1,0:T(8,128)(2,1)}, bf16[2048,768]{1,0:T(8,128)(2,1)}, bf16[2048,768]{1,0:T(8,128)(2,1)}, bf16[768,6912]{1,0:T(8,128)(2,1)}, /*index=5*/f32[16,768]{1,0:T(8,128)}) custom-call(s32[1]{0:T(128)} %bitcast.side, bf16[768,6912]{1,0:T(8,128)(2,1)} %all-gather.2.cloned.1.call-done.weights_in, ...), custom_call_target="tpu_custom_call" | custom-call | flops 130459631616 | bytes 40108032 | tf_op jit(solution)/shard_map/middle/pallas_call | solution.py:1105
  232.5 14.0 %collective-permute-start.1 = (bf16[1024,768]{1,0:T(8,128)(2,1)}, bf16[1024,768]{1,0:T(8,128)(2,1)S(1)}, u32[]{:S(2)}, u32[]{:S(2)}) collective-permute-start(bf16[1024,768]{1,0:T(8,128)(2,1)} %get-tuple-element.57), channel_id=1, source_target_pairs={{0,16},{16,0},{1,17},{17,1},{2,18},{18,2},{3,19},{19,3},{4,20},{20... | collective-permute-start | bytes 4718600 | tf_op jit(solution)/shard_map/ppermute | solution.py:1323
  246.6 54.7 %attention_backward.1 = (bf16[1,2048,768]{2,1,0:T(8,128)(2,1)}, bf16[1,2048,768]{2,1,0:T(8,128)(2,1)}, bf16[1,2048,768]{2,1,0:T(8,128)(2,1)}) custom-call(s32[1,32]{1,0:T(1,128)} %and_select_fusion.1.n_ref, s32[1,1024]{1,0:T(1,128)} %compare_select_fusion.list_ref, s32[1]{0:T(128)} %bitcast.15.total_ref, bf16[1,2048,768]{2,1,0:T(8,128)(2,1)} %bitcast.85, ...), custom_call_target="tpu_custom_call" | custom-call | flops 8053063680 | bytes 25165824 | tf_op jit(solution)/shard_map/attention_backward/pallas_call | solution.py:350
  301.2 83.7 %qkv_backward.1 = (f32[48,768]{1,0:T(8,128)}, f32[48,768]{1,0:T(8,128)}, f32[48,768]{1,0:T(8,128)}, f32[16,768]{1,0:T(8,128)}, bf16[2,1024,768]{2,1,0:T(8,128)(2,1)}) custom-call(bf16[2,4,768,256]{3,2,1,0:T(8,128)(2,1)} %get-tuple-element.59.xt_in, bf16[2048,768]{1,0:T(8,128)(2,1)} %bitcast.93, bf16[2048,768]{1,0:T(8,128)(2,1)} %bitcast.94, ...), custom_call_target="tpu_custom_call" | custom-call | flops 48318382080 | bytes 25165824 | tf_op jit(solution)/shard_map/qkv_backward/pallas_call | solution.py:628
  384.9 3.9 broadcast_select_fusion
  388.9 2.0 broadcast_select_fusion.1
  390.9 0.8 dynamic-slice_bitcast_fusion.1
  391.8 0.7 reshape.753
  392.4 1.6 dynamic-slice_bitcast_fusion.2
  394.0 0.9 slice_reduce_fusion.2
  394.9 0.5 multiply_sqrt_fusion
  395.4 9.8 %collective-permute-done.2 = bf16[48,6912]{1,0:T(8,128)(2,1)} collective-permute-done((bf16[48,6912]{1,0:T(8,128)(2,1)}, bf16[48,6912]{1,0:T(8,128)(2,1)}, u32[]{:S(2)}, u32[]{:S(2)}) %collective-permute-start.2) | collective-permute-done | bytes 663584 | tf_op jit(solution)/shard_map/ppermute | solution.py:1170
  405.2 1.4 convert_add_fusion
  406.7 0.7 slice.62
  407.4 0.3 reshape.751
  407.7 0.7 copy.73
  408.5 1.3 copy.75
  409.7 1.0 reshape.754
  410.7 0.7 copy.83
  411.4 0.7 copy.84
  412.0 0.7 copy.85
  (75 shorter events, 1.5 us)
Async XLA Ops:
  7.2 75.3 %copy-start = (s32[2,32,3]{1,0,2:T(2,128)S(1)}, s32[2,32,3]{1,0,2:T(2,128)}, u32[]{:S(2)}) copy-start(s32[2,32,3]{1,0,2:T(2,128)} %param.22) | copy-start | bytes 2308
  7.2 3.4 copy-start.9
  7.2 4.4 %copy-start.11 = (bf16[48]{0:T(256)(128)(2,1)S(1)}, bf16[48]{0:T(256)(128)(2,1)}, u32[]{:S(2)}) copy-start(bf16[48]{0:T(256)(128)(2,1)} %param.25) | copy-start | bytes 292
  7.2 4.5 %copy-start.12 = (bf16[48]{0:T(256)(128)(2,1)S(1)}, bf16[48]{0:T(256)(128)(2,1)}, u32[]{:S(2)}) copy-start(bf16[48]{0:T(256)(128)(2,1)} %param.28) | copy-start | bytes 292
  7.2 4.6 %copy-start.13 = (bf16[48]{0:T(256)(128)(2,1)S(1)}, bf16[48]{0:T(256)(128)(2,1)}, u32[]{:S(2)}) copy-start(bf16[48]{0:T(256)(128)(2,1)} %param.30) | copy-start | bytes 292
  7.3 4.7 %copy-start.14 = (bf16[48]{0:T(256)(128)(2,1)S(1)}, bf16[48]{0:T(256)(128)(2,1)}, u32[]{:S(2)}) copy-start(bf16[48]{0:T(256)(128)(2,1)} %param.31) | copy-start | bytes 292
  7.3 4.8 %copy-start.15 = (bf16[48]{0:T(256)(128)(2,1)S(1)}, bf16[48]{0:T(256)(128)(2,1)}, u32[]{:S(2)}) copy-start(bf16[48]{0:T(256)(128)(2,1)} %param.32) | copy-start | bytes 292
  7.3 4.9 %copy-start.16 = (bf16[48]{0:T(256)(128)(2,1)S(1)}, bf16[48]{0:T(256)(128)(2,1)}, u32[]{:S(2)}) copy-start(bf16[48]{0:T(256)(128)(2,1)} %param.36) | copy-start | bytes 292
  7.3 5.0 %copy-start.17 = (bf16[48]{0:T(256)(128)(2,1)S(1)}, bf16[48]{0:T(256)(128)(2,1)}, u32[]{:S(2)}) copy-start(bf16[48]{0:T(256)(128)(2,1)} %param.37) | copy-start | bytes 292
  7.3 5.1 %copy-start.18 = (bf16[48]{0:T(256)(128)(2,1)S(1)}, bf16[48]{0:T(256)(128)(2,1)}, u32[]{:S(2)}) copy-start(bf16[48]{0:T(256)(128)(2,1)} %param.38) | copy-start | bytes 292
  7.3 5.2 %copy-start.19 = (bf16[192]{0:T(256)(128)(2,1)S(1)}, bf16[192]{0:T(256)(128)(2,1)}, u32[]{:S(2)}) copy-start(bf16[192]{0:T(256)(128)(2,1)} %param.34) | copy-start | bytes 1156
  7.3 5.3 %copy-start.6 = (bf16[48,768]{1,0:T(8,128)(2,1)S(1)}, bf16[48,768]{1,0:T(8,128)(2,1)}, u32[]{:S(2)}) copy-start(bf16[48,768]{1,0:T(8,128)(2,1)} %param.24) | copy-start | bytes 221188
  7.3 5.3 %copy-start.7 = (bf16[48,768]{1,0:T(8,128)(2,1)S(1)}, bf16[48,768]{1,0:T(8,128)(2,1)}, u32[]{:S(2)}) copy-start(bf16[48,768]{1,0:T(8,128)(2,1)} %param.26) | copy-start | bytes 221188
  7.3 5.3 %copy-start.8 = (bf16[48,768]{1,0:T(8,128)(2,1)S(1)}, bf16[48,768]{1,0:T(8,128)(2,1)}, u32[]{:S(2)}) copy-start(bf16[48,768]{1,0:T(8,128)(2,1)} %param.27) | copy-start | bytes 221188
  7.3 116.7 %all-gather.2.cloned.1.call-start = ((), (), s32[]{:S(2)}) async-start(), calls=%async_computation.1 | async-start | bytes 11280384 | tf_op jit(solution)/shard_map/all_gather | solution.py:1283
  11.5 377.3 %reduce-scatter.2.cloned.1.call-start = ((), (), s32[]{:S(2)}) async-start(), calls=%async_computation.2 | async-start | bytes 11280384 | tf_op jit(solution)/shard_map/reduce_scatter | solution.py:1326
  13.4 68.3 %copy-start.10 = (s32[2,2048]{1,0:T(2,128)S(1)}, s32[2,2048]{1,0:T(2,128)}, u32[]{:S(2)}) copy-start(s32[2,2048]{1,0:T(2,128)} %param.21) | copy-start | bytes 49156
  13.4 69.1 %copy-start.21 = (s32[2,2]{1,0:T(2,128)S(1)}, s32[2,2]{1,0:T(2,128)}, u32[]{:S(2)}) copy-start(s32[2,2]{1,0:T(2,128)} %param.23) | copy-start | bytes 52
  79.9 44.1 %collective-permute-start = (bf16[1024,768]{1,0:T(8,128)(2,1)}, bf16[1024,768]{1,0:T(8,128)(2,1)S(1)}, u32[]{:S(2)}, u32[]{:S(2)}) collective-permute-start(bf16[1024,768]{1,0:T(8,128)(2,1)} %get-tuple-element.52), channel_id=1, source_target_pairs={{0,16},{16,0},{1,17},{17,1},{2,18},{18,2},{3,19},{19,3},{4,20},{20... | collective-permute-start | bytes 4718600 | tf_op jit(solution)/shard_map/ppermute | solution.py:1302
  124.0 1.2 copy-start.20
  232.5 68.7 %collective-permute-start.1 = (bf16[1024,768]{1,0:T(8,128)(2,1)}, bf16[1024,768]{1,0:T(8,128)(2,1)S(1)}, u32[]{:S(2)}, u32[]{:S(2)}) collective-permute-start(bf16[1024,768]{1,0:T(8,128)(2,1)} %get-tuple-element.57), channel_id=1, source_target_pairs={{0,16},{16,0},{1,17},{17,1},{2,18},{18,2},{3,19},{19,3},{4,20},{20... | collective-permute-start | bytes 4718600 | tf_op jit(solution)/shard_map/ppermute | solution.py:1323
  384.9 4.0 copy-start.2
  388.9 16.3 %collective-permute-start.2 = (bf16[48,6912]{1,0:T(8,128)(2,1)}, bf16[48,6912]{1,0:T(8,128)(2,1)}, u32[]{:S(2)}, u32[]{:S(2)}) collective-permute-start(bf16[48,6912]{1,0:T(8,128)(2,1)} %reduce-scatter.2.cloned.1.call-done), channel_id=1, source_target_pairs={{0,16},{16,0},{1,17},{17,1},{2,18},{18,2},{3,19},{19,3},{4,20},{20... | collective-permute-start | bytes 1990664 | tf_op jit(solution)/shard_map/ppermute | solution.py:1170
  407.4 3.3 copy-start.5
  407.4 5.3 %copy-start.1 = (s32[2,32,3]{1,0,2:T(2,128)S(1)}, s32[2,32,3]{1,0,2:T(2,128)}, u32[]{:S(2)}) copy-start(s32[2,32,3]{1,0,2:T(2,128)} %param.22) | copy-start | bytes 2308
  407.7 3.7 copy-start.4
  407.7 4.3 %copy-start.3 = (f32[48,768]{1,0:T(8,128)S(1)}, f32[48,768]{1,0:T(8,128)}, u32[]{:S(2)}) copy-start(f32[48,768]{1,0:T(8,128)} %get-tuple-element.150) | copy-start | bytes 442372
Sparse Core Ops, SparseCore 0:
  11.6 102.8 all-gather.1
  232.7 148.4 reduce-scatter.1

commit v4 on v3

--- a/solution.py
+++ b/solution.py
@@ -907,14 +907,17 @@
 
 
 OUT_B, GAIN_1, BIAS_1, OUTER_B, GAIN_2, BIAS_2, INNER_B = 2, 3, 4, 5, 6, 7, 8
-STEP_ROWS = 512
 SMALL_ROWS = 16
 
 
-def middle_kernel(
+def eights(values):
+    return jnp.sum(values.reshape(-1, 8, values.shape[-1]), axis=0)
+
+
+def middle_forward_kernel(
     chunks, side, weights_in, small, att, tokens, grad_own, grad_other,
-    out_keep, out_send, d_attn, d_att, d_weights, sums,
-    w, acc, act, slope, z_one, flow, rs_one, normed, normed_t, d_mlp, part, load_sem, store_sem,
+    out_keep, out_send, d_mlp, normed, z_one, rs_one, slope, d_weights, sums,
+    w, acc, act, flow, part, load_sem, store_sem,
 ):
     step, steps = pl.program_id(0), pl.num_programs(0)
     rows, width = att.shape
@@ -927,9 +930,9 @@
             weights_in.at[:, pl.ds(i * width, width)], w.at[i], load_sem.at[i]
         )
 
-    def store(i):
+    def store(c):
         return pltpu.make_async_copy(
-            w.at[i], d_weights.at[:, pl.ds(i * width, width)], store_sem.at[i]
+            w.at[1 + chunks + c], d_weights.at[:, pl.ds(c * width, width)], store_sem.at[c]
         )
 
     @pl.when(step == 0)
@@ -942,41 +945,27 @@
             acc[i] = jnp.zeros_like(acc[i])
             return 0
 
-        lax.fori_loop(0, count, clear, 0)
+        lax.fori_loop(0, chunks, clear, 0)
         load(0).wait()
 
     def vector(i):
         return small[i : i + 1, :]
 
-    def eights(values):
-        return jnp.sum(values.reshape(-1, 8, values.shape[-1]), axis=0)
-
     def add_sum(i, values):
         part[i] += eights(values)
 
-    def by_rows(body):
-        def one(r, _):
-            body(pl.ds(pl.multiple_of(r * STEP_ROWS, STEP_ROWS), STEP_ROWS))
-            return 0
-
-        lax.fori_loop(0, rows // STEP_ROWS, one, 0)
-
-    flow[...] = dot_f32(att[...], w[0])
-
-    def norm_one(r):
-        attn = flow[r, :] + vector(OUT_B)
-        resid = tokens[r, :].astype(f32) + attn
-        add_sum(INNER_B + chunks, resid * resid)
-        add_sum(INNER_B + chunks + 1, attn * attn)
-        centred = resid - row_mean(resid)
-        scale = lax.rsqrt(row_mean(centred * centred) + eps_norm)
-        z = centred * scale
-        z_one[r, :] = z
-        rs_one[r, :] = scale
-        normed[r, :] = (z * vector(GAIN_1) + vector(BIAS_1)).astype(bf16)
-
-    by_rows(norm_one)
-    normed_t[...] = normed[...].T
+    attn = dot_f32(att[...], w[0]) + vector(OUT_B)
+    resid = tokens[...].astype(f32) + attn
+    add_sum(INNER_B + chunks, resid * resid)
+    add_sum(INNER_B + chunks + 1, attn * attn)
+    centred = resid - row_mean(resid)
+    scale = lax.rsqrt(row_mean(centred * centred) + eps_norm)
+    z = centred * scale
+    rs_one[...] = scale
+    z_one[...] = z.astype(bf16)
+    full = z * vector(GAIN_1) + vector(BIAS_1)
+    flow[...] = full
+    normed[...] = full.astype(bf16)
 
     def inner(c, _):
         @pl.when(step == 0)
@@ -998,76 +987,131 @@
         for i in range(1 + chunks, count):
             load(i).wait()
 
-    flow[...] = dot_f32(act[0], w[1 + chunks])
-
-    def outer(c, _):
-        flow[...] += dot_f32(act[c], w[1 + chunks + c])
+    mlp = dot_f32(act[0], w[1 + chunks])
+    for c in range(1, chunks):
+        mlp = mlp + dot_f32(act[c], w[1 + chunks + c])
+    mlp = mlp + vector(OUTER_B)
+    add_sum(INNER_B + chunks + 2, mlp * mlp)
+    resid = flow[...] + mlp
+    centred = resid - row_mean(resid)
+    scale = lax.rsqrt(row_mean(centred * centred) + eps_norm)
+    z = centred * scale
+    result = (z * vector(GAIN_2) + vector(BIAS_2)).astype(bf16)
+
+    @pl.when(staying)
+    def _():
+        out_keep[...] = result
+
+    @pl.when(jnp.logical_not(staying))
+    def _():
+        out_send[...] = result
+
+    grad = jnp.where(staying, grad_own[...], grad_other[...]).astype(f32)
+    add_sum(GAIN_2, grad * z)
+    add_sum(BIAS_2, grad)
+    grad = grad * vector(GAIN_2)
+    low = (scale * (grad - row_mean(grad) - z * row_mean(grad * z))).astype(bf16)
+    add_sum(OUTER_B, low.astype(f32))
+    d_mlp[...] = low
+
+    def back(c, _):
+        acc[c] += dot_rows(act[c], d_mlp[...])
+
+        @pl.when(step == steps - 1)
+        def _():
+            w[1 + chunks + c] = acc[c].astype(bf16)
+            store(c).start()
+
         return 0
 
-    lax.fori_loop(1, chunks, outer, 0)
-
-    def norm_two(r):
-        mlp = flow[r, :] + vector(OUTER_B)
-        add_sum(INNER_B + chunks + 2, mlp * mlp)
-        resid = z_one[r, :] * vector(GAIN_1) + vector(BIAS_1) + mlp
-        centred = resid - row_mean(resid)
-        scale = lax.rsqrt(row_mean(centred * centred) + eps_norm)
-        z = centred * scale
-        result = (z * vector(GAIN_2) + vector(BIAS_2)).astype(bf16)
-
-        @pl.when(staying)
+    lax.fori_loop(0, chunks, back, 0)
+
+    @pl.when(step == steps - 1)
+    def _():
+        sums[...] = jnp.sum(part[...], axis=1)
+        for c in range(chunks):
+            store(c).wait()
+
+
+def middle_backward_kernel(
+    chunks, weights_in, small, sums_in, att, d_mlp, normed, z_one, rs_one, slope,
+    d_attn, d_att, d_weights, sums,
+    w, acc, d_pre, flow, part, load_sem, store_sem,
+):
+    step, steps = pl.program_id(0), pl.num_programs(0)
+    rows, width = att.shape
+    f32, bf16 = jnp.float32, jnp.bfloat16
+    count = 2 * chunks + 1
+
+    def load(i):
+        return pltpu.make_async_copy(
+            weights_in.at[:, pl.ds(i * width, width)], w.at[i], load_sem.at[i]
+        )
+
+    def store(i):
+        return pltpu.make_async_copy(
+            w.at[i], d_weights.at[:, pl.ds(i * width, width)], store_sem.at[i]
+        )
+
+    @pl.when(step == 0)
+    def _():
+        for c in range(chunks):
+            load(1 + chunks + c).start()
+            load(1 + c).start()
+        load(0).start()
+        part[...] = jnp.zeros_like(part)
+
+        def clear(i, _):
+            acc[i] = jnp.zeros_like(acc[i])
+            return 0
+
+        lax.fori_loop(0, chunks + 1, clear, 0)
+
+    def vector(i):
+        return small[i : i + 1, :]
+
+    def add_sum(i, values):
+        part[i] += eights(values)
+
+    turned = normed[...].T
+    flow[...] = d_mlp[...].astype(f32)
+
+    def back(c, _):
+        @pl.when(step == 0)
         def _():
-            out_keep[r, :] = result
-
-        @pl.when(jnp.logical_not(staying))
-        def _():
-            out_send[r, :] = result
-
-        grad = jnp.where(staying, grad_own[r, :], grad_other[r, :]).astype(f32)
-        add_sum(GAIN_2, grad * z)
-        add_sum(BIAS_2, grad)
-        grad = grad * vector(GAIN_2)
-        d_resid = scale * (grad - row_mean(grad) - z * row_mean(grad * z))
-        low = d_resid.astype(bf16)
-        add_sum(OUTER_B, low.astype(f32))
-        d_mlp[r, :] = low
-        flow[r, :] = d_resid
-
-    by_rows(norm_two)
-
-    def back(c, _):
+            load(1 + chunks + c).wait()
+            load(1 + c).wait()
+
         for n in range(width // 256):
             cols = slice(n * 256, n * 256 + 256)
             d_act = dot_nt(d_mlp[...], w[1 + chunks + c, cols, :])
-            d_pre = (slope[c, :, cols].astype(f32) * d_act).astype(bf16)
-            part[INNER_B + c, :, cols] += eights(d_pre.astype(f32))
-            slope[c, :, cols] = d_pre
-        acc[1 + chunks + c] += dot_rows(act[c], d_mlp[...])
-        acc[1 + c] += dot_f32(normed_t[...], slope[c])
-        flow[...] += dot_nt(slope[c], w[1 + c])
+            low = (slope[c, :, cols].astype(f32) * d_act).astype(bf16)
+            part[INNER_B + c, :, cols] += eights(low.astype(f32))
+            d_pre[:, cols] = low
+        acc[1 + c] += dot_f32(turned, d_pre[...])
+        flow[...] += dot_nt(d_pre[...], w[1 + c])
 
         @pl.when(step == steps - 1)
         def _():
-            for i in (1 + c, 1 + chunks + c):
-                w[i] = acc[i].astype(bf16)
-                store(i).start()
+            w[1 + c] = acc[1 + c].astype(bf16)
+            store(1 + c).start()
 
         return 0
 
     lax.fori_loop(0, chunks, back, 0)
 
-    def norm_one_back(r):
-        grad = flow[r, :]
-        z = z_one[r, :]
-        add_sum(GAIN_1, grad * z)
-        add_sum(BIAS_1, grad)
-        grad = grad * vector(GAIN_1)
-        d_resid = rs_one[r, :] * (grad - row_mean(grad) - z * row_mean(grad * z))
-        low = d_resid.astype(bf16)
-        add_sum(OUT_B, low.astype(f32))
-        d_attn[r, :] = low
-
-    by_rows(norm_one_back)
+    @pl.when(step == 0)
+    def _():
+        load(0).wait()
+
+    grad = flow[...]
+    z = z_one[...].astype(f32)
+    add_sum(GAIN_1, grad * z)
+    add_sum(BIAS_1, grad)
+    grad = grad * vector(GAIN_1)
+    low = (rs_one[...] * (grad - row_mean(grad) - z * row_mean(grad * z))).astype(bf16)
+    add_sum(OUT_B, low.astype(f32))
+    d_attn[...] = low
     acc[0] += dot_rows(att[...], d_attn[...])
     d_att[...] = dot_nt(d_attn[...], w[0]).astype(bf16)
 
@@ -1075,18 +1119,23 @@
     def _():
         w[0] = acc[0].astype(bf16)
         store(0).start()
-        sums[...] = jnp.sum(part[...], axis=1)
-        for i in range(count):
+        sums[...] = sums_in[...] + jnp.sum(part[...], axis=1)
+        for i in range(chunks + 1):
             store(i).wait()
 
 
-def middle(side, weights, small, att, tokens, grad_own, grad_other):
+def middle_parts(weights, small, tok_count, width):
+    chunks = (weights.shape[1] // width - 1) // 2
+    rows = 512
+    return chunks, rows, tok_count // rows
+
+
+def middle_forward(side, weights, small, att, tokens, grad_own, grad_other):
     tok_count, width = att.shape
-    chunks = (weights.shape[1] // width - 1) // 2
+    chunks, rows, steps = middle_parts(weights, small, tok_count, width)
     count = 2 * chunks + 1
-    rows = 512
     f32, bf16 = jnp.float32, jnp.bfloat16
-    half = tok_count // rows // 2
+    half = steps // 2
 
     def early(i):
         return jnp.minimum(i, half - 1)
@@ -1095,50 +1144,85 @@
         return jnp.maximum(i - half, 0)
 
     tile = pl.BlockSpec((rows, width), lambda i, s: (i, 0))
+    thin = pl.BlockSpec((rows, 1), lambda i, s: (i, 0))
+    deep = pl.BlockSpec((chunks, rows, width), lambda i, s: (0, i, 0))
     keep = pl.BlockSpec((rows, width), lambda i, s: (jnp.where(s[0] == 0, early(i), late(i)), 0))
     send = pl.BlockSpec((rows, width), lambda i, s: (jnp.where(s[0] == 0, late(i), early(i)), 0))
     fixed = pl.BlockSpec(small.shape, lambda i, s: (0, 0), pipeline_mode=pl.Buffered(1))
     anywhere = pl.BlockSpec(memory_space=pl.ANY)
     like = jax.ShapeDtypeStruct((tok_count, width), bf16)
     part = jax.ShapeDtypeStruct((tok_count // 2, width), bf16)
-    flops = 6 * tok_count * width * width * count
     return pl.pallas_call(
-        functools.partial(middle_kernel, chunks),
+        functools.partial(middle_forward_kernel, chunks),
         out_shape=(
-            part, part, like, like,
-            jax.ShapeDtypeStruct(weights.shape, bf16),
+            part, part, like, like, like,
+            jax.ShapeDtypeStruct((tok_count, 1), f32),
+            jax.ShapeDtypeStruct((chunks, tok_count, width), bf16),
+            jax.ShapeDtypeStruct((width, chunks * width), bf16),
             jax.ShapeDtypeStruct(small.shape, f32),
         ),
         grid_spec=pltpu.PrefetchScalarGridSpec(
-          num_scalar_prefetch=1,
-          grid=(tok_count // rows,),
-          in_specs=[anywhere, fixed, tile, tile, keep, send],
-          out_specs=(
-            keep, send, tile, tile, anywhere, pl.BlockSpec(small.shape, lambda i, s: (0, 0))
-          ),
-          scratch_shapes=[
-            pltpu.VMEM((count, width, width), bf16),
-            pltpu.VMEM((count, width, width), f32),
-            pltpu.VMEM((chunks, rows, width), bf16),
-            pltpu.VMEM((chunks, rows, width), bf16),
-            pltpu.VMEM((rows, width), f32),
-            pltpu.VMEM((rows, width), f32),
-            pltpu.VMEM((rows, 1), f32),
-            pltpu.VMEM((rows, width), bf16),
-            pltpu.VMEM((width, rows), bf16),
-            pltpu.VMEM((rows, width), bf16),
-            pltpu.VMEM((small.shape[0], 8, width), f32),
-            pltpu.SemaphoreType.DMA((count,)),
-            pltpu.SemaphoreType.DMA((count,)),
-          ],
+            num_scalar_prefetch=1,
+            grid=(steps,),
+            in_specs=[anywhere, fixed, tile, tile, keep, send],
+            out_specs=(keep, send, tile, tile, tile, thin, deep, anywhere, fixed),
+            scratch_shapes=[
+                pltpu.VMEM((count, width, width), bf16),
+                pltpu.VMEM((chunks, width, width), f32),
+                pltpu.VMEM((chunks, rows, width), bf16),
+                pltpu.VMEM((rows, width), f32),
+                pltpu.VMEM((small.shape[0], 8, width), f32),
+                pltpu.SemaphoreType.DMA((count,)),
+                pltpu.SemaphoreType.DMA((chunks,)),
+            ],
         ),
         compiler_params=pltpu.CompilerParams(vmem_limit_bytes=62 << 20),
         cost_estimate=pl.CostEstimate(
-            flops=2 * flops, transcendentals=tok_count * width * chunks,
-            bytes_accessed=12 * tok_count * width + 4 * weights.size,
+            flops=12 * tok_count * width * width * (count + 1) // 2,
+            transcendentals=tok_count * width * chunks,
+            bytes_accessed=30 * tok_count * width + 4 * weights.size,
         ),
-        name="middle",
+        name="middle_forward",
     )(side.reshape(1), weights, small, att, tokens, grad_own, grad_other)
+
+
+def middle_backward(weights, small, sums, att, d_mlp, normed, z_one, rs_one, slope):
+    tok_count, width = att.shape
+    chunks, rows, steps = middle_parts(weights, small, tok_count, width)
+    count = 2 * chunks + 1
+    f32, bf16 = jnp.float32, jnp.bfloat16
+    tile = pl.BlockSpec((rows, width), lambda i: (i, 0))
+    thin = pl.BlockSpec((rows, 1), lambda i: (i, 0))
+    deep = pl.BlockSpec((chunks, rows, width), lambda i: (0, i, 0))
+    fixed = pl.BlockSpec(small.shape, lambda i: (0, 0), pipeline_mode=pl.Buffered(1))
+    anywhere = pl.BlockSpec(memory_space=pl.ANY)
+    like = jax.ShapeDtypeStruct((tok_count, width), bf16)
+    return pl.pallas_call(
+        functools.partial(middle_backward_kernel, chunks),
+        grid=(steps,),
+        out_shape=(
+            like, like,
+            jax.ShapeDtypeStruct((width, (chunks + 1) * width), bf16),
+            jax.ShapeDtypeStruct(small.shape, f32),
+        ),
+        in_specs=[anywhere, fixed, fixed, tile, tile, tile, tile, thin, deep],
+        out_specs=(tile, tile, anywhere, fixed),
+        scratch_shapes=[
+            pltpu.VMEM((count, width, width), bf16),
+            pltpu.VMEM((chunks + 1, width, width), f32),
+            pltpu.VMEM((rows, width), bf16),
+            pltpu.VMEM((rows, width), f32),
+            pltpu.VMEM((small.shape[0], 8, width), f32),
+            pltpu.SemaphoreType.DMA((count,)),
+            pltpu.SemaphoreType.DMA((chunks + 1,)),
+        ],
+        compiler_params=pltpu.CompilerParams(vmem_limit_bytes=62 << 20),
+        cost_estimate=pl.CostEstimate(
+            flops=12 * tok_count * width * width * (count + 1) // 2, transcendentals=0,
+            bytes_accessed=30 * tok_count * width + 4 * weights.size,
+        ),
+        name="middle_backward",
+    )(weights, small, sums, att, d_mlp, normed, z_one, rs_one, slope)
 
 
 def contract_rows(left, right):
@@ -1316,22 +1400,25 @@
     q, k, v = (regroup.to_heads(split_rows(x)) for x in qkv)
     att, lse = attention_forward(q, k, v, plan)
     att_flat = regroup.from_heads(att).reshape(tok_count, width)
-    kept, sent, d_attn, d_att, d_second, sums = middle(
+    kept, sent, *saved, d_outer, sums = middle_forward(
         side, second, small, att_flat, flat_in, grad_own, grad_other
     )
     if paired:
         sent = lax.ppermute(sent, "seq", swap)
+    d_attn, d_att, d_second, sums = middle_backward(second, small, sums, att_flat, *saved)
 
     def scattered(values):
         return lax.psum_scatter(values, "fsdp", scatter_dimension=0, tiled=True)
 
+    d_outer = scattered(d_outer)
     d_second = scattered(d_second)
     dq, dk, dv = attention_backward(
         q, k, v, att, regroup.to_heads(split_rows(d_att)), lse, plan
     )
     dq, dk, dv = (regroup.from_heads(x).reshape(tok_count, width) for x in (dq, dk, dv))
     mine = lax.axis_index("fsdp")
-    dq, sent = lax.optimization_barrier((dq, sent))
+    dq, sent, d_outer = lax.optimization_barrier((dq, sent, d_outer))
+    d_outer = sum_seq(d_outer)
     if paired:
         d_query_w, d_key_w, d_value_w, sums, d_tokens_in = qkv_backward(
             turned_in, dq, dk, dv, turned_w, d_attn, sums, own
@@ -1355,12 +1442,12 @@
         out_tokens = regroup.scatter(split_rows(jnp.concatenate([kept, sent])))
     d_second = sum_seq(d_second)
     d_inner_w = (
-        d_second[:, width : (1 + chunks) * width]
+        d_second[:, width:]
         .reshape(own, chunks, width)
         .transpose(0, 2, 1)
         .reshape(own, -1)
     )
-    d_outer_w = d_second[:, (1 + chunks) * width :].reshape(own * chunks, width)
+    d_outer_w = d_outer.reshape(own * chunks, width)
     d_vec = lax.dynamic_slice_in_dim(sums, mine * own, own, 1)
     entry_total = tok_count * width * seq_count * fsdp_count
     rms_values = jnp.sqrt(

time: 420 us -> 418 us (level); the launches traced: 420 us -> 413 us
  Pallas kernels: 346 us -> 358 us
  starting transfers between devices: 15.4 us -> 3.99 us
  waiting for transfers between devices: 9.83 us -> 2.43 us
    ppermute x1, starting transfers between devices: 14 us -> 1.2 us  [shards(): sent = lax.ppermute(sent, 'seq', swap)]
    pallas_call x1 -> x2, Pallas kernels: 107 us -> 118 us  [the longest x1 65.4 us: middle_forward(): pl.pallas_call(functools.partial(middle_forward_kernel, chunks), out_shap...]
    ppermute x1 -> x2, waiting for transfers between devices: 9.76 us -> 2.35 us  [sum_seq(): other = lax.ppermute(values, 'seq', [(0, 1), (1, 0)])]
  transfers between devices with their start and end apart: 5 -> 7, of which waited for: 1 -> 2; matrix products, arithmetic and copies ran while one was open for 5% -> 6% of each run, Pallas kernels for 57% -> 71%
where the time goes in v4:
time: 418 us; the launch traced here: 413 us
  Pallas kernels  358 us (86%)
  local copies, waits for them, and re-layouts  21.1 us (5%)
  between operations  14.2 us (3%)
  other arithmetic  13 us (3%)
    pallas_call x1, Pallas kernels, qkv_backward(): pl.pallas_call(functools.partial(qkv_backward_kernel, bits), out_shape=(s...  80.1 us
    pallas_call x1, Pallas kernels, qkv_forward(): pl.pallas_call(functools.partial(qkv_forward_kernel, bits), out_shape=(ja...  66.5 us
    pallas_call x1, Pallas kernels, middle_forward(): pl.pallas_call(functools.partial(middle_forward_kernel, chunks), out_shap...  65.4 us
    pallas_call x1, Pallas kernels, attention_backward(): pl.pallas_call(functools.partial(backward_kernel, group), out_shape=(like...  57.3 us
    pallas_call x1, Pallas kernels, middle_backward(): pl.pallas_call(functools.partial(middle_backward_kernel, chunks), grid=(s...  52.9 us
    pallas_call x1, Pallas kernels, attention_forward(): pl.pallas_call(functools.partial(forward_kernel, group), out_shape=(jax.S...  36 us
  transfers between devices with their start and end apart: 7, of which 2 were waited for; matrix products, arithmetic and copies ran while one was open for 6% of the time, Pallas kernels for 71%

profile of v4, /device:TPU:0, one launch (start us, length us, event | category | flops | bytes accessed | tf_op | source)
XLA Modules:
  0.0 412.9 jit_solution(9312062651848010365)
XLA Ops:
  7.4 1.3 reshape.741
  8.6 1.4 copy.63
  10.0 0.6 copy.64
  10.6 0.9 pad_maximum_fusion
  11.6 0.1 copy.65
  12.2 0.1 reshape.743
  12.6 0.8 concatenate.13.own_in
  13.5 66.5 %qkv_forward.1 = (bf16[1024,768]{1,0:T(8,128)(2,1)}, bf16[2,4,256,768]{3,2,1,0:T(8,128)(2,1)}, bf16[2,4,768,256]{3,2,1,0:T(8,128)(2,1)}, bf16[2,4,256,768]{3,2,1...) custom-call(bf16[2,4,256,768]{3,2,1,0:T(8,128)(2,1)} %bitcast.83, ...), custom_call_target="tpu_custom_call" | custom-call | flops 21743271936 | bytes 25165824 | tf_op jit(solution)/shard_map/qkv_forward/pallas_call | solution.py:842
  79.9 0.9 collective-permute-start
  80.9 0.5 broadcast.492
  81.4 0.7 fusion.16
  82.2 0.2 slice_reduce_fusion
  82.5 0.2 convert_reduce_fusion
  83.1 0.2 multiply_reduce_fusion
  83.3 0.4 select_reduce_fusion
  83.8 0.7 pad_add_fusion
  84.5 0.6 fusion.14
  85.1 2.6 dynamic-slice_bitcast_fusion.grad_own
  87.8 0.5 and_select_fusion.1.n_ref
  88.3 0.6 compare_select_fusion.list_ref
  88.9 1.4 broadcast_in_dim.126.segc_ref
  90.2 36.0 %attention_forward.1 = (bf16[1,2048,768]{2,1,0:T(8,128)(2,1)}, f32[1,32,1,768]{3,2,1,0:T(1,128)}) custom-call(s32[1,32]{1,0:T(1,128)} %and_select_fusion.1.n_ref, s32[1,1024]{1,0:T(1,128)} %compare_select_fusion.list_ref, s32[1]{0:T(128)} %bitcast.15.total_ref, bf16[1,2048,768]{2,1,0:T(8,128)(2,1)} %bitcast.84, bf16[1,2048,768]{2,1,0:T(8,128)(2,1)} %bitcast.86, ...), custom_call_target="tpu_custom_call" | custom-call | flops 3221225472 | bytes 12582912 | tf_op jit(solution)/shard_map/attention_forward/pallas_call | solution.py:226
  126.3 1.1 copy-done.21
  127.4 65.4 %middle_forward.1 = (bf16[1024,768]{1,0:T(8,128)(2,1)}, bf16[1024,768]{1,0:T(8,128)(2,1)}, bf16[2048,768]{1,0:T(8,128)(2,1)}, bf16[2048,768]{1,0:T(8,128)(2,1)},...) custom-call(s32[1]{0:T(128)} %bitcast.side, ...), custom_call_target="tpu_custom_call" | custom-call | flops 72477573120 | bytes 68419584 | tf_op jit(solution)/shard_map/middle_forward/pallas_call | solution.py:1155
  192.9 0.3 reduce-scatter.5.cloned.1.call-start
  193.1 52.9 %middle_backward.1 = (bf16[2048,768]{1,0:T(8,128)(2,1)}, bf16[2048,768]{1,0:T(8,128)(2,1)}, bf16[768,3840]{1,0:T(8,128)(2,1)}, f32[16,768]{1,0:T(8,128)}) custom-call(bf16[768,6912]{1,0:T(8,128)(2,1)} %all-gather.2.cloned.1.call-done.weights_in, f32[16,768]{1,0:T(8,128)} %get-tuple-element.54.small, f32[16,768]{1,0:T(8,128)} %get-tuple-element.62.sums_in, ...), custom_call_target="tpu_custom_call" | custom-call | flops 72477573120 | bytes 68419584 | tf_op jit(solution)/shard_map/middle_backward/pallas_call | solution.py:1200
  246.0 1.2 collective-permute-start.1
  247.2 57.3 %attention_backward.1 = (bf16[1,2048,768]{2,1,0:T(8,128)(2,1)}, bf16[1,2048,768]{2,1,0:T(8,128)(2,1)}, bf16[1,2048,768]{2,1,0:T(8,128)(2,1)}) custom-call(s32[1,32]{1,0:T(1,128)} %and_select_fusion.1.n_ref, s32[1,1024]{1,0:T(1,128)} %compare_select_fusion.list_ref, s32[1]{0:T(128)} %bitcast.15.total_ref, bf16[1,2048,768]{2,1,0:T(8,128)(2,1)} %bitcast.85, ...), custom_call_target="tpu_custom_call" | custom-call | flops 8053063680 | bytes 25165824 | tf_op jit(solution)/shard_map/attention_backward/pallas_call | solution.py:350
  304.5 80.1 %qkv_backward.1 = (f32[48,768]{1,0:T(8,128)}, f32[48,768]{1,0:T(8,128)}, f32[48,768]{1,0:T(8,128)}, f32[16,768]{1,0:T(8,128)}, bf16[2,1024,768]{2,1,0:T(8,128)(2,1)}) custom-call(bf16[2,4,768,256]{3,2,1,0:T(8,128)(2,1)} %get-tuple-element.74.xt_in, bf16[2048,768]{1,0:T(8,128)(2,1)} %bitcast.94, bf16[2048,768]{1,0:T(8,128)(2,1)} %bitcast.95, ...), custom_call_target="tpu_custom_call" | custom-call | flops 48318382080 | bytes 25165824 | tf_op jit(solution)/shard_map/qkv_backward/pallas_call | solution.py:628
  384.8 3.9 broadcast_select_fusion
  388.7 2.2 broadcast_select_fusion.1
  390.9 0.6 collective-permute-done.3
  391.5 1.0 reshape.754
  392.5 1.4 collective-permute-start.2
  393.9 1.6 dynamic-slice_bitcast_fusion.2
  395.6 0.8 dynamic-slice_bitcast_fusion.1
  396.4 0.7 reshape.753
  397.1 0.9 slice_reduce_fusion.2
  397.9 0.5 multiply_sqrt_fusion
  398.5 1.8 collective-permute-done.2
  400.2 1.1 convert_add_fusion
  401.3 0.7 slice.58
  402.1 0.3 reshape.751
  402.4 0.7 copy.73
  403.1 1.3 copy.75
  404.4 0.7 copy.83
  405.1 0.7 copy.84
  405.7 0.7 copy.85
  (84 shorter events, 2.0 us)
Async XLA Ops:
  7.2 73.7 %copy-start = (s32[2,32,3]{1,0,2:T(2,128)S(1)}, s32[2,32,3]{1,0,2:T(2,128)}, u32[]{:S(2)}) copy-start(s32[2,32,3]{1,0,2:T(2,128)} %param.22) | copy-start | bytes 2308
  7.2 3.4 copy-start.10
  7.2 4.4 %copy-start.12 = (bf16[48]{0:T(256)(128)(2,1)S(1)}, bf16[48]{0:T(256)(128)(2,1)}, u32[]{:S(2)}) copy-start(bf16[48]{0:T(256)(128)(2,1)} %param.25) | copy-start | bytes 292
  7.2 4.5 %copy-start.13 = (bf16[48]{0:T(256)(128)(2,1)S(1)}, bf16[48]{0:T(256)(128)(2,1)}, u32[]{:S(2)}) copy-start(bf16[48]{0:T(256)(128)(2,1)} %param.28) | copy-start | bytes 292
  7.2 4.6 %copy-start.14 = (bf16[48]{0:T(256)(128)(2,1)S(1)}, bf16[48]{0:T(256)(128)(2,1)}, u32[]{:S(2)}) copy-start(bf16[48]{0:T(256)(128)(2,1)} %param.30) | copy-start | bytes 292
  7.3 4.7 %copy-start.15 = (bf16[48]{0:T(256)(128)(2,1)S(1)}, bf16[48]{0:T(256)(128)(2,1)}, u32[]{:S(2)}) copy-start(bf16[48]{0:T(256)(128)(2,1)} %param.31) | copy-start | bytes 292
  7.3 4.8 %copy-start.16 = (bf16[48]{0:T(256)(128)(2,1)S(1)}, bf16[48]{0:T(256)(128)(2,1)}, u32[]{:S(2)}) copy-start(bf16[48]{0:T(256)(128)(2,1)} %param.32) | copy-start | bytes 292
  7.3 4.9 %copy-start.17 = (bf16[192]{0:T(256)(128)(2,1)S(1)}, bf16[192]{0:T(256)(128)(2,1)}, u32[]{:S(2)}) copy-start(bf16[192]{0:T(256)(128)(2,1)} %param.34) | copy-start | bytes 1156
  7.3 5.0 %copy-start.18 = (bf16[48]{0:T(256)(128)(2,1)S(1)}, bf16[48]{0:T(256)(128)(2,1)}, u32[]{:S(2)}) copy-start(bf16[48]{0:T(256)(128)(2,1)} %param.36) | copy-start | bytes 292
  7.3 5.1 %copy-start.19 = (bf16[48]{0:T(256)(128)(2,1)S(1)}, bf16[48]{0:T(256)(128)(2,1)}, u32[]{:S(2)}) copy-start(bf16[48]{0:T(256)(128)(2,1)} %param.37) | copy-start | bytes 292
  7.3 5.2 %copy-start.20 = (bf16[48]{0:T(256)(128)(2,1)S(1)}, bf16[48]{0:T(256)(128)(2,1)}, u32[]{:S(2)}) copy-start(bf16[48]{0:T(256)(128)(2,1)} %param.38) | copy-start | bytes 292
  7.3 5.3 %copy-start.9 = (bf16[48,768]{1,0:T(8,128)(2,1)S(1)}, bf16[48,768]{1,0:T(8,128)(2,1)}, u32[]{:S(2)}) copy-start(bf16[48,768]{1,0:T(8,128)(2,1)} %param.27) | copy-start | bytes 221188
  7.3 5.3 %copy-start.8 = (bf16[48,768]{1,0:T(8,128)(2,1)S(1)}, bf16[48,768]{1,0:T(8,128)(2,1)}, u32[]{:S(2)}) copy-start(bf16[48,768]{1,0:T(8,128)(2,1)} %param.26) | copy-start | bytes 221188
  7.3 5.3 %copy-start.7 = (bf16[48,768]{1,0:T(8,128)(2,1)S(1)}, bf16[48,768]{1,0:T(8,128)(2,1)}, u32[]{:S(2)}) copy-start(bf16[48,768]{1,0:T(8,128)(2,1)} %param.24) | copy-start | bytes 221188
  7.3 118.9 %all-gather.2.cloned.1.call-start = ((), (), s32[]{:S(2)}) async-start(), calls=%async_computation.2 | async-start | bytes 11280384 | tf_op jit(solution)/shard_map/all_gather | solution.py:1367
  11.5 293.0 %reduce-scatter.3.cloned.1.call-start = ((), (), s32[]{:S(2)}) async-start(), calls=%async_computation.3 | async-start | bytes 5013504 | tf_op jit(solution)/shard_map/reduce_scatter | solution.py:1411
  13.5 68.0 %copy-start.11 = (s32[2,2048]{1,0:T(2,128)S(1)}, s32[2,2048]{1,0:T(2,128)}, u32[]{:S(2)}) copy-start(s32[2,2048]{1,0:T(2,128)} %param.21) | copy-start | bytes 49156
  13.5 68.7 %copy-start.22 = (s32[2,2]{1,0:T(2,128)S(1)}, s32[2,2]{1,0:T(2,128)}, u32[]{:S(2)}) copy-start(s32[2,2]{1,0:T(2,128)} %param.23) | copy-start | bytes 52
  79.9 46.3 %collective-permute-start = (bf16[1024,768]{1,0:T(8,128)(2,1)}, bf16[1024,768]{1,0:T(8,128)(2,1)S(1)}, u32[]{:S(2)}, u32[]{:S(2)}) collective-permute-start(bf16[1024,768]{1,0:T(8,128)(2,1)} %get-tuple-element.60), channel_id=1, source_target_pairs={{0,16},{16,0},{1,17},{17,1},{2,18},{18,2},{3,19},{19,3},{4,20},{20... | collective-permute-start | bytes 4718600 | tf_op jit(solution)/shard_map/ppermute | solution.py:1386
  126.3 1.1 copy-start.21
  192.9 199.6 %reduce-scatter.5.cloned.1.call-start = ((), (), s32[]{:S(2)}) async-start(), calls=%async_computation.4 | async-start | bytes 6266880 | tf_op jit(solution)/shard_map/reduce_scatter | solution.py:1411
  246.0 58.5 %collective-permute-start.1 = (bf16[1024,768]{1,0:T(8,128)(2,1)}, bf16[1024,768]{1,0:T(8,128)(2,1)S(1)}, u32[]{:S(2)}, u32[]{:S(2)}) collective-permute-start(bf16[1024,768]{1,0:T(8,128)(2,1)} %get-tuple-element.71), channel_id=1, source_target_pairs={{0,16},{16,0},{1,17},{17,1},{2,18},{18,2},{3,19},{19,3},{4,20},{20... | collective-permute-start | bytes 4718600 | tf_op jit(solution)/shard_map/ppermute | solution.py:1407
  304.5 80.2 %copy-start.3 = (bf16[48,3072]{1,0:T(8,128)(2,1)S(1)}, bf16[48,3072]{1,0:T(8,128)(2,1)}, u32[]{:S(2)}) copy-start(bf16[48,3072]{1,0:T(8,128)(2,1)} %reduce-scatter.3.cloned.1.call-done) | copy-start | bytes 884740
  384.7 6.8 %collective-permute-start.3 = (bf16[48,3072]{1,0:T(8,128)(2,1)S(1)}, bf16[48,3072]{1,0:T(8,128)(2,1)S(1)}, u32[]{:S(2)}, u32[]{:S(2)}) collective-permute-start(bf16[48,3072]{1,0:T(8,128)(2,1)S(1)} %copy-done.3), channel_id=1, source_target_pairs={{0,16},{16,0},{1,17},{17,1},{2,18},{18,2},{3,19},{19,3},{4,20},{20... | collective-permute-start | bytes 884744 | tf_op jit(solution)/shard_map/ppermute | solution.py:1254
  384.8 4.0 copy-start.2
  392.5 7.7 %collective-permute-start.2 = (bf16[48,3840]{1,0:T(8,128)(2,1)}, bf16[48,3840]{1,0:T(8,128)(2,1)S(1)}, u32[]{:S(2)}, u32[]{:S(2)}) collective-permute-start(bf16[48,3840]{1,0:T(8,128)(2,1)} %reduce-scatter.5.cloned.1.call-done), channel_id=1, source_target_pairs={{0,16},{16,0},{1,17},{17,1},{2,18},{18,2},{3,19},{19,3},{4,20},{20... | collective-permute-start | bytes 1105928 | tf_op jit(solution)/shard_map/ppermute | solution.py:1254
  402.0 2.4 copy-start.6
  402.0 4.4 %copy-start.1 = (s32[2,32,3]{1,0,2:T(2,128)S(1)}, s32[2,32,3]{1,0,2:T(2,128)}, u32[]{:S(2)}) copy-start(s32[2,32,3]{1,0,2:T(2,128)} %param.22) | copy-start | bytes 2308
  402.1 3.0 copy-start.5
  402.1 3.7 copy-start.4
Sparse Core Ops, SparseCore 0:
  11.7 102.9 all-gather.1
  193.0 83.6 reduce-scatter.2
  281.1 91.2 reduce-scatter.4

commit v5 on v4

--- a/solution.py
+++ b/solution.py
@@ -11,6 +11,7 @@
 HD = 64
 BLK = 64
 CHUNK = 4
+ITEMS = 3
 NEG = -1e30
 
 
@@ -104,6 +105,16 @@
     )
 
 
+def fetch(row, pairs, sem):
+    loads = [
+        pltpu.make_async_copy(src.at[pl.ds(row, 1)], dst, sem.at[i])
+        for i, (src, dst) in enumerate(pairs)
+    ]
+    for load in loads:
+        load.start()
+    return loads
+
+
 def next_item(n_ref, row, nb, a, c):
     more = c + 1 < n_ref[row, a]
     following = jnp.where(more, a, jnp.minimum(a + 1, nb - 1))
@@ -113,44 +124,59 @@
 def run_items(n_ref, total_ref, row, nb, ready, item, finish):
     total = total_ref[row]
 
-    def following(a, c):
-        return next_item(n_ref, row, nb, a, c)
+    def walk(a, c):
+        places = [(a, c)]
+        for _ in range(2 * ITEMS - 1):
+            places.append(next_item(n_ref, row, nb, *places[-1]))
+        return places
 
     def turn(i, carry):
-        before, between, a, c = carry
-        base = lax.rem(i, 2) * 2
-        finish(before)
-        finish(between)
-        a_two, c_two = following(a, c)
-        a_three, c_three = following(a_two, c_two)
-        a_four, c_four = following(a_three, c_three)
-        ready(a_three, 2 - base)
-        ready(a_four, 3 - base)
-        real = 2 * i + 1 < total
-        a_two, c_two = jnp.where(real, a_two, a), jnp.where(real, c_two, c + 1)
-        item(base, a, c, True)
-        item(base + 1, a_two, c_two, real)
-        return a, a_two, a_three, c_three
-
-    ready(0, 0)
-    ready(following(0, 0)[0], 1)
-    before, between, _, _ = lax.fori_loop(0, (total + 1) // 2, turn, (0, 0, 0, 0))
-    finish(before)
-    finish(between)
-
-
-def forward_kernel(group, n_ref, list_ref, total_ref, q_ref, k_ref, v_ref, segc_ref, segr_ref,
-                   o_ref, lse_ref, vt_ref, qst_ref, m_ref, l_ref, acc_ref):
+        before, a, c = carry
+        base = lax.rem(i, 2) * ITEMS
+        for past in before:
+            finish(past)
+        places = walk(a, c)
+        for k in range(ITEMS):
+            ready(places[ITEMS + k][0], ITEMS - base + k)
+        here = [places[0]]
+        item(base, *here[0], True)
+        for k in range(1, ITEMS):
+            real = ITEMS * i + k < total
+            here.append(
+                (
+                    jnp.where(real, places[k][0], here[-1][0]),
+                    jnp.where(real, places[k][1], here[-1][1] + 1),
+                )
+            )
+            item(base + k, *here[k], real)
+        return (tuple(place[0] for place in here), *places[ITEMS])
+
+    for k, place in enumerate(walk(0, 0)[:ITEMS]):
+        ready(place[0], k)
+    before, _, _ = lax.fori_loop(
+        0, (total + ITEMS - 1) // ITEMS, turn, ((0,) * ITEMS, 0, 0)
+    )
+    for past in before:
+        finish(past)
+
+
+def forward_kernel(group, n_ref, list_ref, total_ref, q_in, k_in, v_in, segc_ref, segr_ref,
+                   o_ref, lse_ref, q_ref, k_ref, v_ref, vt_ref, qst_ref, m_ref, l_ref, acc_ref,
+                   sem):
     row = pl.program_id(0)
     width = q_ref.shape[2]
     nb = q_ref.shape[1] // BLK
     groups, halves = width // group, group // 128
     tiles = width // 128
-    turn_all(v_ref, vt_ref, nb, width)
+    loads = fetch(row, ((v_in, v_ref), (q_in, q_ref), (k_in, k_ref)), sem)
     qst_ref[...] = jnp.zeros_like(qst_ref)
     l_ref[...] = jnp.ones_like(l_ref)
     acc_ref[...] = jnp.zeros_like(acc_ref)
     m_ref[...] = jnp.zeros_like(m_ref)
+    loads[0].wait()
+    turn_all(v_ref, vt_ref, nb, width)
+    for load in loads[1:]:
+        load.wait()
 
     def ready(a, slot):
         start = pl.multiple_of(a * BLK, BLK)
@@ -162,7 +188,7 @@
             )
 
     def finish(a):
-        even = lax.rem(a, 2)
+        even = lax.rem(a, ITEMS)
         start = pl.multiple_of(a * BLK, BLK)
         for t in range(tiles):
             lanes = slice(t * 128, t * 128 + 128)
@@ -174,7 +200,7 @@
 
     def item(slot, a, c, real):
         ids, safe = chunk_ids(list_ref, row, a * nb + c * CHUNK, nb, real)
-        even = lax.rem(a, 2)
+        even = lax.rem(a, ITEMS)
         allowed = block_rows(segc_ref, ids, slice(0, 128)) == segr_ref[0, a]
         first = c == 0
         for g in range(groups):
@@ -223,6 +249,8 @@
     tiles = width // 128
     pairs = rows * full_len * full_len // 4 * width
     args = (q, k, v, seg_cols, seg_rows)
+    anywhere = pl.BlockSpec(memory_space=pl.ANY)
+    stretch = pltpu.VMEM((1, full_len, width), jnp.bfloat16)
     return pl.pallas_call(
         functools.partial(forward_kernel, group),
         out_shape=(
@@ -232,14 +260,16 @@
         grid_spec=pltpu.PrefetchScalarGridSpec(
             num_scalar_prefetch=3,
             grid=(rows,),
-            in_specs=[one_spec(x.shape) for x in args],
+            in_specs=[anywhere] * 3 + [one_spec(x.shape) for x in args[3:]],
             out_specs=(one_spec((rows, full_len, width)), one_spec((rows, nb, 1, width))),
             scratch_shapes=[
+                stretch, stretch, stretch,
                 pltpu.VMEM((nb, width, 128), jnp.bfloat16),
-                pltpu.VMEM((4, width // group, group, group), jnp.bfloat16),
-                pltpu.VMEM((2, tiles, 1, 128), jnp.float32),
-                pltpu.VMEM((2, tiles, 1, 128), jnp.float32),
-                pltpu.VMEM((2, tiles, HD, 128), jnp.float32),
+                pltpu.VMEM((2 * ITEMS, width // group, group, group), jnp.bfloat16),
+                pltpu.VMEM((ITEMS, tiles, 1, 128), jnp.float32),
+                pltpu.VMEM((ITEMS, tiles, 1, 128), jnp.float32),
+                pltpu.VMEM((ITEMS, tiles, HD, 128), jnp.float32),
+                pltpu.SemaphoreType.DMA((3,)),
             ],
         ),
         compiler_params=pltpu.CompilerParams(vmem_limit_bytes=62 << 20),
@@ -250,18 +280,28 @@
     )(*tables, *args)
 
 
-def backward_kernel(group, n_ref, list_ref, total_ref, q_ref, k_ref, v_ref, o_ref, do_ref,
-                    lse_ref, segc_ref, segr_ref, dq_ref, dk_ref, dv_ref,
-                    kt_ref, qst_ref, qs_ref, dost_ref, dos_ref, delta_ref, acc_ref,
-                    dk_acc, dv_acc):
+def backward_kernel(group, n_ref, list_ref, total_ref, q_in, k_in, v_in, o_in, do_in,
+                    lse_ref, segc_ref, segr_ref, dq_out, dk_out, dv_out,
+                    q_ref, k_ref, v_ref, o_ref, do_ref, dq_ref, kt_ref, qst_ref, qs_ref, dost_ref, dos_ref, delta_ref, acc_ref,
+                    dk_acc, dv_acc, sem, out_sem):
     row = pl.program_id(0)
     full_len, width = q_ref.shape[1], q_ref.shape[2]
     nb = full_len // BLK
     groups, halves = width // group, group // 128
     tiles = width // 128
+    loads = fetch(
+        row,
+        ((k_in, k_ref), (q_in, q_ref), (do_in, do_ref), (o_in, o_ref), (v_in, v_ref)),
+        sem,
+    )
+    for ref in (qst_ref, qs_ref, dost_ref, dos_ref, acc_ref):
+        ref[...] = jnp.zeros_like(ref)
+    loads[0].wait()
     turn_all(k_ref, kt_ref, nb, width)
-    for ref in (qst_ref, qs_ref, dost_ref, dos_ref, dk_acc, dv_acc, acc_ref):
+    for ref in (dk_acc, dv_acc):
         ref[...] = jnp.zeros_like(ref)
+    for load in loads[1:]:
+        load.wait()
     low = lane_low(1)
 
     def ready(a, slot):
@@ -288,7 +328,7 @@
             )
 
     def finish(a):
-        even = lax.rem(a, 2)
+        even = lax.rem(a, ITEMS)
         start = pl.multiple_of(a * BLK, BLK)
         for t in range(tiles):
             dq_ref[0, pl.ds(start, BLK), t * 128 : t * 128 + 128] = (
@@ -297,7 +337,7 @@
 
     def item(slot, a, c, real):
         ids, safe = chunk_ids(list_ref, row, a * nb + c * CHUNK, nb, real)
-        even = lax.rem(a, 2)
+        even = lax.rem(a, ITEMS)
         allowed = block_rows(segc_ref, ids, slice(0, 128)) == segr_ref[0, a]
         first = c == 0
         for g in range(groups):
@@ -329,13 +369,22 @@
 
     run_items(n_ref, total_ref, row, nb, ready, item, finish)
 
-    def flush(a, _):
-        where = pl.ds(pl.multiple_of(a * BLK, BLK), BLK)
-        dk_ref[0, where, :] = dk_acc[where, :].astype(jnp.bfloat16)
-        dv_ref[0, where, :] = dv_acc[where, :].astype(jnp.bfloat16)
-        return 0
-
-    lax.fori_loop(0, nb, flush, 0, unroll=2)
+    def leave(i, src, dst):
+        return pltpu.make_async_copy(src, dst.at[pl.ds(row, 1)], out_sem.at[i])
+
+    leaving = [leave(0, dq_ref, dq_out)]
+    leaving[0].start()
+    for i, (total, low, out) in enumerate(((dk_acc, q_ref, dk_out), (dv_acc, o_ref, dv_out))):
+        def flush(a, _):
+            where = pl.ds(pl.multiple_of(a * BLK, BLK), BLK)
+            low[0, where, :] = total[where, :].astype(jnp.bfloat16)
+            return 0
+
+        lax.fori_loop(0, nb, flush, 0, unroll=2)
+        leaving.append(leave(1 + i, low, out))
+        leaving[-1].start()
+    for copy in leaving:
+        copy.wait()
 
 
 def attention_backward(q, k, v, o, do, lse, plan):
@@ -345,23 +394,28 @@
     tiles, groups = width // 128, width // group
     pairs = rows * full_len * full_len // 4 * width
     args = (q, k, v, o, do, lse, seg_cols, seg_rows)
+    anywhere = pl.BlockSpec(memory_space=pl.ANY)
+    stretch = pltpu.VMEM((1, full_len, width), jnp.bfloat16)
     like = jax.ShapeDtypeStruct((rows, full_len, width), jnp.bfloat16)
-    square = pltpu.VMEM((4, groups, group, group), jnp.bfloat16)
+    square = pltpu.VMEM((2 * ITEMS, groups, group, group), jnp.bfloat16)
     return pl.pallas_call(
         functools.partial(backward_kernel, group),
         out_shape=(like, like, like),
         grid_spec=pltpu.PrefetchScalarGridSpec(
             num_scalar_prefetch=3,
             grid=(rows,),
-            in_specs=[one_spec(x.shape) for x in args],
-            out_specs=tuple(one_spec(like.shape) for _ in range(3)),
+            in_specs=[anywhere] * 5 + [one_spec(x.shape) for x in args[5:]],
+            out_specs=(anywhere,) * 3,
             scratch_shapes=[
+                stretch, stretch, stretch, stretch, stretch, stretch,
                 pltpu.VMEM((nb, width, 128), jnp.bfloat16),
                 square, square, square, square,
-                pltpu.VMEM((4, tiles, 1, 128), jnp.float32),
-                pltpu.VMEM((2, tiles, HD, 128), jnp.float32),
+                pltpu.VMEM((2 * ITEMS, tiles, 1, 128), jnp.float32),
+                pltpu.VMEM((ITEMS, tiles, HD, 128), jnp.float32),
                 pltpu.VMEM((full_len, width), jnp.float32),
                 pltpu.VMEM((full_len, width), jnp.float32),
+                pltpu.SemaphoreType.DMA((5,)),
+                pltpu.SemaphoreType.DMA((3,)),
             ],
         ),
         compiler_params=pltpu.CompilerParams(vmem_limit_bytes=62 << 20),
@@ -1148,6 +1202,9 @@
     deep = pl.BlockSpec((chunks, rows, width), lambda i, s: (0, i, 0))
     keep = pl.BlockSpec((rows, width), lambda i, s: (jnp.where(s[0] == 0, early(i), late(i)), 0))
     send = pl.BlockSpec((rows, width), lambda i, s: (jnp.where(s[0] == 0, late(i), early(i)), 0))
+    own = pl.BlockSpec(
+        (None, rows, width), lambda i, s: (s[0], jnp.where(s[0] == 0, early(i), late(i)), 0)
+    )
     fixed = pl.BlockSpec(small.shape, lambda i, s: (0, 0), pipeline_mode=pl.Buffered(1))
     anywhere = pl.BlockSpec(memory_space=pl.ANY)
     like = jax.ShapeDtypeStruct((tok_count, width), bf16)
@@ -1164,7 +1221,7 @@
         grid_spec=pltpu.PrefetchScalarGridSpec(
             num_scalar_prefetch=1,
             grid=(steps,),
-            in_specs=[anywhere, fixed, tile, tile, keep, send],
+            in_specs=[anywhere, fixed, tile, tile, own, send],
             out_specs=(keep, send, tile, tile, tile, thin, deep, anywhere, fixed),
             scratch_shapes=[
                 pltpu.VMEM((count, width, width), bf16),
@@ -1384,7 +1441,7 @@
             tokens_in, first, out_grad
         )
         grad_other = lax.ppermute(leaving, "seq", swap)
-        grad_own = lax.dynamic_index_in_dim(out_grad, side, 0, keepdims=False)
+        grad_own = out_grad
     else:
         first = lax.all_gather(first, "fsdp", axis=0, tiled=True)
         small = first[:, width : width + SMALL_ROWS].astype(jnp.float32).T
@@ -1396,7 +1453,8 @@
             for i in range(3)
         ]
         flat_grad = regroup.gather(out_grad).reshape(tok_count, width)
-        grad_own, grad_other = flat_grad[: tok_count // 2], flat_grad[tok_count // 2 :]
+        grad_own = flat_grad.reshape(2, tok_count // 2, width)
+        grad_other = grad_own[1]
     q, k, v = (regroup.to_heads(split_rows(x)) for x in qkv)
     att, lse = attention_forward(q, k, v, plan)
     att_flat = regroup.from_heads(att).reshape(tok_count, width)

time: 418 us -> 410 us (0.981); the launches traced: 413 us -> 410 us
    pallas_call x1, Pallas kernels: 80.1 us -> 70.4 us  [qkv_backward(): pl.pallas_call(functools.partial(qkv_backward_kernel, bits), out_shape=(s...]
    pallas_call x1, Pallas kernels: 57.3 us -> 64.1 us  [attention_backward(): pl.pallas_call(functools.partial(backward_kernel, group), out_shape=(like...]
  transfers between devices with their start and end apart: 7 -> 7, of which waited for: 2 -> 1; matrix products, arithmetic and copies ran while one was open for 6% -> 5% of each run, Pallas kernels for 71% -> 72%
where the time goes in v5:
time: 410 us
  Pallas kernels  359 us (88%)
  local copies, waits for them, and re-layouts  18.5 us (5%)
  between operations  14.2 us (3%)
  other arithmetic  13 us (3%)
    pallas_call x1, Pallas kernels, qkv_backward(): pl.pallas_call(functools.partial(qkv_backward_kernel, bits), out_shape=(s...  70.4 us
    pallas_call x1, Pallas kernels, qkv_forward(): pl.pallas_call(functools.partial(qkv_forward_kernel, bits), out_shape=(ja...  66.5 us
    pallas_call x1, Pallas kernels, middle_forward(): pl.pallas_call(functools.partial(middle_forward_kernel, chunks), out_shap...  65.4 us
    pallas_call x1, Pallas kernels, attention_backward(): pl.pallas_call(functools.partial(backward_kernel, group), out_shape=(like...  64.1 us
    pallas_call x1, Pallas kernels, middle_backward(): pl.pallas_call(functools.partial(middle_backward_kernel, chunks), grid=(s...  53 us
    pallas_call x1, Pallas kernels, attention_forward(): pl.pallas_call(functools.partial(forward_kernel, group), out_shape=(jax.S...  39.4 us
  transfers between devices with their start and end apart: 7, of which 1 were waited for; matrix products, arithmetic and copies ran while one was open for 5% of the time, Pallas kernels for 72%

profile of v5, /device:TPU:0, one launch (start us, length us, event | category | flops | bytes accessed | tf_op | source)
XLA Modules:
  0.0 410.1 jit_solution(9809454781255625175)
XLA Ops:
  7.4 1.3 reshape.741
  8.6 1.4 copy.63
  10.0 0.6 copy.64
  10.6 0.9 pad_maximum_fusion
  11.6 0.1 copy.65
  12.0 0.1 copy.69
  12.2 0.1 reshape.743
  12.3 0.1 copy.70
  12.6 0.8 concatenate.13.own_in
  13.5 66.5 %qkv_forward.1 = (bf16[1024,768]{1,0:T(8,128)(2,1)}, bf16[2,4,256,768]{3,2,1,0:T(8,128)(2,1)}, bf16[2,4,768,256]{3,2,1,0:T(8,128)(2,1)}, bf16[2,4,256,768]{3,2,1...) custom-call(bf16[2,4,256,768]{3,2,1,0:T(8,128)(2,1)} %bitcast.81, ...), custom_call_target="tpu_custom_call" | custom-call | flops 21743271936 | bytes 25165824 | tf_op jit(solution)/shard_map/qkv_forward/pallas_call | solution.py:896
  79.9 0.9 collective-permute-start
  80.9 0.5 broadcast.492
  81.4 0.7 fusion.16
  82.2 0.2 slice_reduce_fusion
  82.5 0.2 convert_reduce_fusion
  83.1 0.2 multiply_reduce_fusion
  83.3 0.4 select_reduce_fusion
  83.8 0.7 pad_add_fusion
  84.5 0.6 fusion.14
  85.1 0.5 and_select_fusion.1.n_ref
  85.6 0.6 compare_select_fusion.list_ref
  86.2 1.4 broadcast_in_dim.126.segc_ref
  87.6 39.4 %attention_forward.1 = (bf16[1,2048,768]{2,1,0:T(8,128)(2,1)}, f32[1,32,1,768]{3,2,1,0:T(1,128)}) custom-call(s32[1,32]{1,0:T(1,128)} %and_select_fusion.1.n_ref, s32[1,1024]{1,0:T(1,128)} %compare_select_fusion.list_ref, s32[1]{0:T(128)} %bitcast.15.total_ref, bf16[1,2048,768]{2,1,0:T(8,128)(2,1)} %bitcast.82, bf16[1,2048,768]{2,1,0:T(8,128)(2,1)} %bitcast.84, ...), custom_call_target="tpu_custom_call" | custom-call | flops 3221225472 | bytes 12582912 | tf_op jit(solution)/shard_map/attention_forward/pallas_call | solution.py:254
  127.1 1.1 copy-done.21
  128.2 65.4 %middle_forward.1 = (bf16[1024,768]{1,0:T(8,128)(2,1)}, bf16[1024,768]{1,0:T(8,128)(2,1)}, bf16[2048,768]{1,0:T(8,128)(2,1)}, bf16[2048,768]{1,0:T(8,128)(2,1)},...) custom-call(s32[1]{0:T(128)} %bitcast.side, ...), custom_call_target="tpu_custom_call" | custom-call | flops 72477573120 | bytes 68419584 | tf_op jit(solution)/shard_map/middle_forward/pallas_call | solution.py:1212
  193.7 0.3 reduce-scatter.5.cloned.1.call-start
  193.9 53.0 %middle_backward.1 = (bf16[2048,768]{1,0:T(8,128)(2,1)}, bf16[2048,768]{1,0:T(8,128)(2,1)}, bf16[768,3840]{1,0:T(8,128)(2,1)}, f32[16,768]{1,0:T(8,128)}) custom-call(bf16[768,6912]{1,0:T(8,128)(2,1)} %all-gather.2.cloned.1.call-done.weights_in, f32[16,768]{1,0:T(8,128)} %get-tuple-element.54.small, f32[16,768]{1,0:T(8,128)} %get-tuple-element.62.sums_in, ...), custom_call_target="tpu_custom_call" | custom-call | flops 72477573120 | bytes 68419584 | tf_op jit(solution)/shard_map/middle_backward/pallas_call | solution.py:1257
  247.1 64.1 %attention_backward.1 = (bf16[1,2048,768]{2,1,0:T(8,128)(2,1)}, bf16[1,2048,768]{2,1,0:T(8,128)(2,1)}, bf16[1,2048,768]{2,1,0:T(8,128)(2,1)}) custom-call(s32[1,32]{1,0:T(1,128)} %and_select_fusion.1.n_ref, s32[1,1024]{1,0:T(1,128)} %compare_select_fusion.list_ref, s32[1]{0:T(128)} %bitcast.15.total_ref, bf16[1,2048,768]{2,1,0:T(8,128)(2,1)} %bitcast.83, ...), custom_call_target="tpu_custom_call" | custom-call | flops 8053063680 | bytes 25165824 | tf_op jit(solution)/shard_map/attention_backward/pallas_call | solution.py:401
  311.3 70.4 %qkv_backward.1 = (f32[48,768]{1,0:T(8,128)}, f32[48,768]{1,0:T(8,128)}, f32[48,768]{1,0:T(8,128)}, f32[16,768]{1,0:T(8,128)}, bf16[2,1024,768]{2,1,0:T(8,128)(2,1)}) custom-call(bf16[2,4,768,256]{3,2,1,0:T(8,128)(2,1)} %get-tuple-element.74.xt_in, bf16[2048,768]{1,0:T(8,128)(2,1)} %bitcast.92, bf16[2048,768]{1,0:T(8,128)(2,1)} %bitcast.93, ...), custom_call_target="tpu_custom_call" | custom-call | flops 48318382080 | bytes 25165824 | tf_op jit(solution)/shard_map/qkv_backward/pallas_call | solution.py:682
  381.7 0.7 collective-permute-start.3
  382.4 3.9 broadcast_select_fusion
  386.3 2.2 broadcast_select_fusion.1
  388.6 1.0 reshape.754
  389.6 1.4 collective-permute-start.2
  391.0 1.6 dynamic-slice_bitcast_fusion.1
  392.6 0.8 dynamic-slice_bitcast_fusion
  393.5 0.7 reshape.753
  394.1 0.9 slice_reduce_fusion.2
  395.0 0.5 multiply_sqrt_fusion
  395.5 1.9 collective-permute-done.2
  397.4 1.1 convert_add_fusion
  398.5 0.7 slice.58
  399.3 0.3 reshape.751
  399.6 0.7 copy.73
  400.3 1.3 copy.75
  401.6 0.7 copy.83
  402.2 0.7 copy.84
  402.9 0.7 copy.85
  (83 shorter events, 1.8 us)
Async XLA Ops:
  7.2 73.7 %copy-start = (s32[2,32,3]{1,0,2:T(2,128)S(1)}, s32[2,32,3]{1,0,2:T(2,128)}, u32[]{:S(2)}) copy-start(s32[2,32,3]{1,0,2:T(2,128)} %param.22) | copy-start | bytes 2308
  7.2 3.4 copy-start.10
  7.2 4.4 %copy-start.12 = (bf16[48]{0:T(256)(128)(2,1)S(1)}, bf16[48]{0:T(256)(128)(2,1)}, u32[]{:S(2)}) copy-start(bf16[48]{0:T(256)(128)(2,1)} %param.25) | copy-start | bytes 292
  7.2 4.5 %copy-start.13 = (bf16[48]{0:T(256)(128)(2,1)S(1)}, bf16[48]{0:T(256)(128)(2,1)}, u32[]{:S(2)}) copy-start(bf16[48]{0:T(256)(128)(2,1)} %param.28) | copy-start | bytes 292
  7.2 4.6 %copy-start.14 = (bf16[48]{0:T(256)(128)(2,1)S(1)}, bf16[48]{0:T(256)(128)(2,1)}, u32[]{:S(2)}) copy-start(bf16[48]{0:T(256)(128)(2,1)} %param.30) | copy-start | bytes 292
  7.3 4.7 %copy-start.15 = (bf16[48]{0:T(256)(128)(2,1)S(1)}, bf16[48]{0:T(256)(128)(2,1)}, u32[]{:S(2)}) copy-start(bf16[48]{0:T(256)(128)(2,1)} %param.31) | copy-start | bytes 292
  7.3 4.8 %copy-start.16 = (bf16[48]{0:T(256)(128)(2,1)S(1)}, bf16[48]{0:T(256)(128)(2,1)}, u32[]{:S(2)}) copy-start(bf16[48]{0:T(256)(128)(2,1)} %param.32) | copy-start | bytes 292
  7.3 4.9 %copy-start.17 = (bf16[192]{0:T(256)(128)(2,1)S(1)}, bf16[192]{0:T(256)(128)(2,1)}, u32[]{:S(2)}) copy-start(bf16[192]{0:T(256)(128)(2,1)} %param.34) | copy-start | bytes 1156
  7.3 5.0 %copy-start.18 = (bf16[48]{0:T(256)(128)(2,1)S(1)}, bf16[48]{0:T(256)(128)(2,1)}, u32[]{:S(2)}) copy-start(bf16[48]{0:T(256)(128)(2,1)} %param.36) | copy-start | bytes 292
  7.3 5.1 %copy-start.19 = (bf16[48]{0:T(256)(128)(2,1)S(1)}, bf16[48]{0:T(256)(128)(2,1)}, u32[]{:S(2)}) copy-start(bf16[48]{0:T(256)(128)(2,1)} %param.37) | copy-start | bytes 292
  7.3 5.2 %copy-start.20 = (bf16[48]{0:T(256)(128)(2,1)S(1)}, bf16[48]{0:T(256)(128)(2,1)}, u32[]{:S(2)}) copy-start(bf16[48]{0:T(256)(128)(2,1)} %param.38) | copy-start | bytes 292
  7.3 5.3 %copy-start.9 = (bf16[48,768]{1,0:T(8,128)(2,1)S(1)}, bf16[48,768]{1,0:T(8,128)(2,1)}, u32[]{:S(2)}) copy-start(bf16[48,768]{1,0:T(8,128)(2,1)} %param.27) | copy-start | bytes 221188
  7.3 5.3 %copy-start.8 = (bf16[48,768]{1,0:T(8,128)(2,1)S(1)}, bf16[48,768]{1,0:T(8,128)(2,1)}, u32[]{:S(2)}) copy-start(bf16[48,768]{1,0:T(8,128)(2,1)} %param.26) | copy-start | bytes 221188
  7.3 5.3 %copy-start.7 = (bf16[48,768]{1,0:T(8,128)(2,1)S(1)}, bf16[48,768]{1,0:T(8,128)(2,1)}, u32[]{:S(2)}) copy-start(bf16[48,768]{1,0:T(8,128)(2,1)} %param.24) | copy-start | bytes 221188
  7.3 119.8 %all-gather.2.cloned.1.call-start = ((), (), s32[]{:S(2)}) async-start(), calls=%async_computation.2 | async-start | bytes 11280384 | tf_op jit(solution)/shard_map/all_gather | solution.py:1424
  11.5 299.7 %reduce-scatter.3.cloned.1.call-start = ((), (), s32[]{:S(2)}) async-start(), calls=%async_computation.3 | async-start | bytes 5013504 | tf_op jit(solution)/shard_map/reduce_scatter | solution.py:1469
  13.5 68.0 %copy-start.11 = (s32[2,2048]{1,0:T(2,128)S(1)}, s32[2,2048]{1,0:T(2,128)}, u32[]{:S(2)}) copy-start(s32[2,2048]{1,0:T(2,128)} %param.21) | copy-start | bytes 49156
  13.5 68.7 %copy-start.22 = (s32[2,2]{1,0:T(2,128)S(1)}, s32[2,2]{1,0:T(2,128)}, u32[]{:S(2)}) copy-start(s32[2,2]{1,0:T(2,128)} %param.23) | copy-start | bytes 52
  79.9 47.1 %collective-permute-start = (bf16[1024,768]{1,0:T(8,128)(2,1)}, bf16[1024,768]{1,0:T(8,128)(2,1)S(1)}, u32[]{:S(2)}, u32[]{:S(2)}) collective-permute-start(bf16[1024,768]{1,0:T(8,128)(2,1)} %get-tuple-element.60), channel_id=1, source_target_pairs={{0,16},{16,0},{1,17},{17,1},{2,18},{18,2},{3,19},{19,3},{4,20},{20... | collective-permute-start | bytes 4718600 | tf_op jit(solution)/shard_map/ppermute | solution.py:1443
  127.1 1.1 copy-start.21
  193.7 195.9 %reduce-scatter.5.cloned.1.call-start = ((), (), s32[]{:S(2)}) async-start(), calls=%async_computation.4 | async-start | bytes 6266880 | tf_op jit(solution)/shard_map/reduce_scatter | solution.py:1469
  247.0 64.3 %collective-permute-start.1 = (bf16[1024,768]{1,0:T(8,128)(2,1)}, bf16[1024,768]{1,0:T(8,128)(2,1)S(1)}, u32[]{:S(2)}, u32[]{:S(2)}) collective-permute-start(bf16[1024,768]{1,0:T(8,128)(2,1)} %get-tuple-element.71), channel_id=1, source_target_pairs={{0,16},{16,0},{1,17},{17,1},{2,18},{18,2},{3,19},{19,3},{4,20},{20... | collective-permute-start | bytes 4718600 | tf_op jit(solution)/shard_map/ppermute | solution.py:1465
  311.3 70.4 %copy-start.3 = (bf16[48,3072]{1,0:T(8,128)(2,1)S(1)}, bf16[48,3072]{1,0:T(8,128)(2,1)}, u32[]{:S(2)}) copy-start(bf16[48,3072]{1,0:T(8,128)(2,1)} %reduce-scatter.3.cloned.1.call-done) | copy-start | bytes 884740
  381.7 6.8 %collective-permute-start.3 = (bf16[48,3072]{1,0:T(8,128)(2,1)S(1)}, bf16[48,3072]{1,0:T(8,128)(2,1)S(1)}, u32[]{:S(2)}, u32[]{:S(2)}) collective-permute-start(bf16[48,3072]{1,0:T(8,128)(2,1)S(1)} %copy-done.3), channel_id=1, source_target_pairs={{0,16},{16,0},{1,17},{17,1},{2,18},{18,2},{3,19},{19,3},{4,20},{20... | collective-permute-start | bytes 884744 | tf_op jit(solution)/shard_map/ppermute | solution.py:1311
  382.4 4.0 copy-start.2
  389.6 7.9 %collective-permute-start.2 = (bf16[48,3840]{1,0:T(8,128)(2,1)}, bf16[48,3840]{1,0:T(8,128)(2,1)S(1)}, u32[]{:S(2)}, u32[]{:S(2)}) collective-permute-start(bf16[48,3840]{1,0:T(8,128)(2,1)} %reduce-scatter.5.cloned.1.call-done), channel_id=1, source_target_pairs={{0,16},{16,0},{1,17},{17,1},{2,18},{18,2},{3,19},{19,3},{4,20},{20... | collective-permute-start | bytes 1105928 | tf_op jit(solution)/shard_map/ppermute | solution.py:1311
  399.2 2.4 copy-start.6
  399.2 4.4 %copy-start.1 = (s32[2,32,3]{1,0,2:T(2,128)S(1)}, s32[2,32,3]{1,0,2:T(2,128)}, u32[]{:S(2)}) copy-start(s32[2,32,3]{1,0,2:T(2,128)} %param.22) | copy-start | bytes 2308
  399.2 3.0 copy-start.5
  399.3 3.7 copy-start.4
Sparse Core Ops, SparseCore 0:
  11.7 102.9 all-gather.1
  193.8 75.4 reduce-scatter.2
  273.8 90.0 reduce-scatter.4

commit v6 on v5

--- a/solution.py
+++ b/solution.py
@@ -450,11 +450,11 @@
 
 
 def qkv_backward_kernel(
-    bits, xt_in, dq_in, dk_in, dv_in, wt_in, res_in, small_in,
-    wq_out, wk_out, wv_out, small_out, tok_out,
+    bits, xt_in, dq_in, dk_in, dv_in, wt_in, res_in, small_in, outer_in,
+    wq_out, wk_out, wv_out, small_out, tok_out, outer_out,
     xt, grads, wt, res, tok, kept, sends, lands, final, small, small_land, result,
     in_sem, tok_send, tok_land, own_sem, send_sem, land_sem, x_send, x_land,
-    small_send, small_recv, out_sem,
+    small_send, small_recv, out_sem, outer_sem,
 ):
     me, side = lax.axis_index("fsdp"), lax.axis_index("seq")
     half = tok.shape[2] * tok.shape[1]
@@ -633,6 +633,11 @@
         return 0
 
     lax.fori_loop(0, 3, begin, 0)
+    outer = pltpu.make_async_remote_copy(
+        src_ref=outer_in, dst_ref=outer_out, send_sem=outer_sem.at[0], recv_sem=outer_sem.at[1],
+        device_id={"seq": 1 - side}, device_id_type=pl.DeviceIdType.MESH,
+    )
+    outer.start()
     column_sums(0, 0)
     column_sums(2, 1)
     small_hop(0).start()
@@ -663,13 +668,15 @@
     for bit in range(bits + 1):
         small_hop(bit).wait_send()
     small_copy.wait()
+    outer.wait_send()
+    outer.wait_recv()
     for i in range(pieces):
         stays(i).wait()
         sent(i).wait_send()
         landed(i).wait_recv()
 
 
-def qkv_backward(xt, dq, dk, dv, wt, resid, small, own):
+def qkv_backward(xt, dq, dk, dv, wt, resid, small, outer, own):
     tokens, width = dq.shape
     bits = lax.axis_size("fsdp").bit_length() - 1
     owners = 1 << bits
@@ -685,9 +692,10 @@
             shard, shard, shard,
             jax.ShapeDtypeStruct(small.shape, f32),
             jax.ShapeDtypeStruct((2, tokens // 2, width), bf16),
+            jax.ShapeDtypeStruct(outer.shape, bf16),
         ),
-        in_specs=[anywhere] * 7,
-        out_specs=(anywhere,) * 5,
+        in_specs=[anywhere] * 8,
+        out_specs=(anywhere,) * 6,
         scratch_shapes=[
             pltpu.VMEM(xt.shape, bf16),
             pltpu.VMEM((3, tokens, width), bf16),
@@ -703,7 +711,7 @@
             pltpu.VMEM((3, own, width), f32),
             dma((11,)), dma((pieces,)), dma((pieces,)), dma((pieces,)),
             dma((3, bits)), dma((3, bits)), dma((3,)), dma((3,)),
-            dma((bits + 1,)), dma((bits + 1,)), dma((4,)),
+            dma((bits + 1,)), dma((bits + 1,)), dma((4,)), dma((2,)),
         ],
         compiler_params=pltpu.CompilerParams(
             collective_id=1, has_side_effects=True, vmem_limit_bytes=62 << 20
@@ -713,7 +721,7 @@
             bytes_accessed=16 * tokens * width,
         ),
         name="qkv_backward",
-    )(xt, dq, dk, dv, wt, resid, small)
+    )(xt, dq, dk, dv, wt, resid, small, outer)
 
 
 def qkv_forward_kernel(
@@ -1476,16 +1484,19 @@
     dq, dk, dv = (regroup.from_heads(x).reshape(tok_count, width) for x in (dq, dk, dv))
     mine = lax.axis_index("fsdp")
     dq, sent, d_outer = lax.optimization_barrier((dq, sent, d_outer))
-    d_outer = sum_seq(d_outer)
     if paired:
-        d_query_w, d_key_w, d_value_w, sums, d_tokens_in = qkv_backward(
-            turned_in, dq, dk, dv, turned_w, d_attn, sums, own
-        )
-        d_second, sums = lax.optimization_barrier((d_second, sums))
+        d_query_w, d_key_w, d_value_w, sums, d_tokens_in, other = qkv_backward(
+            turned_in, dq, dk, dv, turned_w, d_attn, sums, d_outer, own
+        )
+        d_outer = d_outer.astype(jnp.float32) + other.astype(jnp.float32)
+        d_second, sums, d_tokens_in, sent = lax.optimization_barrier(
+            (d_second, sums, d_tokens_in, sent)
+        )
         place = jnp.arange(2, dtype=jnp.int32)[:, None, None]
         out_tokens = jnp.where(place == side, kept[None], sent[None])
         d_tokens_in = jnp.where(place >= -side, d_tokens_in, jnp.zeros_like(d_tokens_in))
     else:
+        d_outer = sum_seq(d_outer)
         for spot, part in ((0, dq), (1, dv)):
             sums = sums.at[spot].set(jnp.sum(part.astype(jnp.float32), axis=0))
         sums = butterfly_sum(butterfly_sum(sums, "fsdp"), "seq")

time: 410 us -> 408 us (level)
    pallas_call x1, Pallas kernels: 70.4 us -> 75.6 us  [qkv_backward(): pl.pallas_call(functools.partial(qkv_backward_kernel, bits), out_shape=(s...]
  transfers between devices with their start and end apart: 7 -> 6, of which waited for: 1 -> 0; matrix products, arithmetic and copies ran while one was open for 5% -> 4% of each run, Pallas kernels for 72% -> 72%
where the time goes in v6:
time: 408 us; the launch traced here: 410 us
  Pallas kernels  359 us (88%)
  local copies, waits for them, and re-layouts  18.5 us (5%)
  between operations  14.2 us (3%)
  other arithmetic  12.7 us (3%)
  starting transfers between devices  5.64 us (1%)
    pallas_call x1, Pallas kernels, qkv_backward(): pl.pallas_call(functools.partial(qkv_backward_kernel, bits), out_shape=(s...  75.6 us
    pallas_call x1, Pallas kernels, qkv_forward(): pl.pallas_call(functools.partial(qkv_forward_kernel, bits), out_shape=(ja...  66.5 us
    pallas_call x1, Pallas kernels, middle_forward(): pl.pallas_call(functools.partial(middle_forward_kernel, chunks), out_shap...  65.4 us
    pallas_call x1, Pallas kernels, attention_backward(): pl.pallas_call(functools.partial(backward_kernel, group), out_shape=(like...  61 us
    pallas_call x1, Pallas kernels, middle_backward(): pl.pallas_call(functools.partial(middle_backward_kernel, chunks), grid=(s...  52.9 us
    pallas_call x1, Pallas kernels, attention_forward(): pl.pallas_call(functools.partial(forward_kernel, group), out_shape=(jax.S...  37.7 us
  transfers between devices with their start and end apart: 6, of which 0 were waited for; matrix products, arithmetic and copies ran while one was open for 4% of the time, Pallas kernels for 72%

profile of v6, /device:TPU:0, one launch (start us, length us, event | category | flops | bytes accessed | tf_op | source)
XLA Modules:
  0.0 410.2 jit_solution(6133142008720288181)
XLA Ops:
  7.4 1.3 reshape.741
  8.6 1.4 copy.63
  10.0 0.6 copy.64
  10.6 0.9 pad_maximum_fusion
  11.6 0.1 copy.65
  11.9 0.1 copy.68
  12.0 0.1 copy.69
  12.2 0.1 reshape.743
  12.3 0.1 copy.70
  12.6 0.8 concatenate.13.own_in
  13.5 66.5 %qkv_forward.1 = (bf16[1024,768]{1,0:T(8,128)(2,1)}, bf16[2,4,256,768]{3,2,1,0:T(8,128)(2,1)}, bf16[2,4,768,256]{3,2,1,0:T(8,128)(2,1)}, bf16[2,4,256,768]{3,2,1...) custom-call(bf16[2,4,256,768]{3,2,1,0:T(8,128)(2,1)} %bitcast.81, ...), custom_call_target="tpu_custom_call" | custom-call | flops 21743271936 | bytes 25165824 | tf_op jit(solution)/shard_map/qkv_forward/pallas_call | solution.py:904
  79.9 0.9 collective-permute-start
  80.9 0.5 broadcast.492
  81.4 0.7 fusion.16
  82.2 0.2 slice_reduce_fusion
  82.5 0.2 convert_reduce_fusion
  83.1 0.2 multiply_reduce_fusion
  83.3 0.4 select_reduce_fusion
  83.8 0.7 pad_add_fusion
  84.5 0.6 fusion.14
  85.1 0.5 and_select_fusion.1.n_ref
  85.6 0.6 compare_select_fusion.list_ref
  86.2 1.4 broadcast_in_dim.126.segc_ref
  87.6 37.7 %attention_forward.1 = (bf16[1,2048,768]{2,1,0:T(8,128)(2,1)}, f32[1,32,1,768]{3,2,1,0:T(1,128)}) custom-call(s32[1,32]{1,0:T(1,128)} %and_select_fusion.1.n_ref, s32[1,1024]{1,0:T(1,128)} %compare_select_fusion.list_ref, s32[1]{0:T(128)} %bitcast.15.total_ref, bf16[1,2048,768]{2,1,0:T(8,128)(2,1)} %bitcast.82, bf16[1,2048,768]{2,1,0:T(8,128)(2,1)} %bitcast.84, ...), custom_call_target="tpu_custom_call" | custom-call | flops 3221225472 | bytes 12582912 | tf_op jit(solution)/shard_map/attention_forward/pallas_call | solution.py:254
  125.3 1.1 copy-done.22
  126.4 65.4 %middle_forward.1 = (bf16[1024,768]{1,0:T(8,128)(2,1)}, bf16[1024,768]{1,0:T(8,128)(2,1)}, bf16[2048,768]{1,0:T(8,128)(2,1)}, bf16[2048,768]{1,0:T(8,128)(2,1)},...) custom-call(s32[1]{0:T(128)} %bitcast.side, ...), custom_call_target="tpu_custom_call" | custom-call | flops 72477573120 | bytes 68419584 | tf_op jit(solution)/shard_map/middle_forward/pallas_call | solution.py:1220
  191.9 0.3 reduce-scatter.3.cloned.1.call-start
  192.2 52.9 %middle_backward.1 = (bf16[2048,768]{1,0:T(8,128)(2,1)}, bf16[2048,768]{1,0:T(8,128)(2,1)}, bf16[768,3840]{1,0:T(8,128)(2,1)}, f32[16,768]{1,0:T(8,128)}) custom-call(bf16[768,6912]{1,0:T(8,128)(2,1)} %all-gather.2.cloned.1.call-done.weights_in, f32[16,768]{1,0:T(8,128)} %get-tuple-element.57.small, f32[16,768]{1,0:T(8,128)} %get-tuple-element.65.sums_in, ...), custom_call_target="tpu_custom_call" | custom-call | flops 72477573120 | bytes 68419584 | tf_op jit(solution)/shard_map/middle_backward/pallas_call | solution.py:1265
  245.1 1.2 collective-permute-start.1
  246.3 61.0 %attention_backward.1 = (bf16[1,2048,768]{2,1,0:T(8,128)(2,1)}, bf16[1,2048,768]{2,1,0:T(8,128)(2,1)}, bf16[1,2048,768]{2,1,0:T(8,128)(2,1)}) custom-call(s32[1,32]{1,0:T(1,128)} %and_select_fusion.1.n_ref, s32[1,1024]{1,0:T(1,128)} %compare_select_fusion.list_ref, s32[1]{0:T(128)} %bitcast.15.total_ref, bf16[1,2048,768]{2,1,0:T(8,128)(2,1)} %bitcast.83, ...), custom_call_target="tpu_custom_call" | custom-call | flops 8053063680 | bytes 25165824 | tf_op jit(solution)/shard_map/attention_backward/pallas_call | solution.py:401
  307.4 75.6 %qkv_backward.1 = (f32[48,768]{1,0:T(8,128)}, f32[48,768]{1,0:T(8,128)}, f32[48,768]{1,0:T(8,128)}, f32[16,768]{1,0:T(8,128)}, bf16[2,1024,768]{2,1,0:T(8,128)(2,1)}, /*index=5*/bf16[48,3072]{1,0:T(8,128)(2,1)}) custom-call(bf16[2,4,768,256]{3,2,1,0:T(8,128)(2,1)} %get-tuple-element.72.xt_in, bf16[2048,768]{1,0:T(8,128)(2,1)} %bitcast.92, ...), custom_call_target="tpu_custom_call" | custom-call | flops 48318382080 | bytes 25165824 | tf_op jit(solution)/shard_map/qkv_backward/pallas_call | solution.py:689
  383.0 1.0 convert_add_fusion.1
  384.0 1.0 reshape.754
  385.0 0.9 slice_reduce_fusion.2
  385.8 0.5 multiply_sqrt_fusion
  386.4 0.8 dynamic-slice_bitcast_fusion
  387.2 0.7 reshape.753
  387.9 3.1 collective-permute-start.2
  391.0 3.8 broadcast_select_fusion
  394.9 1.6 dynamic-slice_bitcast_fusion.1
  396.5 2.0 broadcast_select_fusion.1
  398.6 0.7 slice.58
  399.3 0.3 reshape.751
  399.6 0.7 copy.73
  400.4 1.3 copy.75
  401.6 0.7 copy.83
  402.3 0.7 copy.84
  403.0 0.7 copy.85
  (83 shorter events, 1.7 us)
Async XLA Ops:
  7.2 73.7 %copy-start = (s32[2,32,3]{1,0,2:T(2,128)S(1)}, s32[2,32,3]{1,0,2:T(2,128)}, u32[]{:S(2)}) copy-start(s32[2,32,3]{1,0,2:T(2,128)} %param.22) | copy-start | bytes 2308
  7.2 3.4 copy-start.11
  7.2 4.4 %copy-start.13 = (bf16[48]{0:T(256)(128)(2,1)S(1)}, bf16[48]{0:T(256)(128)(2,1)}, u32[]{:S(2)}) copy-start(bf16[48]{0:T(256)(128)(2,1)} %param.25) | copy-start | bytes 292
  7.2 4.5 %copy-start.14 = (bf16[48]{0:T(256)(128)(2,1)S(1)}, bf16[48]{0:T(256)(128)(2,1)}, u32[]{:S(2)}) copy-start(bf16[48]{0:T(256)(128)(2,1)} %param.28) | copy-start | bytes 292
  7.2 4.6 %copy-start.15 = (bf16[48]{0:T(256)(128)(2,1)S(1)}, bf16[48]{0:T(256)(128)(2,1)}, u32[]{:S(2)}) copy-start(bf16[48]{0:T(256)(128)(2,1)} %param.30) | copy-start | bytes 292
  7.3 4.7 %copy-start.16 = (bf16[48]{0:T(256)(128)(2,1)S(1)}, bf16[48]{0:T(256)(128)(2,1)}, u32[]{:S(2)}) copy-start(bf16[48]{0:T(256)(128)(2,1)} %param.31) | copy-start | bytes 292
  7.3 4.8 %copy-start.17 = (bf16[48]{0:T(256)(128)(2,1)S(1)}, bf16[48]{0:T(256)(128)(2,1)}, u32[]{:S(2)}) copy-start(bf16[48]{0:T(256)(128)(2,1)} %param.32) | copy-start | bytes 292
  7.3 4.9 %copy-start.18 = (bf16[192]{0:T(256)(128)(2,1)S(1)}, bf16[192]{0:T(256)(128)(2,1)}, u32[]{:S(2)}) copy-start(bf16[192]{0:T(256)(128)(2,1)} %param.34) | copy-start | bytes 1156
  7.3 5.0 %copy-start.19 = (bf16[48]{0:T(256)(128)(2,1)S(1)}, bf16[48]{0:T(256)(128)(2,1)}, u32[]{:S(2)}) copy-start(bf16[48]{0:T(256)(128)(2,1)} %param.36) | copy-start | bytes 292
  7.3 5.1 %copy-start.20 = (bf16[48]{0:T(256)(128)(2,1)S(1)}, bf16[48]{0:T(256)(128)(2,1)}, u32[]{:S(2)}) copy-start(bf16[48]{0:T(256)(128)(2,1)} %param.37) | copy-start | bytes 292
  7.3 5.2 %copy-start.21 = (bf16[48]{0:T(256)(128)(2,1)S(1)}, bf16[48]{0:T(256)(128)(2,1)}, u32[]{:S(2)}) copy-start(bf16[48]{0:T(256)(128)(2,1)} %param.38) | copy-start | bytes 292
  7.3 5.3 %copy-start.10 = (bf16[48,768]{1,0:T(8,128)(2,1)S(1)}, bf16[48,768]{1,0:T(8,128)(2,1)}, u32[]{:S(2)}) copy-start(bf16[48,768]{1,0:T(8,128)(2,1)} %param.27) | copy-start | bytes 221188
  7.3 5.3 %copy-start.9 = (bf16[48,768]{1,0:T(8,128)(2,1)S(1)}, bf16[48,768]{1,0:T(8,128)(2,1)}, u32[]{:S(2)}) copy-start(bf16[48,768]{1,0:T(8,128)(2,1)} %param.26) | copy-start | bytes 221188
  7.3 5.3 %copy-start.8 = (bf16[48,768]{1,0:T(8,128)(2,1)S(1)}, bf16[48,768]{1,0:T(8,128)(2,1)}, u32[]{:S(2)}) copy-start(bf16[48,768]{1,0:T(8,128)(2,1)} %param.24) | copy-start | bytes 221188
  7.3 118.0 %all-gather.2.cloned.1.call-start = ((), (), s32[]{:S(2)}) async-start(), calls=%async_computation.2 | async-start | bytes 11280384 | tf_op jit(solution)/shard_map/all_gather | solution.py:1432
  11.5 295.8 %reduce-scatter.5.cloned.1.call-start = ((), (), s32[]{:S(2)}) async-start(), calls=%async_computation.4 | async-start | bytes 5013504 | tf_op jit(solution)/shard_map/reduce_scatter | solution.py:1477
  13.5 68.0 %copy-start.12 = (s32[2,2048]{1,0:T(2,128)S(1)}, s32[2,2048]{1,0:T(2,128)}, u32[]{:S(2)}) copy-start(s32[2,2048]{1,0:T(2,128)} %param.21) | copy-start | bytes 49156
  13.5 68.7 %copy-start.23 = (s32[2,2]{1,0:T(2,128)S(1)}, s32[2,2]{1,0:T(2,128)}, u32[]{:S(2)}) copy-start(s32[2,2]{1,0:T(2,128)} %param.23) | copy-start | bytes 52
  79.9 45.3 %collective-permute-start = (bf16[1024,768]{1,0:T(8,128)(2,1)}, bf16[1024,768]{1,0:T(8,128)(2,1)S(1)}, u32[]{:S(2)}, u32[]{:S(2)}) collective-permute-start(bf16[1024,768]{1,0:T(8,128)(2,1)} %get-tuple-element.63), channel_id=1, source_target_pairs={{0,16},{16,0},{1,17},{17,1},{2,18},{18,2},{3,19},{19,3},{4,20},{20... | collective-permute-start | bytes 4718600 | tf_op jit(solution)/shard_map/ppermute | solution.py:1451
  125.3 1.1 copy-start.22
  191.9 193.1 %reduce-scatter.3.cloned.1.call-start = ((), (), s32[]{:S(2)}) async-start(), calls=%async_computation.3 | async-start | bytes 6266880 | tf_op jit(solution)/shard_map/reduce_scatter | solution.py:1477
  245.1 62.3 %collective-permute-start.1 = (bf16[1024,768]{1,0:T(8,128)(2,1)}, bf16[1024,768]{1,0:T(8,128)(2,1)S(1)}, u32[]{:S(2)}, u32[]{:S(2)}) collective-permute-start(bf16[1024,768]{1,0:T(8,128)(2,1)} %get-tuple-element.76), channel_id=1, source_target_pairs={{0,16},{16,0},{1,17},{17,1},{2,18},{18,2},{3,19},{19,3},{4,20},{20... | collective-permute-start | bytes 4718600 | tf_op jit(solution)/shard_map/ppermute | solution.py:1473
  307.4 75.6 %copy-start.4 = (bf16[48,3072]{1,0:T(8,128)(2,1)S(1)}, bf16[48,3072]{1,0:T(8,128)(2,1)}, u32[]{:S(2)}) copy-start(bf16[48,3072]{1,0:T(8,128)(2,1)} %reduce-scatter.5.cloned.1.call-done.outer_in) | copy-start | bytes 884740
  387.9 8.6 %copy-start.2 = (bf16[1024,768]{1,0:T(8,128)(2,1)S(1)}, bf16[1024,768]{1,0:T(8,128)(2,1)}, u32[]{:S(2)}) copy-start(bf16[1024,768]{1,0:T(8,128)(2,1)} %get-tuple-element.64) | copy-start | bytes 4718596
  387.9 10.6 %collective-permute-start.2 = (bf16[48,3840]{1,0:T(8,128)(2,1)}, bf16[48,3840]{1,0:T(8,128)(2,1)S(1)}, u32[]{:S(2)}, u32[]{:S(2)}) collective-permute-start(bf16[48,3840]{1,0:T(8,128)(2,1)} %reduce-scatter.3.cloned.1.call-done), channel_id=1, source_target_pairs={{0,16},{16,0},{1,17},{17,1},{2,18},{18,2},{3,19},{19,3},{4,20},{20... | collective-permute-start | bytes 1105928 | tf_op jit(solution)/shard_map/ppermute | solution.py:1319
  396.5 2.0 copy-start.3
  399.3 2.4 copy-start.7
  399.3 4.4 %copy-start.1 = (s32[2,32,3]{1,0,2:T(2,128)S(1)}, s32[2,32,3]{1,0,2:T(2,128)}, u32[]{:S(2)}) copy-start(s32[2,32,3]{1,0,2:T(2,128)} %param.22) | copy-start | bytes 2308
  399.3 3.0 copy-start.6
  399.3 3.7 copy-start.5
Sparse Core Ops, SparseCore 0:
  11.7 102.9 all-gather.1
  192.0 79.1 reduce-scatter.4
  275.7 99.3 reduce-scatter.2
